TPU v7x, 32 devices: a whole 2x2x4 slice. The times are simulated.
32 devices in a mesh: dp: 8 (over z, y), tensor: 4 (over x, core).
Axes of the slice: x: 2, y: 2, z: 4, core: 2. Of those that a mesh axis runs over, the one named last changes fastest.
Arguments:
- tokens: bfloat16 [16384, 2048], P(('dp', 'tensor')), may hold values from -6 to 6
- cotangent: bfloat16 [16384, 2048], P(('dp', 'tensor')), may hold values from -6 to 6
- lengths: int32 [16, 4], replicated, may hold values from 1 to 896, 1024 in all within a row
- sequence_adapter_index: int32 [16, 4], replicated, may hold values from 0 to 7
- deal: int32 [16], replicated, may hold values from 0 to 15, each once
- input_norm_gain: float32 [2048], replicated, may hold values from 0.5 to 1.5
- inner_projection_weight: bfloat16 [2048, 2, 4096], P(None, None, 'tensor'), may hold values from -0.125 to 0.125
- state_projection_weight: bfloat16 [2048, 256], replicated, may hold values from -0.125 to 0.125
- step_projection_weight: bfloat16 [2048, 64], P(None, 'tensor'), may hold values from -0.125 to 0.125
- inner_conv_taps: float32 [5, 4096], P(None, 'tensor'), may hold values from -3 to 3
- state_conv_taps: float32 [5, 256], replicated, may hold values from -3 to 3
- head_parameters: float32 [3, 64], P(None, 'tensor'), may hold values from -14 to 3, as said below
- gated_norm_gain: float32 [4096], P('tensor'), may hold values from 0.5 to 1.5
- output_projection_weight: bfloat16 [4096, 2048], P('tensor'), may hold values from -0.09375 to 0.09375
- adapter_input_down: bfloat16 [2048, 8, 16], replicated, may hold values from -0.125 to 0.125
- adapter_input_up: bfloat16 [8, 16, 2, 4096], P(None, None, None, 'tensor'), may hold values from -1 to 1
- adapter_output_down: bfloat16 [4096, 8, 16], P('tensor'), may hold values from -0.09375 to 0.09375
- adapter_output_up: bfloat16 [8, 16, 2048], replicated, may hold values from -1 to 1
Outputs:
- output: bfloat16 [16384, 2048], P(('dp', 'tensor'))
- grad_in: float32 [16384, 2048], P(('dp', 'tensor'))
- grad_in_down: float32 [2048, 8, 16], replicated
- input_up_gradient: float32 [8, 16, 2, 4096], P(None, None, None, 'tensor')
- grad_out_down: float32 [4096, 8, 16], P('tensor')
- output_up_gradient: float32 [8, 16, 2048], replicated
Inputs may be any that keep to these rules, and one draw needn't show every extreme that they name: `lengths`: each row sums to 1024, and each row has one sequence of exactly 896. `deal`: a permutation of the packed rows. `head_parameters`: row 0 is the step bias, row 1 the logarithm of the decay rate (0 to log 16), row 2 the skip gain (0.5 to 1.5).
All inputs are finite; a program needn't handle non-finite values.
Results may differ from a plain program's by a relative error of at most 0.012.
Values may be sent and summed in bfloat16 or wider, within the bound.
A program may use at most 256 MiB of HBM per device.

v0:
```python
import jax
import jax.numpy as jnp
from jax import lax
from jax.sharding import PartitionSpec as P

P_SIZE = 64
BLOCK = 256
ROW_LEN = 1024


epsilon = 1e-05
top_precision = lax.Precision.HIGHEST


def segment_info(lengths_rows, ids_rows, row_length):
    ends = jnp.cumsum(lengths_rows, axis=1)
    starts = ends - lengths_rows
    position = jnp.arange(row_length, dtype=jnp.int32)
    segment = jnp.sum((position[None, :, None] >= ends[:, None, :]).astype(jnp.int32), axis=2)
    member = (
        segment[:, :, None] == jnp.arange(lengths_rows.shape[1], dtype=jnp.int32)[None, None, :]
    )
    begins = jnp.sum(jnp.where(member, starts[:, None, :], 0), axis=2)
    within = position[None, :] - begins
    adapter = jnp.sum(jnp.where(member, ids_rows[:, None, :], 0), axis=2)
    return (segment, within, adapter)


def selection(adapter, number_of_adapters, adapter_rank_width):
    column = (
        jnp.arange(number_of_adapters * adapter_rank_width, dtype=jnp.int32) // adapter_rank_width
    )
    return (adapter.reshape(-1, 1) == column[None, :]).astype(jnp.float32)


def causal_conv(values, taps, within):
    seq_len = values.shape[1]
    tap_count = taps.shape[0] - 1
    summed = taps[tap_count] + jnp.zeros_like(values)
    for lag_steps in range(tap_count):
        shifted = jnp.pad(values, ((0, 0), (lag_steps, 0), (0, 0)))[:, :seq_len]
        usable = (within >= lag_steps)[:, :, None]
        summed = summed + jnp.where(usable, shifted, 0.0) * taps[tap_count - 1 - lag_steps]
    return jax.nn.silu(summed)


def state_scan(weighted, log_decay, input_mat, output_mat, segment, block_len):
    seq_rows, seq_len, head_count, head_size = weighted.shape
    block_count = seq_len // block_len

    def split_blocks(array_in):
        return jnp.moveaxis(
            array_in.reshape((seq_rows, block_count, block_len) + array_in.shape[2:]), 1, 0
        )

    inputs = tuple(
        (
            split_blocks(member_array)
            for member_array in (weighted, log_decay, input_mat, output_mat, segment)
        )
    )
    start_state = jnp.zeros((seq_rows, head_count, head_size, input_mat.shape[2]), jnp.float32)
    start_prev = jnp.full((seq_rows,), -1, jnp.int32)
    lower_tri = jnp.tril(jnp.ones((block_len, block_len), jnp.bool_))

    def advance(carried_in, block_data):
        state, previous = carried_in
        xdt, decay_blk, in_blk, out_blk, seg_blk = block_data
        cumul = jnp.cumsum(decay_blk, axis=1)
        allowed = (seg_blk[:, :, None] == seg_blk[:, None, :]) & lower_tri[None]
        allowed = allowed[..., None]
        spread = cumul[:, :, None, :] - cumul[:, None, :, :]
        weights = jnp.where(allowed, jnp.exp(jnp.where(allowed, spread, 0.0)), 0.0)
        scores = jnp.einsum("rin,rjn->rij", out_blk, in_blk, precision=top_precision)
        inside = jnp.einsum(
            "rijh,rjhp->rihp", weights * scores[..., None], xdt, precision=top_precision
        )
        carried = jnp.where((seg_blk == previous[:, None])[..., None], jnp.exp(cumul), 0.0)
        inside = (
            inside
            + jnp.einsum("rin,rhpn->rihp", out_blk, state, precision=top_precision)
            * carried[..., None]
        )
        last_seg = seg_blk[:, -1]
        tail_w = jnp.where(
            (seg_blk == last_seg[:, None])[..., None], jnp.exp(cumul[:, -1:, :] - cumul), 0.0
        )
        keep_w = jnp.where((last_seg == previous)[:, None], jnp.exp(cumul[:, -1, :]), 0.0)
        state = keep_w[:, :, None, None] * state + jnp.einsum(
            "rjh,rjn,rjhp->rhpn", tail_w, in_blk, xdt, precision=top_precision
        )
        return ((state, last_seg), inside)

    final_carry, outputs = lax.scan(jax.checkpoint(advance), (start_state, start_prev), inputs)
    return jnp.moveaxis(outputs, 0, 1).reshape(seq_rows, seq_len, head_count, head_size)


def mixer(
    gate_inner_projection,
    proj_bc,
    proj_dt,
    inner_conv_taps,
    state_conv_taps,
    head_parameters,
    segment,
    within,
    head_size,
    block_len,
):
    gate_in = gate_inner_projection[:, :, 0, :]
    inner_in = gate_inner_projection[:, :, 1, :]
    conv_out = causal_conv(inner_in, inner_conv_taps, within)
    state_io = causal_conv(proj_bc, state_conv_taps, within)
    state_dim = proj_bc.shape[2] // 2
    input_mat = state_io[:, :, :state_dim]
    output_mat = state_io[:, :, state_dim:]
    step_size = jax.nn.softplus(proj_dt + head_parameters[0])
    log_decay = -jnp.exp(head_parameters[1]) * step_size
    seq_rows, seq_len, channel_width = conv_out.shape
    head_count = channel_width // head_size
    values = conv_out.reshape(seq_rows, seq_len, head_count, head_size)
    result = state_scan(
        values * step_size[..., None], log_decay, input_mat, output_mat, segment, block_len
    )
    result = result + head_parameters[2][:, None] * values
    return result.reshape(seq_rows, seq_len, channel_width) * jax.nn.silu(gate_in)


def on_device(
    tokens,
    cotangent,
    lengths,
    sequence_adapter_index,
    deal,
    input_norm_gain,
    inner_projection_weight,
    state_projection_weight,
    step_projection_weight,
    inner_conv_taps,
    state_conv_taps,
    head_parameters,
    gated_norm_gain,
    output_projection_weight,
    adapter_input_down,
    adapter_input_up,
    adapter_output_down,
    adapter_output_up,
):
    tok_dev, model_width = tokens.shape
    parts = lax.axis_size("tensor")
    group_len = tok_dev * parts
    row_count = group_len // ROW_LEN
    first_row = lax.axis_index("dp") * row_count
    my_rows = lax.dynamic_slice_in_dim(deal, first_row, row_count)
    segment, within, adapter = segment_info(
        jnp.take(lengths, my_rows, axis=0),
        jnp.take(sequence_adapter_index, my_rows, axis=0),
        ROW_LEN,
    )
    number_of_adapters = adapter_input_down.shape[1]
    adapter_rank_width = adapter_input_down.shape[2]
    reduced_count = number_of_adapters * adapter_rank_width
    adapter_selector = selection(adapter, number_of_adapters, adapter_rank_width)
    channel_width = inner_projection_weight.shape[2]
    full_inner = channel_width * parts
    input_down_factor = adapter_input_down.reshape(model_width, reduced_count)
    input_up_factor = adapter_input_up.reshape(reduced_count, 2 * channel_width)
    output_down_factor = adapter_output_down.reshape(channel_width, reduced_count)
    output_up_factor = adapter_output_up.reshape(reduced_count, model_width)
    zx_weight = inner_projection_weight.reshape(model_width, 2 * channel_width)
    residual = tokens.astype(jnp.float32)
    inv_rms = lax.rsqrt(jnp.mean(residual * residual, axis=1, keepdims=True) + epsilon)
    normalized_input = (residual * inv_rms * input_norm_gain).astype(jnp.bfloat16)
    picked_factors = lax.all_gather(normalized_input, "tensor", axis=0, tiled=True)
    adapter_middle = (
        jnp.dot(picked_factors, input_down_factor, preferred_element_type=jnp.float32)
        * adapter_selector
    ).astype(jnp.bfloat16)
    gate_inner_projection = jnp.dot(
        picked_factors, zx_weight, preferred_element_type=jnp.float32
    ) + jnp.dot(adapter_middle, input_up_factor, preferred_element_type=jnp.float32)
    proj_bc = jnp.dot(picked_factors, state_projection_weight, preferred_element_type=jnp.float32)
    proj_dt = jnp.dot(picked_factors, step_projection_weight, preferred_element_type=jnp.float32)

    def local_mix(zx_part, bc_part, dt_part):
        return mixer(
            zx_part.reshape(row_count, ROW_LEN, 2, channel_width),
            bc_part.reshape(row_count, ROW_LEN, -1),
            dt_part.reshape(row_count, ROW_LEN, -1),
            inner_conv_taps,
            state_conv_taps,
            head_parameters,
            segment,
            within,
            P_SIZE,
            BLOCK,
        ).reshape(group_len, channel_width)

    gated, mix_pull = jax.vjp(local_mix, gate_inner_projection, proj_bc, proj_dt)
    square_sum = lax.psum(jnp.sum(gated * gated, axis=1), "tensor")
    factor = lax.rsqrt(square_sum / full_inner + epsilon)[:, None]
    mixer_input = (gated * factor * gated_norm_gain).astype(jnp.bfloat16)
    adapter_backward = (
        jnp.dot(mixer_input, output_down_factor, preferred_element_type=jnp.float32)
        * adapter_selector
    ).astype(jnp.bfloat16)
    adapter_update = lax.psum_scatter(
        (
            jnp.dot(mixer_input, output_projection_weight, preferred_element_type=jnp.float32)
            + jnp.dot(adapter_backward, output_up_factor, preferred_element_type=jnp.float32)
        ).astype(jnp.bfloat16),
        "tensor",
        scatter_dimension=0,
        tiled=True,
    ).astype(jnp.float32)
    output = (residual + adapter_update).astype(jnp.bfloat16)
    whole_cotangent = lax.all_gather(cotangent, "tensor", axis=0, tiled=True)
    cot_low = (
        jnp.dot(whole_cotangent, output_up_factor.T, preferred_element_type=jnp.float32)
        * adapter_selector
    ).astype(jnp.bfloat16)
    grad_mix = jnp.dot(
        whole_cotangent, output_projection_weight.T, preferred_element_type=jnp.float32
    ) + jnp.dot(cot_low, output_down_factor.T, preferred_element_type=jnp.float32)
    grad_out_down = jnp.dot(mixer_input.T, cot_low, preferred_element_type=jnp.float32)
    output_up_gradient = jnp.dot(
        adapter_backward.T, whole_cotangent, preferred_element_type=jnp.float32
    )
    scaled = grad_mix * gated_norm_gain
    cross_sum = lax.psum(jnp.sum(scaled * gated, axis=1), "tensor")
    grad_gated = factor * scaled - gated * factor**3 * (cross_sum[:, None] / full_inner)
    grad_zx, grad_bc, grad_dt = mix_pull(grad_gated)
    gate_inner_reduced = grad_zx.astype(jnp.bfloat16)
    bc_low = grad_bc.astype(jnp.bfloat16)
    dt_low = grad_dt.astype(jnp.bfloat16)
    grad_mid = (
        jnp.dot(gate_inner_reduced, input_up_factor.T, preferred_element_type=jnp.float32)
        * adapter_selector
    ).astype(jnp.bfloat16)
    input_up_gradient = jnp.dot(
        adapter_middle.T, gate_inner_reduced, preferred_element_type=jnp.float32
    )
    grad_in_down = jnp.dot(picked_factors.T, grad_mid, preferred_element_type=jnp.float32)
    summed = jnp.dot(gate_inner_reduced, zx_weight.T, preferred_element_type=jnp.float32)
    summed = summed + jnp.dot(bc_low, state_projection_weight.T, preferred_element_type=jnp.float32)
    summed = summed + jnp.dot(dt_low, step_projection_weight.T, preferred_element_type=jnp.float32)
    grad_normed = lax.psum_scatter(
        (
            summed + jnp.dot(grad_mid, input_down_factor.T, preferred_element_type=jnp.float32)
        ).astype(jnp.bfloat16),
        "tensor",
        scatter_dimension=0,
        tiled=True,
    ).astype(jnp.float32)
    scaled_in = grad_normed * input_norm_gain
    grad_tokens = (
        cotangent.astype(jnp.float32)
        + inv_rms * scaled_in
        - residual
        * inv_rms**3
        * (jnp.sum(scaled_in * residual, axis=1, keepdims=True) / model_width)
    )
    sum_in_down, sum_out_up = lax.psum((grad_in_down, output_up_gradient), ("dp", "tensor"))
    sum_in_up, sum_out_down = (
        lax.psum(input_up_gradient.astype(jnp.bfloat16), "dp").astype(jnp.float32),
        lax.psum(grad_out_down.astype(jnp.bfloat16), "dp").astype(jnp.float32),
    )
    return (
        output,
        grad_tokens,
        sum_in_down.reshape(model_width, number_of_adapters, adapter_rank_width),
        sum_in_up.reshape(number_of_adapters, adapter_rank_width, 2, channel_width),
        sum_out_down.reshape(channel_width, number_of_adapters, adapter_rank_width),
        sum_out_up.reshape(number_of_adapters, adapter_rank_width, model_width),
    )


def solution(mesh):
    return jax.shard_map(
        on_device,
        mesh=mesh,
        in_specs=(
            P(("dp", "tensor"), None),
            P(("dp", "tensor"), None),
            P(),
            P(),
            P(),
            P(),
            P(None, None, "tensor"),
            P(),
            P(None, "tensor"),
            P(None, "tensor"),
            P(),
            P(None, "tensor"),
            P("tensor"),
            P("tensor", None),
            P(),
            P(None, None, None, "tensor"),
            P("tensor", None, None),
            P(),
        ),
        out_specs=(
            P(("dp", "tensor"), None),
            P(("dp", "tensor"), None),
            P(),
            P(None, None, None, "tensor"),
            P("tensor", None, None),
            P(),
        ),
        check_vma=False,
    )
```

profile of v0, /device:TPU:0, one launch (start us, length us, event | category | flops | bytes accessed | tf_op | source)
XLA Modules:
  0.0 1428.5 jit_solution(9176744381876958058)
XLA Ops:
  18.0 11.6 copy.329
  30.6 44.6 %all-gather.3.cloned.1.call-done = bf16[2048,2048]{1,0:T(8,128)(2,1)} async-done(((bf16[512,2048]{1,0:T(8,128)(2,1)}), bf16[2048,2048]{1,0:T(8,128)(2,1)}) %all-gather.3.cloned.1.call-update) | async-done | bytes 8388624 | tf_op jit(solution)/shard_map/all_gather | solution.py:174
  96.9 23.9 %convolution_add_fusion.2 = f32[2048,2048]{1,0:T(8,128)} fusion(f32[2048,2048]{1,0:T(8,128)} %fusion.174, bf16[2048,2048]{1,0:T(8,128)(2,1)S(1)} %bitcast.541, bf16[2048,2048]{1,0:T(8,128)(2,1)} %bitcast.543), kind=kOutput, calls=%fused_computation.152 | convolution fusion | flops 17184063488 | bytes 50331648 | tf_op jit(solution)/shard_map/dot_general | solution.py:179
  120.8 22.0 %reshape.529 = f32[2,1024,2,1024]{3,2,1,0:T(2,128)} reshape(f32[2048,2048]{1,0:T(8,128)} %convolution_add_fusion.2) | data formatting | bytes 33554432 | tf_op jit(solution)/shard_map/jvp()/reshape | solution.py:187
  142.8 19.9 %fusion.168 = (f32[2,1024,1,1024]{3,2,1,0:T(1,128)}, f32[2,1024,1,1024]{3,2,1,0:T(1,128)}) fusion(f32[2,1024,2,1024]{3,2,1,0:T(2,128)} %reshape.529), kind=kLoop, calls=%fused_computation.299 | loop fusion | bytes 33554432 | tf_op jit(solution)/shard_map/jvp()/slice | solution.py:111
  162.7 20.7 %copy.298 = f32[2,1024,1,1024]{1,3,0,2:T(8,128)} copy(f32[2,1024,1,1024]{3,2,1,0:T(1,128)} %get-tuple-element.787) | data formatting | bytes 16777216
  183.5 18.6 %fusion.121 = (f32[2,1024,1024]{1,2,0:T(8,128)}, f32[2,1024,1024]{1,2,0:T(8,128)}) fusion(f32[1024]{0:T(1024)S(1)} %bitcast.575, f32[2,1024,1024]{1,2,0:T(8,128)} %bitcast.539, pred[2,1024]{1,0:T(4,128)(4,1)S(1)} %get-tuple-element.814, f32[1024]{0:T(1024)S(1)} %bitcast.577, pred[2,1024]{1,0:T(4,128)(4,1)S(1)} %get-tuple-element.813, ...), kind=kLoop, calls=%fused_computation.198 | loop fusion | flops 33554432 | bytes 25194496 | tf_op jit(solution)/shard_map/jvp(jit(silu))/mul | solution.py:44
  248.6 113.8 %while.44 = (s32[]{:T(128)}, f32[2,16,64,128]{3,2,1,0:T(8,128)S(1)}, s32[2]{0:T(128)S(1)}, f32[4,2,256,16,64]{2,4,3,1,0:T(8,128)}, f32[4,2,16,64,128]{4,3,2,1,0:...) while((s32[]{:T(128)}, ...), condition=%wide.region_8.10_spmd.clone, body=%wide.region_5.9_spmd.clone.sunk | while | flops 3435234304 | bytes 18669148 | solution.py:94
  253.7 11.8 fusion.286
  282.1 11.8 fusion.286
  310.4 11.8 fusion.286
  338.8 11.8 fusion.286
  362.4 13.8 copy.257
  387.0 20.7 %copy.299 = f32[2,1024,1,1024]{1,3,0,2:T(8,128)} copy(f32[2,1024,1,1024]{3,2,1,0:T(1,128)} %get-tuple-element.788) | data formatting | bytes 16777216
  418.2 12.9 multiply_reduce_fusion.4
  446.3 13.0 fusion.177
  489.1 13.3 reshape.591
  502.4 14.0 copy.265
  533.2 354.7 %while.45 = (s32[]{:T(128)}, f32[2,16,64,128]{3,2,1,0:T(8,128)}, f32[4,2,256,16,64]{2,4,3,1,0:T(8,128)}, f32[4,2,256,16]{2,3,1,0:T(8,128)}, f32[4,2,256,128]{3,2...) while((s32[]{:T(128)}, f32[2,16,64,128]{3,2,1,0:T(8,128)}, ...), condition=%wide.region_25.27_spmd.clone, body=%wide.region_14.26_spmd.clone.sunk | while | flops 7891780608 | bytes 78642952 | solution.py:94
  576.7 13.5 fusion.308
  663.6 13.5 fusion.308
  750.4 13.4 fusion.308
  837.3 13.5 fusion.308
  887.9 13.9 copy.270
  921.8 21.5 %multiply_select_fusion = (f32[2,1024,1024]{1,2,0:T(8,128)}, f32[2,1024,1024]{1,2,0:T(8,128)S(1)}, f32[2,1024,1,1024]{1,3,0,2:T(8,128)}) fusion(f32[1024]{0:T(1024)S(1)} %bitcast.574, pred[2,1024]{1,0:T(4,128)(4,1)S(1)} %copy-done.48, f32[2,1024,1024]{1,2,0:T(8,128)} %get-tuple-element.768, f32[2,1024,1024]{1,2,0:T(8,128)} %reshape.540, ...), kind=kLoop, calls=%fused_computation.188 | loop fusion | flops 60817408 | bytes 67250176 | tf_op jit(solution)/shard_map/transpose(jvp(jit(_where)))/select_n | solution.py:43
  950.6 13.8 fusion.106
  973.7 21.4 %copy.273 = bf16[2,1024,2,1024]{3,2,1,0:T(2,128)(2,1)} copy(bf16[2,1024,2,1024]{1,3,0,2:T(8,128)(2,1)} %add_convert_fusion.1) | data formatting | bytes 16777216 | tf_op jit(solution)/shard_map/convert_element_type | solution.py:233
  1061.1 31.8 %add_convert_fusion = bf16[2048,2048]{1,0:T(8,128)(2,1)} fusion(f32[2048,2048]{1,0:T(8,128)} %fusion.179, f32[2048,2048]{1,0:T(8,128)} %fusion.154, f32[2048,2048]{1,0:T(8,128)} %fusion.178, bf16[2048,2048]{1,0:T(8,128)(2,1)} %bitcast.534, bf16[2048,2048]{1,0:T(8,128)(2,1)} %bitcast.544), kind=kOutput, calls=%fused_computation.141 | convolution fusion | flops 17196646400 | bytes 75497472 | tf_op jit(solution)/shard_map/dot_general | solution.py:244
  1109.8 15.3 %fusion.176 = f32[2048,2048]{1,0:T(8,128)} fusion(bf16[2048,1024]{1,0:T(8,128)(2,1)} %get-tuple-element.790, bf16[1024,2048]{1,0:T(8,128)(2,1)} %param.37), kind=kOutput, calls=%fused_computation.307 | convolution fusion | flops 8589934592 | bytes 25165824 | tf_op jit(solution)/shard_map/dot_general | solution.py:209
  1154.4 47.8 %reduce-scatter.5.cloned.1.call-done = bf16[512,2048]{1,0:T(8,128)(2,1)} async-done(((bf16[2048,2048]{1,0:T(8,128)(2,1)}), bf16[512,2048]{1,0:T(8,128)(2,1)}) %reduce-scatter.5.cloned.1.call-update) | async-done | bytes 2097168 | tf_op jit(solution)/shard_map/reduce_scatter | solution.py:247
  1204.5 71.5 %reduce-scatter.3.cloned.1.call-done = bf16[512,2048]{1,0:T(8,128)(2,1)} async-done(((bf16[2048,2048]{1,0:T(8,128)(2,1)}), bf16[512,2048]{1,0:T(8,128)(2,1)}) %reduce-scatter.3.cloned.1.call-update) | async-done | bytes 2097168 | tf_op jit(solution)/shard_map/reduce_scatter | solution.py:207
  1281.5 135.2 %all-reduce.24.cloned.1.call-done = (f32[2048,8,16]{0,2,1:T(8,128)}, f32[8,16,2048]{2,1,0:T(8,128)}) async-done(((f32[2048,8,16]{0,2,1:T(8,128)}, f32[8,16,2048]{2,1,0:T(8,128)}), (f32[2048,8,16]{0,2,1:T(8,128)}, f32[8,16,2048]{2,1,0:T(8,128)})) %all-reduce.24.cloned.1.call-update) | async-done | bytes 2097168 | tf_op jit(solution)/shard_map/psum | solution.py:263
  (711 shorter events, 680.2 us)
Async XLA Ops:
  7.2 224.6 %copy-start = (bf16[2048,256]{1,0:T(8,128)(2,1)S(1)}, bf16[2048,256]{1,0:T(8,128)(2,1)}, u32[]{:S(2)}) copy-start(bf16[2048,256]{1,0:T(8,128)(2,1)} %param.31) | copy-start | bytes 3145732
  7.2 68.0 %all-gather.3.cloned.1.call-start = ((), (), s32[]{:S(2)}) async-start(), calls=%async_computation.2 | async-start | bytes 10485760 | tf_op jit(solution)/shard_map/all_gather | solution.py:174
  14.0 426.3 %all-gather.5.cloned.1.call-start = ((), (), s32[]{:S(2)}) async-start(), calls=%async_computation.4 | async-start | bytes 10485760 | tf_op jit(solution)/shard_map/all_gather | solution.py:217
  14.8 1135.5 %all-reduce.26.cloned.1.call-start = ((), (), s32[]{:S(2)}) async-start(), calls=%async_computation.7 | async-start | bytes 1572864 | tf_op jit(solution)/shard_map/psum | solution.py:265
  16.6 65.2 %copy-start.93 = (s32[128]{0:T(128)}, s32[128]{0:T(128)S(1)}, u32[]{:S(2)}) copy-start(s32[128]{0:T(128)S(1)} %and_select_fusion) | copy-start | bytes 1540
  17.8 64.0 %copy-start.85 = (s32[1,8,2,128]{3,1,2,0:T(8,128)}, s32[1,8,2,128]{3,1,2,0:T(8,128)S(1)}, u32[]{:S(2)}) copy-start(s32[1,8,2,128]{3,1,2,0:T(8,128)S(1)} %copy.361) | copy-start | bytes 24580
  17.9 70.9 %copy-start.20 = (bf16[16,8,2,1024]{3,1,2,0:T(8,128)(2,1)}, bf16[16,8,2,1024]{3,1,2,0:T(8,128)(2,1)S(1)}, u32[]{:S(2)}) copy-start(bf16[16,8,2,1024]{3,1,2,0:T(8,128)(2,1)S(1)} %copy.331) | copy-start | bytes 1572868
  18.0 57.2 %copy-start.41 = (bf16[2048,16]{0,1:T(8,128)(2,1)S(1)}, bf16[2048,16]{0,1:T(8,128)(2,1)}, u32[]{:S(2)}) copy-start(bf16[2048,16]{0,1:T(8,128)(2,1)} %param.32) | copy-start | bytes 196612
  29.6 52.1 %copy-start.28 = (bf16[2048,8,16]{0,2,1:T(8,128)(2,1)S(1)}, bf16[2048,8,16]{0,2,1:T(8,128)(2,1)}, u32[]{:S(2)}) copy-start(bf16[2048,8,16]{0,2,1:T(8,128)(2,1)} %param.38) | copy-start | bytes 1572868
  29.7 207.9 %copy-start.45 = (pred[2,1024]{1,0:T(4,128)(4,1)}, pred[2,1024]{1,0:T(4,128)(4,1)S(1)}, u32[]{:S(2)}) copy-start(pred[2,1024]{1,0:T(4,128)(4,1)S(1)} %get-tuple-element.811) | copy-start | bytes 6148
  29.7 207.9 %copy-start.47 = (pred[2,1024]{1,0:T(4,128)(4,1)}, pred[2,1024]{1,0:T(4,128)(4,1)S(1)}, u32[]{:S(2)}) copy-start(pred[2,1024]{1,0:T(4,128)(4,1)S(1)} %get-tuple-element.812) | copy-start | bytes 6148
  29.7 207.9 %copy-start.49 = (pred[2,1024]{1,0:T(4,128)(4,1)}, pred[2,1024]{1,0:T(4,128)(4,1)S(1)}, u32[]{:S(2)}) copy-start(pred[2,1024]{1,0:T(4,128)(4,1)S(1)} %get-tuple-element.813) | copy-start | bytes 6148
  29.7 207.9 %copy-start.51 = (pred[2,1024]{1,0:T(4,128)(4,1)}, pred[2,1024]{1,0:T(4,128)(4,1)S(1)}, u32[]{:S(2)}) copy-start(pred[2,1024]{1,0:T(4,128)(4,1)S(1)} %get-tuple-element.814) | copy-start | bytes 6148
  29.7 153.7 %copy-start.61 = (f32[1,1024]{1,0:T(1,128)}, f32[1,1024]{1,0:T(1,128)S(1)}, u32[]{:S(2)}) copy-start(f32[1,1024]{1,0:T(1,128)S(1)} %get-tuple-element.801) | copy-start | bytes 12292
  29.7 153.7 %copy-start.63 = (f32[1,1024]{1,0:T(1,128)}, f32[1,1024]{1,0:T(1,128)S(1)}, u32[]{:S(2)}) copy-start(f32[1,1024]{1,0:T(1,128)S(1)} %get-tuple-element.800) | copy-start | bytes 12292
  29.8 153.7 %copy-start.65 = (f32[1,1024]{1,0:T(1,128)}, f32[1,1024]{1,0:T(1,128)S(1)}, u32[]{:S(2)}) copy-start(f32[1,1024]{1,0:T(1,128)S(1)} %get-tuple-element.802) | copy-start | bytes 12292
  29.8 153.7 %copy-start.67 = (f32[1,1024]{1,0:T(1,128)}, f32[1,1024]{1,0:T(1,128)S(1)}, u32[]{:S(2)}) copy-start(f32[1,1024]{1,0:T(1,128)S(1)} %get-tuple-element.803) | copy-start | bytes 12292
  29.8 183.3 %copy-start.71 = (f32[16]{0:T(128)}, f32[16]{0:T(128)S(1)}, u32[]{:S(2)}) copy-start(f32[16]{0:T(128)S(1)} %get-tuple-element.819) | copy-start | bytes 196
  29.8 183.3 %copy-start.82 = (f32[16]{0:T(128)}, f32[16]{0:T(128)S(1)}, u32[]{:S(2)}) copy-start(f32[16]{0:T(128)S(1)} %get-tuple-element.818) | copy-start | bytes 196
  29.8 207.8 %copy-start.74 = (f32[1,256]{1,0:T(1,128)}, f32[1,256]{1,0:T(1,128)S(1)}, u32[]{:S(2)}) copy-start(f32[1,256]{1,0:T(1,128)S(1)} %get-tuple-element.808) | copy-start | bytes 3076
  29.8 207.8 %copy-start.76 = (f32[1,256]{1,0:T(1,128)}, f32[1,256]{1,0:T(1,128)S(1)}, u32[]{:S(2)}) copy-start(f32[1,256]{1,0:T(1,128)S(1)} %get-tuple-element.809) | copy-start | bytes 3076
  29.8 207.8 %copy-start.78 = (f32[1,256]{1,0:T(1,128)}, f32[1,256]{1,0:T(1,128)S(1)}, u32[]{:S(2)}) copy-start(f32[1,256]{1,0:T(1,128)S(1)} %get-tuple-element.810) | copy-start | bytes 3076
  29.9 207.8 %copy-start.80 = (f32[1,256]{1,0:T(1,128)}, f32[1,256]{1,0:T(1,128)S(1)}, u32[]{:S(2)}) copy-start(f32[1,256]{1,0:T(1,128)S(1)} %get-tuple-element.807) | copy-start | bytes 3076
  921.8 21.5 %copy-start.50 = (pred[2,1024]{1,0:T(4,128)(4,1)S(1)}, pred[2,1024]{1,0:T(4,128)(4,1)}, u32[]{:S(2)}) copy-start(pred[2,1024]{1,0:T(4,128)(4,1)} %copy-done.49) | copy-start | bytes 6148
  921.8 21.5 %copy-start.52 = (pred[2,1024]{1,0:T(4,128)(4,1)S(1)}, pred[2,1024]{1,0:T(4,128)(4,1)}, u32[]{:S(2)}) copy-start(pred[2,1024]{1,0:T(4,128)(4,1)} %copy-done.51) | copy-start | bytes 6148
  1052.8 149.4 %reduce-scatter.5.cloned.1.call-start = ((), (), s32[]{:S(2)}) async-start(), calls=%async_computation.5 | async-start | bytes 10485760 | tf_op jit(solution)/shard_map/reduce_scatter | solution.py:247
  1092.9 183.1 %reduce-scatter.3.cloned.1.call-start = ((), (), s32[]{:S(2)}) async-start(), calls=%async_computation.3 | async-start | bytes 10485760 | tf_op jit(solution)/shard_map/reduce_scatter | solution.py:207
  1136.7 279.9 %all-reduce.24.cloned.1.call-start = ((), (), s32[]{:S(2)}) async-start(), calls=%async_computation.6 | async-start | bytes 4194304 | tf_op jit(solution)/shard_map/psum | solution.py:263
  1143.9 58.3 %copy-start.7 = (bf16[512,2048]{1,0:T(8,128)(2,1)S(1)}, bf16[512,2048]{1,0:T(8,128)(2,1)}, u32[]{:S(2)}) copy-start(bf16[512,2048]{1,0:T(8,128)(2,1)} %param.24) | copy-start | bytes 6291460
  1143.9 58.3 %copy-start.53 = (f32[2048]{0:T(1024)S(1)}, f32[2048]{0:T(1024)}, u32[]{:S(2)}) copy-start(f32[2048]{0:T(1024)} %param.29) | copy-start | bytes 24580
  1143.9 132.2 %copy-start.70 = (f32[512]{0:T(512)S(1)}, f32[512]{0:T(512)}, u32[]{:S(2)}) copy-start(f32[512]{0:T(512)} %copy-done.69) | copy-start | bytes 6148
  1143.9 132.2 %copy-start.84 = (f32[512]{0:T(512)S(1)}, f32[512]{0:T(512)}, u32[]{:S(2)}) copy-start(f32[512]{0:T(512)} %get-tuple-element.815) | copy-start | bytes 6148
  (141 other events, 1565.1 us)
Sparse Core Ops, SparseCore 0:
  14.1 61.0 all-gather.2
  76.8 58.2 all-gather.4
  1052.9 76.2 all-reduce.25
  1131.6 70.5 reduce-scatter.4
  1204.6 71.3 reduce-scatter.2
  1282.0 134.6 all-reduce.23
where the time goes:
time: 1450 us; the launch traced here: 1430 us
  matrix products  467 us (32%)
  local copies, waits for them, and re-layouts  381 us (26%)
  waiting for transfers between devices  300 us (21%)
  other arithmetic  243 us (17%)
  between operations  15.6 us (1%)
    dot_general x12, matrix products, advance(): jnp.einsum('rijh,rjhp->rihp', weights * scores[..., None], xdt, precision...  140 us
    psum x1, waiting for transfers between devices, on_device(): lax.psum((grad_in_down, output_up_gradient), ('dp', 'tensor'))  135 us
    unnamed x180, local copies, waits for them, and re-layouts  80.4 us
    reduce_scatter x1, waiting for transfers between devices, on_device(): lax.psum_scatter((jnp.dot(mixer_input, output_projection_weight, preferre...  71.5 us
    dot_general x16, matrix products, advance(): jnp.einsum('rin,rhpn->rihp', out_blk, state, precision=top_precision)  60.2 us
    dot_general x12, matrix products, advance(): jnp.einsum('rjh,rjn,rjhp->rhpn', tail_w, in_blk, xdt, precision=top_preci...  49.7 us
    squeeze x32, local copies, waits for them, and re-layouts, state_scan(): lax.scan(jax.checkpoint(advance), (start_state, start_prev), inputs)  48.2 us
    reduce_scatter x1, waiting for transfers between devices, on_device(): lax.psum_scatter((summed + jnp.dot(grad_mid, input_down_factor.T, preferr...  47.8 us
  transfers between devices with their start and end apart: 6, of which 4 were waited for; matrix products, arithmetic and copies ran while one was open for 34% of the time, Pallas kernels for 0%

commit v1 on v0

v1 whole, which is shorter than its diff:
```python
import functools

import jax
import jax.numpy as jnp
from jax import lax
from jax.experimental import pallas as pl
from jax.experimental.pallas import tpu as pltpu
from jax.sharding import PartitionSpec as P

F32, BF16 = jnp.float32, jnp.bfloat16
L = 128
HEAD = 64
HALO = 8
NN = (((1,), (0,)), ((), ()))
NT = (((1,), (1,)), ((), ()))
TN = (((0,), (0,)), ((), ()))


def mm(a, b, dims=NN):
    return lax.dot_general(a, b, dims, preferred_element_type=F32)


def split2(v):
    hi = v.astype(BF16)
    return hi, (v - hi.astype(F32)).astype(BF16)


def split3(v):
    hi = v.astype(BF16)
    rest = v - hi.astype(F32)
    mid = rest.astype(BF16)
    return hi, mid, (rest - mid.astype(F32)).astype(BF16)


def sigmoid(v):
    return 0.5 * jnp.tanh(0.5 * v) + 0.5


def starts_of(pos, ends, count):
    start = jnp.zeros_like(pos)
    for k in range(count - 1):
        start = jnp.where(pos >= ends[k], jnp.maximum(start, ends[k]), start)
    return start


def scalar_start(pos, ends, count):
    start = jnp.int32(0)
    for k in range(count - 1):
        start = jnp.where(pos >= ends[k], jnp.maximum(start, ends[k]), start)
    return start


def chunk_geometry(t0, ends, count):
    rows = t0 + lax.broadcasted_iota(jnp.int32, (L, L), 0)
    cols = t0 + lax.broadcasted_iota(jnp.int32, (L, L), 1)
    row_start = starts_of(rows, ends, count)
    col_start = starts_of(cols, ends, count)
    last_start = scalar_start(t0 + (L - 1), ends, count)
    return rows, cols, row_start, col_start, last_start


def conv_tile(ext, taps, within):
    total = ext[HALO:] * taps[3:4] + taps[4:5]
    for lag in range(1, 4):
        moved = pltpu.roll(ext, lag, 0)[HALO:]
        total = total + jnp.where(within >= lag, moved, 0.0) * taps[3 - lag : 4 - lag]
    return total


def conv_back(ext, taps, ok):
    size = ext.shape[0]
    total = ext[:L] * taps[3:4]
    for lag in range(1, 4):
        moved = pltpu.roll(ext, size - lag, 0)[:L]
        total = total + jnp.where(ok[lag - 1], moved, 0.0) * taps[3 - lag : 4 - lag]
    return total


def step_terms(dt_raw, bias, rate, low_mask):
    raw = dt_raw + bias
    dt = jnp.maximum(raw, 0.0) + jnp.log1p(jnp.exp(-jnp.abs(raw)))
    decay = dt * rate
    cum = sum(mm(low_mask, part) for part in split3(decay))
    return raw, dt, cum


def lane_pair(low, value, h):
    first = jnp.broadcast_to(value[:, h : h + 1], (L, 128))
    second = jnp.broadcast_to(value[:, h + 1 : h + 2], (L, 128))
    return first, second, jnp.where(low, first, second)


def forward_kernel(
    count, ends, z_ref, x_ref, bc_ref, dt_ref, taps_ref, bct_ref, head_ref, chan_ref,
    y_ref, g_ref, sum_ref, st_ref, state, xprev, bcprev,
):
    c = pl.program_id(0)
    pairs = x_ref.shape[1] // 128

    @pl.when(c == 0)
    def _():
        state[...] = jnp.zeros_like(state)
        xprev[...] = jnp.zeros_like(xprev)
        bcprev[...] = jnp.zeros_like(bcprev)

    t0 = c * L
    rows, cols, row_start, col_start, last_start = chunk_geometry(t0, ends, count)
    within = rows - row_start
    mask = (row_start == col_start) & (cols <= rows)
    low_mask = jnp.where(mask, 1.0, 0.0).astype(BF16)
    contin = row_start < t0
    tail = row_start == last_start
    keep = jnp.where(last_start < t0, 1.0, 0.0).astype(F32)
    low = lax.broadcasted_iota(jnp.int32, (L, 128), 1) < HEAD

    bc_halves = []
    for half in range(2):
        cut = slice(half * 128, half * 128 + 128)
        ext = jnp.concatenate([bcprev[:, cut], bc_ref[:, cut]], axis=0)
        pre = conv_tile(ext, bct_ref[:, cut], within)
        bc_halves.append((pre * sigmoid(pre)))
    b_mat, c_mat = bc_halves
    b_low, c_low = b_mat.astype(BF16), c_mat.astype(BF16)
    b_turn = b_mat.T.astype(BF16)
    scores = jnp.where(mask, mm(c_low, b_low, NT), 0.0)

    _, dt, cum = step_terms(dt_ref[...], head_ref[0:1], head_ref[1:2], low_mask)
    cum_turn = cum.T

    squares = jnp.zeros((L, 128), F32)
    for p in range(pairs):
        cut = slice(p * 128, p * 128 + 128)
        ext = jnp.concatenate([xprev[:, cut], x_ref[:, cut]], axis=0)
        pre = conv_tile(ext, taps_ref[:, cut], within)
        xc = pre * sigmoid(pre)
        c0, c1, c_both = lane_pair(low, cum, 2 * p)
        _, _, dt_both = lane_pair(low, dt, 2 * p)
        xt = xc * dt_both
        xb = xt.astype(BF16)
        zero = jnp.zeros_like(xb)
        x2 = jnp.concatenate([jnp.where(low, xb, zero), jnp.where(low, zero, xb)], axis=0)
        g0 = (scores * jnp.exp(jnp.minimum(c0 - cum_turn[2 * p : 2 * p + 1], 0.0))).astype(BF16)
        g1 = (scores * jnp.exp(jnp.minimum(c1 - cum_turn[2 * p + 1 : 2 * p + 2], 0.0))).astype(BF16)
        inside = mm(jnp.concatenate([g0, g1], axis=1), x2)
        old = state[:, cut]
        old_low = old.astype(BF16)
        st_ref[0, :, cut] = old_low
        carried = jnp.where(contin, jnp.exp(c_both), 0.0)
        y = inside + mm(c_low, old_low) * carried
        y_ref[:, cut] = y
        c_last = c_both[L - 1 :, :]
        tail_w = jnp.where(tail, jnp.exp(c_last - c_both), 0.0)
        state[:, cut] = (keep * jnp.exp(c_last)) * old + mm(b_turn, (xt * tail_w).astype(BF16))
        z = z_ref[:, cut]
        gated = (y + chan_ref[0:1, cut] * xc) * (z * sigmoid(z))
        gained = gated * chan_ref[1:2, cut]
        g_ref[:, cut] = gained.astype(BF16)
        squares = squares + gated * gated
    ones = jnp.ones((8, 128), BF16)
    sq_row = sum(mm(ones, part, NT) for part in split3(squares))
    sum_ref[...] = sq_row
    xprev[...] = x_ref[L - HALO :, :]
    bcprev[...] = bc_ref[L - HALO :, :]


def backward_kernel(
    count, seq, ends, z_ref, x_ref, xh_ref, bc_ref, bch_ref, dt_ref, gm_ref, y_ref, st_ref, rk_ref,
    taps_ref, bct_ref, head_ref, chan_ref,
    dzx_ref, dbc_ref, ddt_ref, dstate, dnext, dbnext, ends_row,
):
    g = pl.program_id(0)
    c = pl.num_programs(0) - 1 - g
    width = x_ref.shape[1]
    pairs = width // 128

    @pl.when(g == 0)
    def _():
        dstate[...] = jnp.zeros_like(dstate)
        dnext[...] = jnp.zeros_like(dnext)
        dbnext[...] = jnp.zeros_like(dbnext)
        ends_row[...] = jnp.zeros_like(ends_row)

    t0 = c * L
    rows, cols, row_start, col_start, last_start = chunk_geometry(t0, ends, count)
    within = rows - row_start
    same = row_start == col_start
    low_mask = jnp.where(same & (cols <= rows), 1.0, 0.0).astype(BF16)
    up = same & (rows <= cols)
    up_mask = jnp.where(up, 1.0, 0.0).astype(BF16)
    contin = row_start < t0
    tail = row_start == last_start
    keep = jnp.where(last_start < t0, 1.0, 0.0).astype(F32)
    lane = lax.broadcasted_iota(jnp.int32, (L, 128), 1)
    sub = lax.broadcasted_iota(jnp.int32, (L, 128), 0)
    low = lane < HEAD
    ok = [
        (rows + lag < seq) & (starts_of(rows + lag, ends, count) <= rows) for lag in range(1, 4)
    ]

    parts = []
    for half in range(2):
        cut = slice(half * 128, half * 128 + 128)
        ext = jnp.concatenate([bch_ref[:, cut], bc_ref[:, cut]], axis=0)
        pre = conv_tile(ext, bct_ref[:, cut], within)
        sg = sigmoid(pre)
        act = pre * sg
        parts.append((act, sg + act * (1.0 - sg)))
    (b_mat, b_slope), (c_mat, c_slope) = parts
    b_low, c_low = b_mat.astype(BF16), c_mat.astype(BF16)
    c_turn = c_mat.T.astype(BF16)
    scores = jnp.where(up, mm(b_low, c_low, NT), 0.0)

    raw, dt, cum = step_terms(dt_ref[...], head_ref[0:1], head_ref[1:2], low_mask)
    cum_turn = cum.T
    inv, kappa = rk_ref[:, :128], rk_ref[:, 128:]

    d_scores = jnp.zeros((L, L), F32)
    d_b = jnp.zeros((L, 128), F32)
    d_c = jnp.zeros((L, 128), F32)
    d_cum = jnp.zeros((L, 128), F32)
    d_dt = jnp.zeros((L, 128), F32)
    d_end = jnp.zeros((8, 128), F32)
    for p in range(pairs):
        cut = slice(p * 128, p * 128 + 128)
        pick = jnp.where(lane == 2 * p + jnp.where(sub >= HEAD, 1, 0), 1.0, 0.0).astype(BF16)
        ext = jnp.concatenate([xh_ref[:, cut], x_ref[:, cut]], axis=0)
        taps = taps_ref[:, cut]
        pre = conv_tile(ext, taps, within)
        sg = sigmoid(pre)
        xc = pre * sg
        skip = chan_ref[0:1, cut]
        z = z_ref[:, cut]
        sz = sigmoid(z)
        sil = z * sz
        y = y_ref[:, cut]
        yt = y + skip * xc
        gg = inv * (gm_ref[:, cut] * chan_ref[1:2, cut] - kappa * (yt * sil))
        dzx_ref[:, cut] = (gg * yt * (sz + sil * (1.0 - sz))).astype(BF16)
        dyt = gg * sil
        dyb = dyt.astype(BF16)
        zero = jnp.zeros_like(dyb)
        dy2 = jnp.concatenate([jnp.where(low, dyb, zero), jnp.where(low, zero, dyb)], axis=0)
        c0, c1, c_both = lane_pair(low, cum, 2 * p)
        _, _, dt_both = lane_pair(low, dt, 2 * p)
        xt = xc * dt_both
        xb = xt.astype(BF16)
        dg = mm(xb, dy2, NT)
        w0 = jnp.exp(jnp.minimum(cum_turn[2 * p : 2 * p + 1] - c0, 0.0))
        w1 = jnp.exp(jnp.minimum(cum_turn[2 * p + 1 : 2 * p + 2] - c1, 0.0))
        d_scores = d_scores + dg[:, :L] * w0 + dg[:, L:] * w1
        gt = jnp.concatenate([(scores * w0).astype(BF16), (scores * w1).astype(BF16)], axis=1)
        carried = jnp.where(contin, jnp.exp(c_both), 0.0)
        c_last = c_both[L - 1 :, :]
        tail_w = jnp.where(tail, jnp.exp(c_last - c_both), 0.0)
        ds = dstate[:, cut]
        ds_low = ds.astype(BF16)
        dxt = mm(gt, dy2) + mm(b_low, ds_low) * tail_w
        dyc = (dyt * carried).astype(BF16)
        st = st_ref[0, :, cut]
        d_c = d_c + mm(dyc, st, NT)
        d_b = d_b + mm((xt * tail_w).astype(BF16), ds_low, NT)
        ds_new = (keep * jnp.exp(c_last)) * ds + mm(c_turn, dyc)
        dstate[:, cut] = ds_new
        both = jnp.sum(ds_new * st.astype(F32), axis=0, keepdims=True)
        both = jnp.broadcast_to(both, (8, 128))
        d_end = d_end + sum(mm(part, pick) for part in split2(both))
        v = dyb.astype(F32) * y - xb.astype(F32) * dxt
        d_cum = d_cum + sum(mm(part, pick) for part in split2(v))
        d_dt = d_dt + sum(mm(part, pick) for part in split2(dxt * xc))
        dpre = (skip * dyt + dt_both * dxt) * (sg + xc * (1.0 - sg))
        ext = jnp.concatenate([dpre, dnext[:, cut]], axis=0)
        dzx_ref[:, slice(width + p * 128, width + p * 128 + 128)] = conv_back(ext, taps, ok).astype(BF16)
        dnext[:, cut] = dpre[:HALO]

    d_scores = jnp.where(up, d_scores, 0.0)
    d_b = d_b + mm(d_scores.astype(BF16), c_low)
    d_c = d_c + mm(d_scores.T.astype(BF16), b_low)
    for half, (grad, slope) in enumerate(((d_b, b_slope), (d_c, c_slope))):
        cut = slice(half * 128, half * 128 + 128)
        dpre = grad * slope
        ext = jnp.concatenate([dpre, dbnext[:, cut]], axis=0)
        dbc_ref[:, cut] = conv_back(ext, bct_ref[:, cut], ok).astype(BF16)
        dbnext[:, cut] = dpre[:HALO]
    d_cum = d_cum + jnp.where(sub == L - 1, ends_row[0:1, :], 0.0)
    ends_row[...] = d_end
    d_decay = sum(mm(up_mask, part) for part in split3(d_cum))
    ddt_ref[...] = ((d_dt + head_ref[1:2] * d_decay) * sigmoid(raw)).astype(BF16)


def mixer_forward(ends, zx, small, taps, bctaps, heads, chans):
    seq, width = zx.shape[0], zx.shape[1] // 2
    count = ends.shape[0] - 1
    chunks = seq // L
    place = lambda c, e: lax.rem(c + e[count] * (chunks // 2), chunks)
    fixed = lambda shape: pl.BlockSpec(shape, lambda c, e: (0,) * len(shape))
    blk = lambda w, j=0: pl.BlockSpec((L, w), lambda c, e: (place(c, e), j))
    return pl.pallas_call(
        functools.partial(forward_kernel, count),
        grid_spec=pltpu.PrefetchScalarGridSpec(
            num_scalar_prefetch=1,
            grid=(chunks,),
            in_specs=[
                blk(width, 0), blk(width, 1), blk(256, 0), blk(128, 2),
                fixed((5, width)), fixed((5, 256)), fixed((2, 128)), fixed((2, width)),
            ],
            out_specs=[
                blk(width), blk(width), pl.BlockSpec((8, L), lambda c, e: (0, place(c, e))),
                pl.BlockSpec((1, 128, width), lambda c, e: (c, 0, 0)),
            ],
            scratch_shapes=[
                pltpu.VMEM((128, width), F32), pltpu.VMEM((HALO, width), F32), pltpu.VMEM((HALO, 256), F32),
            ],
        ),
        out_shape=[
            jax.ShapeDtypeStruct((seq, width), F32),
            jax.ShapeDtypeStruct((seq, width), BF16),
            jax.ShapeDtypeStruct((8, seq), F32),
            jax.ShapeDtypeStruct((chunks, 128, width), BF16),
        ],
        compiler_params=pltpu.CompilerParams(dimension_semantics=("arbitrary",)),
        cost_estimate=pl.CostEstimate(
            flops=seq * width * 1200, bytes_accessed=seq * width * 16, transcendentals=seq * width * 6
        ),
        name="mixer_forward",
    )(ends, zx, zx, small, small, taps, bctaps, heads, chans)


def mixer_backward(ends, zx, small, gm, y, states, rk, taps, bctaps, heads, chans):
    seq, width = gm.shape
    count = ends.shape[0] - 1
    chunks = seq // L
    last = chunks - 1
    step = L // HALO
    place = lambda c, e: lax.rem(c + e[count] * (chunks // 2), chunks)
    fixed = lambda shape: pl.BlockSpec(shape, lambda g, e: (0,) * len(shape))
    blk = lambda w, j=0: pl.BlockSpec((L, w), lambda g, e: (place(last - g, e), j))
    halo = lambda w, j=0: pl.BlockSpec(
        (HALO, w), lambda g, e: (place(jnp.maximum(last - g - 1, 0), e) * step + step - 1, j)
    )
    return pl.pallas_call(
        functools.partial(backward_kernel, count, seq),
        grid_spec=pltpu.PrefetchScalarGridSpec(
            num_scalar_prefetch=1,
            grid=(chunks,),
            in_specs=[
                blk(width, 0), blk(width, 1), halo(width, 1), blk(256, 0), halo(256, 0), blk(128, 2),
                blk(width), blk(width), pl.BlockSpec((1, 128, width), lambda g, e: (last - g, 0, 0)), blk(256),
                fixed((5, width)), fixed((5, 256)), fixed((2, 128)), fixed((2, width)),
            ],
            out_specs=[blk(2 * width), blk(256), blk(128)],
            scratch_shapes=[
                pltpu.VMEM((128, width), F32), pltpu.VMEM((HALO, width), F32), pltpu.VMEM((HALO, 256), F32),
                pltpu.VMEM((8, 128), F32),
            ],
        ),
        out_shape=[
            jax.ShapeDtypeStruct((seq, 2 * width), BF16),
            jax.ShapeDtypeStruct((seq, 256), BF16),
            jax.ShapeDtypeStruct((seq, 128), BF16),
        ],
        compiler_params=pltpu.CompilerParams(dimension_semantics=("arbitrary",)),
        cost_estimate=pl.CostEstimate(
            flops=seq * width * 3000, bytes_accessed=seq * width * 24, transcendentals=seq * width * 8
        ),
        name="mixer_backward",
    )(ends, zx, zx, zx, small, small, small, gm, y, states, rk, taps, bctaps, heads, chans)


EPS = 1e-05
ROW_LEN = 1024


def dot(a, b, dims=NN):
    return lax.dot_general(a, b, dims, preferred_element_type=F32)


def row_places(own_row, core, flipped):
    shift = core * (ROW_LEN // 2) if flipped else 0
    return jnp.remainder(jnp.arange(ROW_LEN, dtype=jnp.int32) + shift, ROW_LEN)


def row_select(ends, ids, places, columns):
    segment = jnp.sum((places[:, None] >= ends[None, :]).astype(jnp.int32), axis=1)
    member = segment[:, None] == jnp.arange(ends.shape[0], dtype=jnp.int32)[None, :]
    adapter = jnp.sum(jnp.where(member, ids[None, :], 0), axis=1)
    return (adapter[:, None] == columns[None, :]).astype(F32)


def flip(v):
    half = v.shape[-1] // 2
    return jnp.concatenate([v[..., half:], v[..., :half]], axis=-1)


class PairedLinks:
    flipped = True

    def __init__(self):
        me = lax.axis_index("tensor")
        self.own_row, self.core = me // 2, me % 2
        self.across = [(i, i ^ 2) for i in range(4)]
        self.beside = [(i, i ^ 1) for i in range(4)]

    def far(self, v):
        return lax.ppermute(v, "tensor", self.across)

    def near(self, v):
        return lax.ppermute(v, "tensor", self.beside)

    def gather(self, v):
        own = jnp.concatenate([v, self.near(v)], axis=0)
        came = self.far(v)
        return own, jnp.concatenate([came, self.near(came)], axis=0)

    def sum_stats(self, own, other):
        both = jnp.stack([own, other])
        both = both + flip(self.near(both))
        came = self.far(both)
        return both[0] + came[1], both[1] + came[0]

    def reduce_other(self, project):
        half = ROW_LEN // 2
        second = self.near(project(half, ROW_LEN).astype(BF16))
        first = project(0, half)
        return self.far((first + second.astype(F32)).astype(BF16))

    def reduce_own(self, project, came):
        half = ROW_LEN // 2
        second = self.near(project(half, ROW_LEN).astype(BF16))
        return project(0, half) + second.astype(F32) + came.astype(F32)

    def mine(self, own_stat):
        return own_stat[: ROW_LEN // 2]


class GroupLinks:
    flipped = False

    def __init__(self, parts, rows):
        me = lax.axis_index("tensor")
        per_row = parts // rows
        self.own_row, self.core = me // per_row, me % per_row
        self.per_row = per_row

    def gather(self, v):
        whole = lax.all_gather(v, "tensor", axis=0, tiled=True).reshape(2, ROW_LEN, v.shape[1])
        return (
            lax.dynamic_index_in_dim(whole, self.own_row, 0, False),
            lax.dynamic_index_in_dim(whole, 1 - self.own_row, 0, False),
        )

    def sum_stats(self, own, other):
        first = jnp.where(self.own_row == 0, own, other)
        second = jnp.where(self.own_row == 0, other, own)
        total = lax.psum(jnp.stack([first, second]), "tensor")
        return (
            lax.dynamic_index_in_dim(total, self.own_row, 0, False),
            lax.dynamic_index_in_dim(total, 1 - self.own_row, 0, False),
        )

    def reduce_other(self, project):
        return project(0, ROW_LEN).astype(BF16)

    def reduce_own(self, project, other):
        own = project(0, ROW_LEN).astype(BF16)
        first = jnp.where(self.own_row == 0, own, other)
        second = jnp.where(self.own_row == 0, other, own)
        whole = jnp.concatenate([first, second], axis=0)
        return lax.psum_scatter(whole, "tensor", scatter_dimension=0, tiled=True).astype(F32)

    def mine(self, own_stat):
        size = ROW_LEN // self.per_row
        return lax.dynamic_slice_in_dim(own_stat, self.core * size, size, 0)


def on_device(
    tokens, cotangent, lengths, ids, deal, norm_gain, zx_weight, state_weight, step_weight,
    conv_taps, state_taps, head_values, gated_gain, out_weight, in_down, in_up, out_down, out_up,
):
    tok_dev, model = tokens.shape
    parts = lax.axis_size("tensor")
    rows = tok_dev * parts // ROW_LEN
    assert rows == 2
    links = PairedLinks() if parts == 4 else GroupLinks(parts, rows)
    adapters, rank = in_down.shape[1:]
    reduced = adapters * rank
    width = zx_weight.shape[2]
    inner = width * parts
    heads_here = width // HEAD
    in_down = in_down.reshape(model, reduced)
    in_up = in_up.reshape(reduced, 2 * width)
    out_down = out_down.reshape(width, reduced)
    out_up = out_up.reshape(reduced, model)
    zx_weight = zx_weight.reshape(model, 2 * width)
    pad = lambda v: jnp.pad(v, ((0, 0), (0, 128 - heads_here)))
    small_weight = jnp.concatenate([state_weight, pad(step_weight), in_down], axis=1)
    heads = jnp.concatenate([pad(head_values[0:1]), pad(-jnp.exp(head_values[1:2]))], axis=0)
    chans = jnp.stack([jnp.repeat(head_values[2], HEAD), gated_gain])
    columns = jnp.arange(reduced, dtype=jnp.int32) // rank

    places = row_places(links.own_row, links.core, links.flipped)
    turn = (links.core if links.flipped else 0) * jnp.ones((1,), jnp.int32)
    base = lax.axis_index("dp") * rows
    row_data = []
    for which in (links.own_row, 1 - links.own_row):
        packed = lax.dynamic_index_in_dim(deal, base + which, 0, False)
        ends = jnp.cumsum(lax.dynamic_index_in_dim(lengths, packed, 0, False))
        row_ids = lax.dynamic_index_in_dim(ids, packed, 0, False)
        select = row_select(ends, row_ids, places, columns)
        row_data.append((jnp.concatenate([ends, turn]).astype(jnp.int32), select))

    residual = tokens.astype(F32)
    inv_rms = lax.rsqrt(jnp.mean(residual * residual, axis=1, keepdims=True) + EPS)
    normed = links.gather((residual * inv_rms * norm_gain).astype(BF16))
    cots = links.gather(cotangent)

    def forward(row):
        ends, select = row_data[row]
        nb = normed[row]
        small = dot(nb, small_weight)
        lora = (small[:, 384:] * select).astype(BF16)
        zx = dot(nb, zx_weight) + dot(lora, in_up)
        y, gained, squares, states = mixer_forward(ends, zx, small, conv_taps, state_taps, heads, chans)
        return small, lora, zx, y, gained, squares, states

    def cotangents(row):
        low = (dot(cots[row], out_up, NT) * row_data[row][1]).astype(BF16)
        return low, dot(cots[row], out_weight, NT) + dot(low, out_down, NT)

    def project_out(row, gained):
        def part(first, last):
            piece = gained[first:last]
            low = (dot(piece, out_down) * row_data[row][1][first:last]).astype(BF16)
            return dot(piece, out_weight) + dot(low, out_up)

        return part

    fw = [forward(0), forward(1)]
    back = [cotangents(0), cotangents(1)]
    crosses = [jnp.sum(back[r][1] * fw[r][4].astype(F32), axis=1) for r in range(2)]
    stats = [jnp.stack([fw[r][5][0], crosses[r]]) for r in range(2)]
    stats = links.sum_stats(stats[0], stats[1])
    came = links.reduce_other(project_out(1, fw[1][4]))
    out_sum = links.reduce_own(project_out(0, fw[0][4]), came)
    inv, rks = [], []
    for r in range(2):
        scale = lax.rsqrt(stats[r][0] / inner + EPS)
        kappa = scale * scale * (stats[r][1] / inner)
        inv.append(scale)
        rks.append(
            jnp.concatenate(
                [jnp.broadcast_to(scale[:, None], (ROW_LEN, 128)), jnp.broadcast_to(kappa[:, None], (ROW_LEN, 128))],
                axis=1,
            )
        )
    output = (residual + links.mine(inv[0])[:, None] * out_sum).astype(BF16)

    grads = [None, None]
    out_grads = [None, None]
    for r in (1, 0):
        low, gm = back[r]
        gained = fw[r][4]
        select = row_data[r][1]
        scaled_low = (low.astype(F32) * inv[r][:, None]).astype(BF16)
        lora_back = (dot(gained, out_down) * select * inv[r][:, None]).astype(BF16)
        out_grads[r] = (
            lax.dot_general(gained, scaled_low, TN, preferred_element_type=F32),
            lax.dot_general(lora_back, cots[r], TN, preferred_element_type=F32),
        )
    down_total, up_total = [a + b for a, b in zip(*out_grads)]

    in_grads = [None, None]
    for r in (1, 0):
        ends, select = row_data[r]
        small, lora, zx, y, gained, _, states = fw[r]
        dzx, dbc, ddt = mixer_backward(
            ends, zx, small, back[r][1], y, states, rks[r], conv_taps, state_taps, heads, chans
        )
        mid = (dot(dzx, in_up, NT) * select).astype(BF16)
        in_grads[r] = (
            lax.dot_general(lora, dzx, TN, preferred_element_type=F32),
            lax.dot_general(normed[r], mid, TN, preferred_element_type=F32),
        )
        dsmall = jnp.concatenate([dbc, ddt, mid], axis=1)

        def part(first, last, dzx=dzx, dsmall=dsmall):
            return dot(dzx[first:last], zx_weight, NT) + dot(dsmall[first:last], small_weight, NT)

        grads[r] = part
        if r == 1:
            came = links.reduce_other(part)
    grad_normed = links.reduce_own(grads[0], came)
    in_up_total, in_down_total = [a + b for a, b in zip(*in_grads)]

    scaled = grad_normed * norm_gain
    grad_tokens = (
        cotangent.astype(F32)
        + inv_rms * scaled
        - residual * inv_rms**3 * (jnp.sum(scaled * residual, axis=1, keepdims=True) / model)
    )
    out_up_sum = lax.psum(up_total.astype(BF16), ("dp", "tensor")).astype(F32)
    out_down_sum = lax.psum(down_total.astype(BF16), "dp").astype(F32)
    in_down_sum = lax.psum(in_down_total.astype(BF16), ("dp", "tensor")).astype(F32)
    in_up_sum = lax.psum(in_up_total.astype(BF16), "dp").astype(F32)
    return (
        output,
        grad_tokens,
        in_down_sum.reshape(model, adapters, rank),
        in_up_sum.reshape(adapters, rank, 2, width),
        out_down_sum.reshape(width, adapters, rank),
        out_up_sum.reshape(adapters, rank, model),
    )


def solution(mesh):
    return jax.shard_map(
        on_device,
        mesh=mesh,
        in_specs=(
            P(("dp", "tensor"), None), P(("dp", "tensor"), None), P(), P(), P(), P(),
            P(None, None, "tensor"), P(), P(None, "tensor"), P(None, "tensor"), P(), P(None, "tensor"),
            P("tensor"), P("tensor", None), P(), P(None, None, None, "tensor"), P("tensor", None, None), P(),
        ),
        out_specs=(
            P(("dp", "tensor"), None), P(("dp", "tensor"), None), P(),
            P(None, None, None, "tensor"), P("tensor", None, None), P(),
        ),
        check_vma=False,
    )
```

time: 1450 us -> 568 us (0.39)
  local copies, waits for them, and re-layouts: 381 us -> 41.2 us
  matrix products: 467 us -> 186 us
  other arithmetic: 243 us -> 34.7 us
  waiting for transfers between devices: 300 us -> 166 us
  Pallas kernels: 0 us -> 105 us
    dot_general x76 -> x38, matrix products: 467 us -> 186 us  [the longest x30 163 us: dot(): return lax.dot_general(a, b, dims, preferred_element_type=F32)]
    reduce_scatter x2 -> x0, waiting for transfers between devices: 119 us -> none  [the longest x1 71.5 us: on_device(): lax.psum_scatter((jnp.dot(mixer_input, output_projection_weight, preferre...]
    pallas_call x0 -> x4, Pallas kernels: none -> 105 us  [the longest x2 68.1 us: mixer_backward(): pl.pallas_call(functools.partial(backward_kernel, count, seq), grid_spec=...]
    reshape x17 -> x2, local copies, waits for them, and re-layouts: 104 us -> 2.15 us  [the longest x1 1.15 us: on_device(): in_up_sum.reshape(adapters, rank, 2, width)]
    squeeze x37 -> x0, local copies, waits for them, and re-layouts: 58.8 us -> none  [the longest x32 48.2 us: state_scan(): lax.scan(jax.checkpoint(advance), (start_state, start_prev), inputs)]
    unnamed x180 -> x140, local copies, waits for them, and re-layouts: 80.4 us -> 29 us
    another operation x38 -> x6, other arithmetic: 49.2 us -> 0.99 us  [the longest x1 0.6 us: on_device(): chans = jnp.stack([jnp.repeat(head_values[2], HEAD), gated_gain])]
    all_gather x2 -> x0, waiting for transfers between devices: 44.6 us -> none  [the longest x1 44.6 us: on_device(): lax.all_gather(normalized_input, 'tensor', axis=0, tiled=True)]
  transfers between devices with their start and end apart: 6 -> 16, of which waited for: 4 -> 3; matrix products, arithmetic and copies ran while one was open for 34% -> 43% of each run, Pallas kernels for 0% -> 19%
where the time goes in v1:
time: 568 us; the launch traced here: 561 us
  matrix products  186 us (33%)
  waiting for transfers between devices  166 us (29%)
  Pallas kernels  105 us (18%)
  local copies, waits for them, and re-layouts  41.2 us (7%)
  other arithmetic  34.7 us (6%)
  between operations  19.3 us (3%)
  starting transfers between devices  8.75 us (2%)
    dot_general x30, matrix products, dot(): return lax.dot_general(a, b, dims, preferred_element_type=F32)  163 us
    psum x1, waiting for transfers between devices, on_device(): lax.psum(in_down_total.astype(BF16), ('dp', 'tensor')).astype(F32)  89.6 us
    psum x1, waiting for transfers between devices, on_device(): in_up_sum = lax.psum(in_up_total.astype(BF16), 'dp').astype(F32)  73.6 us
    pallas_call x2, Pallas kernels, mixer_backward(): pl.pallas_call(functools.partial(backward_kernel, count, seq), grid_spec=...  68.1 us
    pallas_call x2, Pallas kernels, mixer_forward(): pl.pallas_call(functools.partial(forward_kernel, count), grid_spec=pltpu....  36.8 us
    unnamed x140, local copies, waits for them, and re-layouts  29 us
    dot_general x2, matrix products, on_device(): lax.dot_general(lora_back, cots[r], TN, preferred_element_type=F32)  11.6 us
  transfers between devices with their start and end apart: 16, of which 3 were waited for; matrix products, arithmetic and copies ran while one was open for 43% of the time, Pallas kernels for 19%

profile of v1, /device:TPU:0, one launch (start us, length us, event | category | flops | bytes accessed | tf_op | source)
XLA Modules:
  0.0 560.8 jit_solution(5896719371085380826)
XLA Ops:
  23.5 10.3 %copy.47 = bf16[256,8,2,1024]{3,1,2,0:T(8,128)(2,1)} copy(bf16[256,8,2,1024]{3,2,1,0:T(2,128)(2,1)} %bitcast.98) | data formatting | bytes 16777216
  41.4 5.0 fusion.25.bc_ref.dt_ref.bch_ref
  47.8 13.4 %convolution_add_fusion.1.z_ref.x_ref.xh_ref = f32[1024,2048]{1,0:T(8,128)} fusion(f32[1024,2048]{1,0:T(8,128)S(1)} %fusion.97, bf16[2048,2048]{1,0:T(8,128)(2,1)S(1)} %bitcast.106, bf16[512,2048]{1,0:T(8,128)(2,1)} %collective-permute-done, bf16[512,2048]{1,0:T(8,128)(2,1)} %fusion.2), kind=kOutput, calls=%fused_computation.27 | convolution fusion | flops 8600420352 | bytes 29360128 | tf_op jit(solution)/shard_map/dot_general | solution.py:374
  61.1 18.4 %mixer_forward.2 = (f32[1024,1024]{1,0:T(8,128)}, bf16[1024,1024]{1,0:T(8,128)(2,1)}, f32[8,1024]{1,0:T(8,128)}, bf16[8,128,1024]{2,1,0:T(8,128)(2,1)}) custom-call(s32[5]{0:T(128)} %pad_add_fusion.ends, f32[1024,2048]{1,0:T(8,128)} %convolution_add_fusion.1.z_ref.x_ref.xh_ref, f32[1024,2048]{1,0:T(8,128)} %convolution_add_fusion.1.z_ref.x_ref.xh_ref, ...), custom_call_target="tpu_custom_call" | custom-call | flops 1258291200 | bytes 16777216 | tf_op jit(solution)/shard_map/mixer_forward/pallas_call | solution.py:297
  88.2 6.4 %multiply_reduce_fusion.1 = (f32[1024]{0:T(1024)S(1)}, f32[1024,1024]{1,0:T(8,128)}) fusion(bf16[1024,1024]{1,0:T(8,128)(2,1)S(1)} %copy-done.4, f32[1024,1024]{1,0:T(8,128)S(1)} %fusion.108, bf16[1024,2048]{1,0:T(8,128)(2,1)S(1)} %copy-done.16, bf16[1024,2048]{1,0:T(8,128)(2,1)S(1)} %copy-done.58), kind=kOutput, calls=%fused_computation.23 | convolution fusion | flops 4299160576 | bytes 18878464 | tf_op jit(solution)/shard_map/dot_general | solution.py:374
  94.7 4.4 fusion.50
  99.8 5.2 add_convert_fusion.5
  114.4 4.4 fusion.38
  118.8 6.7 %fusion.54 = f32[512,2048]{1,0:T(8,128)} fusion(bf16[1024,2048]{1,0:T(8,128)(2,1)} %param.31, bf16[1024,1024]{1,0:T(8,128)(2,1)S(1)} %copy-done.4), kind=kOutput, calls=%fused_computation.93 | convolution fusion | flops 2147483648 | bytes 9437184 | tf_op jit(solution)/shard_map/dot_general | solution.py:374
  131.4 13.6 %convolution_add_fusion.z_ref.x_ref.xh_ref = f32[1024,2048]{1,0:T(8,128)} fusion(f32[1024,2048]{1,0:T(8,128)S(1)} %fusion.93, bf16[1024,2048]{1,0:T(8,128)(2,1)S(1)} %constant_dynamic-update-slice_fusion.2, bf16[2048,2048]{1,0:T(8,128)(2,1)} %bitcast.99), kind=kOutput, calls=%fused_computation.26 | convolution fusion | flops 8592031744 | bytes 29360128 | tf_op jit(solution)/shard_map/dot_general | solution.py:374
  152.7 18.4 %mixer_forward.3 = (f32[1024,1024]{1,0:T(8,128)}, bf16[1024,1024]{1,0:T(8,128)(2,1)}, f32[8,1024]{1,0:T(8,128)}, bf16[8,128,1024]{2,1,0:T(8,128)(2,1)}) custom-call(s32[5]{0:T(128)} %pad_add_fusion.1.ends, f32[1024,2048]{1,0:T(8,128)} %convolution_add_fusion.z_ref.x_ref.xh_ref, f32[1024,2048]{1,0:T(8,128)} %convolution_add_fusion.z_ref.x_ref.xh_ref, ...), custom_call_target="tpu_custom_call" | custom-call | flops 1258291200 | bytes 16777216 | tf_op jit(solution)/shard_map/mixer_forward/pallas_call | solution.py:297
  171.1 7.1 %fusion.42 = f32[512,2048]{1,0:T(8,128)} fusion(bf16[1024,2048]{1,0:T(8,128)(2,1)} %param.31, bf16[1024,1024]{1,0:T(8,128)(2,1)} %get-tuple-element.23), kind=kOutput, calls=%fused_computation.84 | convolution fusion | flops 2147483648 | bytes 9437184 | tf_op jit(solution)/shard_map/dot_general | solution.py:374
  179.4 6.6 %multiply_reduce_fusion = (f32[1024]{0:T(1024)S(1)}, f32[1024,1024]{1,0:T(8,128)}) fusion(bf16[1024,1024]{1,0:T(8,128)(2,1)S(1)} %copy-done.6, f32[1024,1024]{1,0:T(8,128)S(1)} %copy-done.18, bf16[1024,2048]{1,0:T(8,128)(2,1)S(1)} %copy-done.15, bf16[1024,2048]{1,0:T(8,128)(2,1)S(1)} %copy-done.59), kind=kOutput, calls=%fused_computation.22 | convolution fusion | flops 4299160576 | bytes 18878464 | tf_op jit(solution)/shard_map/dot_general | solution.py:374
  187.4 4.4 fusion.46
  193.7 5.7 %add_convert_fusion.4 = bf16[512,2048]{1,0:T(8,128)(2,1)} fusion(f32[512,2048]{1,0:T(8,128)} %fusion.42, bf16[128,2048]{1,0:T(8,128)(2,1)S(1)} %bitcast.89, bf16[1024,128]{0,1:T(8,128)(2,1)S(1)} %bitcast.94, bf16[1024,1024]{1,0:T(8,128)(2,1)} %get-tuple-element.23, f32[1024,128]{1,0:T(8,128)} %get-tuple-element.62), kind=kOutput, calls=%fused_computation.20 | convolution fusion | flops 404881408 | bytes 8388608 | tf_op jit(solution)/shard_map/dot_general | solution.py:374
  199.5 5.4 fusion.33
  206.3 34.0 %mixer_backward.2 = (bf16[1024,2048]{1,0:T(8,128)(2,1)}, bf16[1024,256]{1,0:T(8,128)(2,1)}, bf16[1024,128]{1,0:T(8,128)(2,1)}) custom-call(s32[5]{0:T(128)} %pad_add_fusion.ends, f32[1024,2048]{1,0:T(8,128)} %convolution_add_fusion.1.z_ref.x_ref.xh_ref, f32[1024,2048]{1,0:T(8,128)} %convolution_add_fusion.1.z_ref.x_ref.xh_ref, ...), custom_call_target="tpu_custom_call" | custom-call | flops 3145728000 | bytes 25165824 | tf_op jit(solution)/shard_map/mixer_backward/pallas_call | solution.py:340
  240.4 4.3 fusion.30
  244.7 9.6 %fusion.18 = f32[512,2048]{1,0:T(8,128)} fusion(bf16[2048,2048]{1,0:T(8,128)(2,1)} %bitcast.100, bf16[1024,2048]{1,0:T(8,128)(2,1)S(1)} %copy-done.19), kind=kOutput, calls=%fused_computation.40 | convolution fusion | flops 4294967296 | bytes 14680064 | tf_op jit(solution)/shard_map/dot_general | solution.py:374
  255.8 34.0 %mixer_backward.3 = (bf16[1024,2048]{1,0:T(8,128)(2,1)}, bf16[1024,256]{1,0:T(8,128)(2,1)}, bf16[1024,128]{1,0:T(8,128)(2,1)}) custom-call(s32[5]{0:T(128)} %pad_add_fusion.1.ends, f32[1024,2048]{1,0:T(8,128)} %convolution_add_fusion.z_ref.x_ref.xh_ref, f32[1024,2048]{1,0:T(8,128)} %convolution_add_fusion.z_ref.x_ref.xh_ref, ...), custom_call_target="tpu_custom_call" | custom-call | flops 3145728000 | bytes 25165824 | tf_op jit(solution)/shard_map/mixer_backward/pallas_call | solution.py:340
  289.8 4.3 fusion.31
  294.1 9.6 %fusion.14 = f32[512,2048]{1,0:T(8,128)} fusion(bf16[2048,2048]{1,0:T(8,128)(2,1)} %bitcast.101, bf16[1024,2048]{1,0:T(8,128)(2,1)S(1)} %copy-done.21), kind=kOutput, calls=%fused_computation.36 | convolution fusion | flops 4294967296 | bytes 14680064 | tf_op jit(solution)/shard_map/dot_general | solution.py:374
  303.8 6.2 %fusion.11 = bf16[128,2048]{1,0:T(8,128)(2,1)} fusion(f32[128,2048]{1,0:T(8,128)} %fusion.33, bf16[1024,2048]{1,0:T(8,128)(2,1)} %copy-done.14, bf16[1024,1024]{1,0:T(8,128)(2,1)} %get-tuple-element.23, bf16[1024,128]{0,1:T(8,128)(2,1)S(1)} %bitcast.96, f32[1024]{0:T(1024)S(1)} %bitcast.123, s32[128]{0:T(128)S(1)} %and_select_fusion, ...), kind=kOutput, calls=%fused_computation.33 | convolution fusion | flops 806354944 | bytes 8135168 | tf_op jit(solution)/shard_map/dot_general | solution.py:567
  311.3 5.7 %add_convert_fusion.2 = bf16[512,2048]{1,0:T(8,128)(2,1)} fusion(f32[512,2048]{1,0:T(8,128)} %fusion.18, bf16[1024,512]{1,0:T(8,128)(2,1)S(1)} %pad_maximum_fusion.5, bf16[2048,16]{1,0:T(8,128)(2,1)S(1)} %copy-done.34, bf16[2048,128]{1,0:T(8,128)(2,1)} %copy.33, bf16[2048,256]{1,0:T(8,128)(2,1)} %param.25), kind=kOutput, calls=%fused_computation.18 | convolution fusion | flops 1086324736 | bytes 8912896 | tf_op jit(solution)/shard_map/dot_general | solution.py:374
  333.0 7.4 %fusion.16 = f32[512,2048]{1,0:T(8,128)S(1)} fusion(bf16[2048,2048]{1,0:T(8,128)(2,1)} %bitcast.102, bf16[1024,2048]{1,0:T(8,128)(2,1)S(1)} %copy-done.22), kind=kOutput, calls=%fused_computation.38 | convolution fusion | flops 4294967296 | bytes 14680064 | tf_op jit(solution)/shard_map/dot_general | solution.py:374
  340.5 3.9 add_convert_fusion
  347.4 5.7 %add_convert_fusion.3 = bf16[512,2048]{1,0:T(8,128)(2,1)} fusion(bf16[512,2048]{1,0:T(8,128)(2,1)} %collective-permute-done.9, f32[512,2048]{1,0:T(8,128)} %fusion.46, bf16[128,2048]{1,0:T(8,128)(2,1)S(1)} %bitcast.88, bf16[1024,128]{0,1:T(8,128)(2,1)S(1)} %bitcast.97, bf16[1024,1024]{1,0:T(8,128)(2,1)S(1)} %copy-done.7, f32[1024,128]{1,0:T(8,128)} %get-tuple-element.62), kind=kOutput, calls=%fused_computation.19 | convolution fusion | flops 406978560 | bytes 10485760 | tf_op jit(solution)/shard_map/dot_general | solution.py:374
  354.8 10.6 %fusion.20 = f32[512,2048]{1,0:T(8,128)} fusion(bf16[2048,2048]{1,0:T(8,128)(2,1)} %bitcast.103, bf16[1024,2048]{1,0:T(8,128)(2,1)} %get-tuple-element.26), kind=kOutput, calls=%fused_computation.42 | convolution fusion | flops 4294967296 | bytes 14680064 | tf_op jit(solution)/shard_map/dot_general | solution.py:374
  368.7 89.6 %all-reduce.8.cloned.1.call-done = (bf16[2048,8,16]{0,2,1:T(8,128)(2,1)}, bf16[8,16,2048]{2,1,0:T(8,128)(2,1)}) async-done(((bf16[2048,8,16]{0,2,1:T(8,128)(2,1)}, bf16[8,16,2048]{2,1,0:T(8,128)(2,1)}), (bf16[2048,8,16]{0,2,1:T(8,128)(2,1)}, bf16[8,16,2048]{2,1,0:T(8,128)(2,1)})) %all-reduce.8.cloned.1.call-update) | async-done | bytes 1048592 | tf_op jit(solution)/shard_map/psum | solution.py:602
  462.6 73.6 %all-reduce.10.cloned.1.call-done = (bf16[8,16,2,1024]{3,2,1,0:T(2,128)(2,1)}, bf16[1024,8,16]{0,2,1:T(8,128)(2,1)}) async-done(((bf16[8,16,2,1024]{3,2,1,0:T(2,128)(2,1)}, bf16[1024,8,16]{0,2,1:T(8,128)(2,1)}), (bf16[8,16,2,1024]{3,2,1,0:T(2,128)(2,1)}, bf16[1024,8,16]{0,2,1:T(8,128)(2,1)})) %all-reduce.10.cloned.1.call-update) | async-done | bytes 786448 | tf_op jit(solution)/shard_map/psum | solution.py:603
  540.4 6.1 %fusion.6 = (f32[512]{0:T(512)S(1)}, f32[512,2048]{1,0:T(8,128)S(1)}) fusion(bf16[512,2048]{1,0:T(8,128)(2,1)S(1)} %copy-done.3, f32[2048]{0:T(1024)S(1)} %copy-done.49, bf16[512,2048]{1,0:T(8,128)(2,1)} %collective-permute-done.13, bf16[512,2048]{1,0:T(8,128)(2,1)} %collective-permute-done.11, f32[512,2048]{1,0:T(8,128)} %fusion.20, f32[512,2048]{1,0:T(8,128)} %fusion.61), kind=kLoop, calls=%fused_computation.13 | loop fusion | flops 9436672 | bytes 18884608 | tf_op jit(solution)/shard_map/reduce_sum | solution.py:598
  547.4 6.0 %fusion.5 = (f32[512,2048]{1,0:T(8,128)}, bf16[512,2048]{1,0:T(8,128)(2,1)}) fusion(bf16[512,2048]{1,0:T(8,128)(2,1)S(1)} %copy-done.3, f32[512,2048]{1,0:T(8,128)S(1)} %get-tuple-element.45, bf16[512,2048]{1,0:T(8,128)(2,1)} %param.19, f32[512]{0:T(512)S(1)} %broadcast_multiply_fusion, f32[512]{0:T(512)S(1)} %copy-done.52, f32[512]{0:T(512)S(1)} %copy-done.51, ...), kind=kLoop, calls=%fused_computation.12 | loop fusion | flops 15728640 | bytes 27271168 | tf_op jit(solution)/shard_map/sub | solution.py:596
  (238 shorter events, 95.3 us)
Async XLA Ops:
  7.2 75.6 %copy-start = (bf16[8,16,2048]{2,1,0:T(8,128)(2,1)S(1)}, bf16[8,16,2048]{2,1,0:T(8,128)(2,1)}, u32[]{:S(2)}) copy-start(bf16[8,16,2048]{2,1,0:T(8,128)(2,1)} %param.35) | copy-start | bytes 1572868
  7.2 14.3 %copy-start.54 = (s32[16,4]{0,1:T(4,128)S(1)}, s32[16,4]{0,1:T(4,128)}, u32[]{:S(2)}) copy-start(s32[16,4]{0,1:T(4,128)} %param.20) | copy-start | bytes 772
  7.2 14.3 %copy-start.53 = (s32[16,4]{0,1:T(4,128)S(1)}, s32[16,4]{0,1:T(4,128)}, u32[]{:S(2)}) copy-start(s32[16,4]{0,1:T(4,128)} %param.21) | copy-start | bytes 772
  7.2 14.9 %copy-start.38 = (bf16[2048,8,16]{0,2,1:T(8,128)(2,1)S(1)}, bf16[2048,8,16]{0,2,1:T(8,128)(2,1)}, u32[]{:S(2)}) copy-start(bf16[2048,8,16]{0,2,1:T(8,128)(2,1)} %param.32) | copy-start | bytes 1572868
  7.2 15.9 %copy-start.48 = (bf16[2048,16]{0,1:T(8,128)(2,1)S(1)}, bf16[2048,16]{0,1:T(8,128)(2,1)}, u32[]{:S(2)}) copy-start(bf16[2048,16]{0,1:T(8,128)(2,1)} %param.26) | copy-start | bytes 196612
  7.2 16.2 %copy-start.39 = (bf16[8,16,2,1024]{3,2,1,0:T(2,128)(2,1)S(1)}, bf16[8,16,2,1024]{3,2,1,0:T(2,128)(2,1)}, u32[]{:S(2)}) copy-start(bf16[8,16,2,1024]{3,2,1,0:T(2,128)(2,1)} %param.33) | copy-start | bytes 1572868
  7.2 451.1 %all-reduce.8.cloned.1.call-start = ((), (), s32[]{:S(2)}) async-start(), calls=%async_computation | async-start | bytes 2097152 | tf_op jit(solution)/shard_map/psum | solution.py:602
  10.1 23.8 %copy-start.50 = (f32[512]{0:T(512)}, f32[512]{0:T(512)S(1)}, u32[]{:S(2)}) copy-start(f32[512]{0:T(512)S(1)} %get-tuple-element.57) | copy-start | bytes 6148
  13.5 27.8 %collective-permute-start = (bf16[512,2048]{1,0:T(8,128)(2,1)}, bf16[512,2048]{1,0:T(8,128)(2,1)}, u32[]{:S(2)}, u32[]{:S(2)}) collective-permute-start(bf16[512,2048]{1,0:T(8,128)(2,1)} %fusion.2), channel_id=1, source_target_pairs={{0,1},{1,0},{2,3},{3,2},{4,5},{5,4},{6,7},{7,6},{8,9},{9,8},{10,11... | collective-permute-start | bytes 6291464 | tf_op jit(solution)/shard_map/ppermute | solution.py:407
  14.0 73.1 %collective-permute-start.2 = (bf16[512,2048]{1,0:T(8,128)(2,1)}, bf16[512,2048]{1,0:T(8,128)(2,1)}, u32[]{:S(2)}, u32[]{:S(2)}) collective-permute-start(bf16[512,2048]{1,0:T(8,128)(2,1)} %fusion.2), channel_id=1, source_target_pairs={{0,2},{1,3},{2,0},{3,1},{4,6},{5,7},{6,4},{7,5},{8,10},{9,11},{10,... | collective-permute-start | bytes 6291464 | tf_op jit(solution)/shard_map/ppermute | solution.py:404
  16.5 63.0 %collective-permute-start.1 = (bf16[512,2048]{1,0:T(8,128)(2,1)}, bf16[512,2048]{1,0:T(8,128)(2,1)}, u32[]{:S(2)}, u32[]{:S(2)}) collective-permute-start(bf16[512,2048]{1,0:T(8,128)(2,1)} %param.19), channel_id=1, source_target_pairs={{0,1},{1,0},{2,3},{3,2},{4,5},{5,4},{6,7},{7,6},{8,9},{9,8},{10,11... | collective-permute-start | bytes 6291464 | tf_op jit(solution)/shard_map/ppermute | solution.py:407
  16.7 91.3 %collective-permute-start.4 = (bf16[512,2048]{1,0:T(8,128)(2,1)}, bf16[512,2048]{1,0:T(8,128)(2,1)}, u32[]{:S(2)}, u32[]{:S(2)}) collective-permute-start(bf16[512,2048]{1,0:T(8,128)(2,1)} %param.19), channel_id=1, source_target_pairs={{0,2},{1,3},{2,0},{3,1},{4,6},{5,7},{6,4},{7,5},{8,10},{9,11},{10,... | collective-permute-start | bytes 6291464 | tf_op jit(solution)/shard_map/ppermute | solution.py:404
  23.4 18.0 %copy-start.32 = (bf16[2048,16]{1,0:T(8,128)(2,1)}, bf16[2048,16]{1,0:T(8,128)(2,1)S(1)}, u32[]{:S(2)}) copy-start(bf16[2048,16]{1,0:T(8,128)(2,1)S(1)} %copy.46) | copy-start | bytes 196612
  23.5 12.3 %copy-start.55 = (f32[1024]{0:T(1024)S(1)}, f32[1024]{0:T(1024)}, u32[]{:S(2)}) copy-start(f32[1024]{0:T(1024)} %param.30) | copy-start | bytes 12292
  87.1 38.4 %collective-permute-start.3 = (bf16[512,2048]{1,0:T(8,128)(2,1)}, bf16[512,2048]{1,0:T(8,128)(2,1)}, u32[]{:S(2)}, u32[]{:S(2)}) collective-permute-start(bf16[512,2048]{1,0:T(8,128)(2,1)} %collective-permute-done.2), channel_id=1, source_target_pairs={{0,1},{1,0},{2,3},{3,2},{4,5},{5,4},{6,7},{7,6},{8,9},{9,8},{10,11... | collective-permute-start | bytes 6291464 | tf_op jit(solution)/shard_map/ppermute | solution.py:407
  105.0 441.5 %collective-permute-start.8 = (bf16[512,2048]{1,0:T(8,128)(2,1)}, bf16[512,2048]{1,0:T(8,128)(2,1)}, u32[]{:S(2)}, u32[]{:S(2)}) collective-permute-start(bf16[512,2048]{1,0:T(8,128)(2,1)} %add_convert_fusion.5), channel_id=1, source_target_pairs={{0,1},{1,0},{2,3},{3,2},{4,5},{5,4},{6,7},{7,6},{8,9},{9,8},{10,11... | collective-permute-start | bytes 6291464 | tf_op jit(solution)/shard_map/ppermute | solution.py:407
  108.1 36.9 %collective-permute-start.5 = (bf16[512,2048]{1,0:T(8,128)(2,1)}, bf16[512,2048]{1,0:T(8,128)(2,1)}, u32[]{:S(2)}, u32[]{:S(2)}) collective-permute-start(bf16[512,2048]{1,0:T(8,128)(2,1)} %collective-permute-done.4), channel_id=1, source_target_pairs={{0,1},{1,0},{2,3},{3,2},{4,5},{5,4},{6,7},{7,6},{8,9},{9,8},{10,11... | collective-permute-start | bytes 6291464 | tf_op jit(solution)/shard_map/ppermute | solution.py:407
  131.4 13.6 %copy-start.13 = (bf16[1024,2048]{1,0:T(8,128)(2,1)S(1)}, bf16[1024,2048]{1,0:T(8,128)(2,1)}, u32[]{:S(2)}) copy-start(bf16[1024,2048]{1,0:T(8,128)(2,1)} %constant_dynamic-update-slice_fusion.5) | copy-start | bytes 12582916
  149.9 21.2 %copy-start.25 = (bf16[1024,128]{1,0:T(8,128)(2,1)}, bf16[1024,128]{1,0:T(8,128)(2,1)S(1)}, u32[]{:S(2)}) copy-start(bf16[1024,128]{1,0:T(8,128)(2,1)S(1)} %fusion.29) | copy-start | bytes 786436
  186.9 5.0 collective-permute-start.6
  191.9 7.5 %collective-permute-start.7 = (f32[2,2,1024]{2,1,0:T(2,128)S(1)}, f32[2,2,1024]{2,1,0:T(2,128)S(1)}, u32[]{:S(2)}, u32[]{:S(2)}) collective-permute-start(f32[2,2,1024]{2,1,0:T(2,128)S(1)} %maximum_add_fusion), channel_id=1, source_target_pairs={{0,2},{1,3},{2,0},{3,1},{4,6},{5,7},{6,4},{7,5},{8,10},{9,11},{10,... | collective-permute-start | bytes 49160 | tf_op jit(solution)/shard_map/ppermute | solution.py:404
  199.4 148.0 %collective-permute-start.9 = (bf16[512,2048]{1,0:T(8,128)(2,1)}, bf16[512,2048]{1,0:T(8,128)(2,1)}, u32[]{:S(2)}, u32[]{:S(2)}) collective-permute-start(bf16[512,2048]{1,0:T(8,128)(2,1)} %add_convert_fusion.4), channel_id=1, source_target_pairs={{0,1},{1,0},{2,3},{3,2},{4,5},{5,4},{6,7},{7,6},{8,9},{9,8},{10,11... | collective-permute-start | bytes 6291464 | tf_op jit(solution)/shard_map/ppermute | solution.py:407
  317.0 223.3 %collective-permute-start.11 = (bf16[512,2048]{1,0:T(8,128)(2,1)}, bf16[512,2048]{1,0:T(8,128)(2,1)}, u32[]{:S(2)}, u32[]{:S(2)}) collective-permute-start(bf16[512,2048]{1,0:T(8,128)(2,1)} %add_convert_fusion.2), channel_id=1, source_target_pairs={{0,1},{1,0},{2,3},{3,2},{4,5},{5,4},{6,7},{7,6},{8,9},{9,8},{10,11... | collective-permute-start | bytes 6291464 | tf_op jit(solution)/shard_map/ppermute | solution.py:407
  326.5 13.9 %collective-permute-start.12 = (bf16[512,2048]{1,0:T(8,128)(2,1)}, bf16[512,2048]{1,0:T(8,128)(2,1)}, u32[]{:S(2)}, u32[]{:S(2)}) collective-permute-start(bf16[512,2048]{1,0:T(8,128)(2,1)} %add_convert_fusion.1), channel_id=1, source_target_pairs={{0,1},{1,0},{2,3},{3,2},{4,5},{5,4},{6,7},{7,6},{8,9},{9,8},{10,11... | collective-permute-start | bytes 6291464 | tf_op jit(solution)/shard_map/ppermute | solution.py:407
  326.7 209.5 %all-reduce.10.cloned.1.call-start = ((), (), s32[]{:S(2)}) async-start(), calls=%async_computation.1 | async-start | bytes 1572864 | tf_op jit(solution)/shard_map/psum | solution.py:603
  344.4 196.0 %collective-permute-start.13 = (bf16[512,2048]{1,0:T(8,128)(2,1)}, bf16[512,2048]{1,0:T(8,128)(2,1)}, u32[]{:S(2)}, u32[]{:S(2)}) collective-permute-start(bf16[512,2048]{1,0:T(8,128)(2,1)} %add_convert_fusion), channel_id=1, source_target_pairs={{0,2},{1,3},{2,0},{3,1},{4,6},{5,7},{6,4},{7,5},{8,10},{9,11},{10,... | collective-permute-start | bytes 6291464 | tf_op jit(solution)/shard_map/ppermute | solution.py:404
  353.2 12.3 %copy-start.37 = (bf16[2048,16]{1,0:T(8,128)(2,1)S(1)}, bf16[2048,16]{1,0:T(8,128)(2,1)}, u32[]{:S(2)}) copy-start(bf16[2048,16]{1,0:T(8,128)(2,1)} %copy-done.32) | copy-start | bytes 196612
  353.2 12.3 %copy-start.44 = (bf16[2048,128]{1,0:T(8,128)(2,1)S(1)}, bf16[2048,128]{1,0:T(8,128)(2,1)}, u32[]{:S(2)}) copy-start(bf16[2048,128]{1,0:T(8,128)(2,1)} %copy.33) | copy-start | bytes 1572868
  353.2 12.3 %copy-start.63 = (bf16[2048,256]{1,0:T(8,128)(2,1)S(1)}, bf16[2048,256]{1,0:T(8,128)(2,1)}, u32[]{:S(2)}) copy-start(bf16[2048,256]{1,0:T(8,128)(2,1)} %param.25) | copy-start | bytes 3145732
  353.2 193.3 %collective-permute-start.10 = (bf16[512,2048]{1,0:T(8,128)(2,1)}, bf16[512,2048]{1,0:T(8,128)(2,1)}, u32[]{:S(2)}, u32[]{:S(2)}) collective-permute-start(bf16[512,2048]{1,0:T(8,128)(2,1)} %add_convert_fusion.3), channel_id=1, source_target_pairs={{0,2},{1,3},{2,0},{3,1},{4,6},{5,7},{6,4},{7,5},{8,10},{9,11},{10,... | collective-permute-start | bytes 6291464 | tf_op jit(solution)/shard_map/ppermute | solution.py:404
  368.7 171.6 %copy-start.3 = (bf16[512,2048]{1,0:T(8,128)(2,1)S(1)}, bf16[512,2048]{1,0:T(8,128)(2,1)}, u32[]{:S(2)}) copy-start(bf16[512,2048]{1,0:T(8,128)(2,1)} %param.18) | copy-start | bytes 6291460
  368.7 171.6 %copy-start.49 = (f32[2048]{0:T(1024)S(1)}, f32[2048]{0:T(1024)}, u32[]{:S(2)}) copy-start(f32[2048]{0:T(1024)} %param.23) | copy-start | bytes 24580
  (51 other events, 264.1 us)
Sparse Core Ops, SparseCore 0:
  326.8 131.4 all-reduce.7
  461.9 74.2 all-reduce.9

commit v2 on v1

--- a/solution.py
+++ b/solution.py
@@ -406,10 +406,14 @@
     def near(self, v):
         return lax.ppermute(v, "tensor", self.beside)
 
-    def gather(self, v):
-        own = jnp.concatenate([v, self.near(v)], axis=0)
-        came = self.far(v)
-        return own, jnp.concatenate([came, self.near(came)], axis=0)
+    def gather_own(self, v):
+        return jnp.concatenate([v, self.near(v)], axis=0)
+
+    def send_other(self, v):
+        return self.far(v)
+
+    def gather_other(self, came):
+        return jnp.concatenate([came, self.near(came)], axis=0)
 
     def sum_stats(self, own, other):
         both = jnp.stack([own, other])
@@ -417,16 +421,17 @@
         came = self.far(both)
         return both[0] + came[1], both[1] + came[0]
 
-    def reduce_other(self, project):
+    def reduce_near(self, whole):
         half = ROW_LEN // 2
-        second = self.near(project(half, ROW_LEN).astype(BF16))
-        first = project(0, half)
-        return self.far((first + second.astype(F32)).astype(BF16))
-
-    def reduce_own(self, project, came):
-        half = ROW_LEN // 2
-        second = self.near(project(half, ROW_LEN).astype(BF16))
-        return project(0, half) + second.astype(F32) + came.astype(F32)
+        second = self.near(whole[half:])
+        return whole[:half].astype(F32) + second.astype(F32)
+
+    def reduce_other(self, whole):
+        sent = self.reduce_near(whole).astype(BF16)
+        return sent, self.far(sent)
+
+    def reduce_own(self, whole, came):
+        return self.reduce_near(whole) + came.astype(F32)
 
     def mine(self, own_stat):
         return own_stat[: ROW_LEN // 2]
@@ -441,12 +446,18 @@
         self.own_row, self.core = me // per_row, me % per_row
         self.per_row = per_row
 
-    def gather(self, v):
+    def gather_row(self, v, row):
         whole = lax.all_gather(v, "tensor", axis=0, tiled=True).reshape(2, ROW_LEN, v.shape[1])
-        return (
-            lax.dynamic_index_in_dim(whole, self.own_row, 0, False),
-            lax.dynamic_index_in_dim(whole, 1 - self.own_row, 0, False),
-        )
+        return lax.dynamic_index_in_dim(whole, row, 0, False)
+
+    def gather_own(self, v):
+        return self.gather_row(v, self.own_row)
+
+    def send_other(self, v):
+        return v
+
+    def gather_other(self, v):
+        return self.gather_row(v, 1 - self.own_row)
 
     def sum_stats(self, own, other):
         first = jnp.where(self.own_row == 0, own, other)
@@ -457,11 +468,10 @@
             lax.dynamic_index_in_dim(total, 1 - self.own_row, 0, False),
         )
 
-    def reduce_other(self, project):
-        return project(0, ROW_LEN).astype(BF16)
-
-    def reduce_own(self, project, other):
-        own = project(0, ROW_LEN).astype(BF16)
+    def reduce_other(self, whole):
+        return whole, whole
+
+    def reduce_own(self, own, other):
         first = jnp.where(self.own_row == 0, own, other)
         second = jnp.where(self.own_row == 0, other, own)
         whole = jnp.concatenate([first, second], axis=0)
@@ -470,6 +480,86 @@
     def mine(self, own_stat):
         size = ROW_LEN // self.per_row
         return lax.dynamic_slice_in_dim(own_stat, self.core * size, size, 0)
+
+
+def after(v, *done):
+    return lax.optimization_barrier((v,) + done)[0]
+
+
+def exchange_steps(axis):
+    size = lax.axis_size(axis)
+    assert size & (size - 1) == 0
+    steps, mask = [], 1
+    while mask < size:
+        bit = (lax.axis_index(axis) // mask) % 2
+        steps.append((axis, bit, [(i, i ^ mask) for i in range(size)]))
+        mask *= 2
+    return steps
+
+
+def half_of(v, which):
+    size = v.shape[0] // 2
+    return lax.dynamic_slice_in_dim(v, which * size, size, 0)
+
+
+def scatter_sum(arrays, step):
+    axis, bit, pairs = step
+    sent = jnp.concatenate([half_of(v, 1 - bit) for v in arrays], axis=0).astype(BF16)
+    came = lax.ppermute(sent, axis, pairs).astype(F32)
+    sums, first = [], 0
+    for v in arrays:
+        size = v.shape[0] // 2
+        sums.append(half_of(v, bit) + came[first : first + size])
+        first += size
+    return sums
+
+
+def gather_halves(arrays, step):
+    axis, bit, pairs = step
+    came = lax.ppermute(jnp.concatenate(arrays, axis=0), axis, pairs)
+    wholes, first = [], 0
+    for v in arrays:
+        other = came[first : first + v.shape[0]]
+        first += v.shape[0]
+        wholes.append(
+            jnp.concatenate([jnp.where(bit == 0, v, other), jnp.where(bit == 0, other, v)], axis=0)
+        )
+    return wholes
+
+
+class FactorSum:
+    def __init__(self, shared, split):
+        self.near, self.far = exchange_steps("tensor"), exchange_steps("dp")
+        self.arrays, self.split, self.done = [shared], split, 0
+
+    def hop(self):
+        near, far = len(self.near), len(self.far)
+        at, total = self.done, 2 * (near + far)
+        if at == total:
+            return
+        if at == near:
+            self.arrays = self.arrays + [self.split]
+        if at == near + far:
+            self.arrays = [v.astype(BF16) for v in self.arrays]
+        steps = self.near + self.far
+        if at < near + far:
+            self.arrays = scatter_sum(self.arrays, steps[at])
+        else:
+            self.arrays = gather_halves(self.arrays, steps[total - 1 - at])
+        self.done += 1
+        if self.done == near + 2 * far:
+            self.split = self.arrays[1]
+            self.arrays = self.arrays[:1]
+
+    def cover(self, v):
+        v, *self.arrays = lax.optimization_barrier((v, *self.arrays))
+        self.hop()
+        return v
+
+    def finish(self):
+        while self.done < 2 * (len(self.near) + len(self.far)):
+            self.hop()
+        return self.arrays[0].astype(F32), self.split.astype(F32)
 
 
 def on_device(
@@ -510,37 +600,61 @@
 
     residual = tokens.astype(F32)
     inv_rms = lax.rsqrt(jnp.mean(residual * residual, axis=1, keepdims=True) + EPS)
-    normed = links.gather((residual * inv_rms * norm_gain).astype(BF16))
-    cots = links.gather(cotangent)
-
-    def forward(row):
+    normed_here = (residual * inv_rms * norm_gain).astype(BF16)
+    normed = [links.gather_own(normed_here), links.gather_other(links.send_other(normed_here))]
+    cots = [links.gather_own(cotangent), None]
+
+    def forward(row, nb):
         ends, select = row_data[row]
-        nb = normed[row]
         small = dot(nb, small_weight)
         lora = (small[:, 384:] * select).astype(BF16)
         zx = dot(nb, zx_weight) + dot(lora, in_up)
         y, gained, squares, states = mixer_forward(ends, zx, small, conv_taps, state_taps, heads, chans)
         return small, lora, zx, y, gained, squares, states
 
-    def cotangents(row):
-        low = (dot(cots[row], out_up, NT) * row_data[row][1]).astype(BF16)
-        return low, dot(cots[row], out_weight, NT) + dot(low, out_down, NT)
+    def cotangents(row, cot, gained):
+        low = (dot(cot, out_up, NT) * row_data[row][1]).astype(BF16)
+        grad = dot(cot, out_weight, NT) + dot(low, out_down, NT)
+        return low, grad, jnp.sum(grad * gained.astype(F32), axis=1)
 
     def project_out(row, gained):
-        def part(first, last):
-            piece = gained[first:last]
-            low = (dot(piece, out_down) * row_data[row][1][first:last]).astype(BF16)
-            return dot(piece, out_weight) + dot(low, out_up)
-
-        return part
-
-    fw = [forward(0), forward(1)]
-    back = [cotangents(0), cotangents(1)]
-    crosses = [jnp.sum(back[r][1] * fw[r][4].astype(F32), axis=1) for r in range(2)]
-    stats = [jnp.stack([fw[r][5][0], crosses[r]]) for r in range(2)]
+        low = (dot(gained, out_down) * row_data[row][1]).astype(BF16)
+        return (dot(gained, out_weight) + dot(low, out_up)).astype(BF16)
+
+    def out_gradients(row, low, gained, scale):
+        select = row_data[row][1]
+        scaled_low = (low.astype(F32) * scale[:, None]).astype(BF16)
+        lora_back = (dot(gained, out_down) * select * scale[:, None]).astype(BF16)
+        return (
+            lax.dot_general(gained, scaled_low, TN, preferred_element_type=F32),
+            lax.dot_general(lora_back, cots[row], TN, preferred_element_type=F32),
+        )
+
+    def backward(row, gm):
+        ends, select = row_data[row]
+        small, lora, zx, y, gained, _, states = fw[row]
+        return mixer_backward(
+            ends, zx, small, gm, y, states, rks[row], conv_taps, state_taps, heads, chans
+        )
+
+    def in_gradients(row, dzx, mid):
+        return (
+            lax.dot_general(dzx, fw[row][1], TN, preferred_element_type=F32),
+            lax.dot_general(normed[row], mid, TN, preferred_element_type=F32),
+        )
+
+    def project_in(row, dzx, dsmall):
+        return (dot(dzx, zx_weight, NT) + dot(dsmall, small_weight, NT)).astype(BF16)
+
+    fw = [forward(0, normed[0]), None]
+    came_cot = links.send_other(after(cotangent, fw[0][4]))
+    back = [cotangents(0, after(cots[0], fw[0][4]), fw[0][4]), None]
+    fw[1] = forward(1, after(normed[1], back[0][1]))
+    cots[1] = links.gather_other(after(came_cot, fw[1][4]))
+    back[1] = cotangents(1, cots[1], fw[1][4])
+    stats = [jnp.stack([fw[r][5][0], back[r][2]]) for r in range(2)]
     stats = links.sum_stats(stats[0], stats[1])
-    came = links.reduce_other(project_out(1, fw[1][4]))
-    out_sum = links.reduce_own(project_out(0, fw[0][4]), came)
+    sent_out, came_out = links.reduce_other(project_out(1, after(fw[1][4], back[1][2])))
     inv, rks = [], []
     for r in range(2):
         scale = lax.rsqrt(stats[r][0] / inner + EPS)
@@ -552,55 +666,41 @@
                 axis=1,
             )
         )
+    grads_1 = out_gradients(1, back[1][0], fw[1][4], inv[1])
+    grads_0 = out_gradients(0, back[0][0], fw[0][4], inv[0])
+    down_total, up_total = [a + b for a, b in zip(grads_0, grads_1)]
+    out_chain = FactorSum(up_total.T, down_total)
+
+    gm_1 = after(out_chain.cover(back[1][1]), sent_out, down_total)
+    dzx_1, dbc_1, ddt_1 = backward(1, gm_1)
+    dzx_1 = out_chain.cover(after(dzx_1, came_out))
+    mid_1 = (dot(dzx_1, in_up, NT) * row_data[1][1]).astype(BF16)
+    sent_in, came_in = links.reduce_other(project_in(1, dzx_1, jnp.concatenate([dbc_1, ddt_1, mid_1], axis=1)))
+    in_1 = in_gradients(1, out_chain.cover(after(dzx_1, sent_in)), mid_1)
+    gm_0 = out_chain.cover(after(back[0][1], sent_in, *in_1))
+    dzx_0, dbc_0, ddt_0 = backward(0, gm_0)
+    dzx_0 = out_chain.cover(after(dzx_0, came_in))
+    mid_0 = (dot(dzx_0, in_up, NT) * row_data[0][1]).astype(BF16)
+    in_0 = in_gradients(0, dzx_0, out_chain.cover(mid_0))
+    in_up_total, in_down_total = [a + b for a, b in zip(in_1, in_0)]
+    in_chain = FactorSum(in_down_total, in_up_total)
+
+    dzx_0 = after(in_chain.cover(dzx_0), in_up_total)
+    whole_in = project_in(0, dzx_0, jnp.concatenate([dbc_0, ddt_0, mid_0], axis=1))
+    gained_0 = after(in_chain.cover(fw[0][4]), whole_in)
+    whole_out = project_out(0, gained_0)
+    out_sum = links.reduce_own(in_chain.cover(whole_out), came_out)
     output = (residual + links.mine(inv[0])[:, None] * out_sum).astype(BF16)
-
-    grads = [None, None]
-    out_grads = [None, None]
-    for r in (1, 0):
-        low, gm = back[r]
-        gained = fw[r][4]
-        select = row_data[r][1]
-        scaled_low = (low.astype(F32) * inv[r][:, None]).astype(BF16)
-        lora_back = (dot(gained, out_down) * select * inv[r][:, None]).astype(BF16)
-        out_grads[r] = (
-            lax.dot_general(gained, scaled_low, TN, preferred_element_type=F32),
-            lax.dot_general(lora_back, cots[r], TN, preferred_element_type=F32),
-        )
-    down_total, up_total = [a + b for a, b in zip(*out_grads)]
-
-    in_grads = [None, None]
-    for r in (1, 0):
-        ends, select = row_data[r]
-        small, lora, zx, y, gained, _, states = fw[r]
-        dzx, dbc, ddt = mixer_backward(
-            ends, zx, small, back[r][1], y, states, rks[r], conv_taps, state_taps, heads, chans
-        )
-        mid = (dot(dzx, in_up, NT) * select).astype(BF16)
-        in_grads[r] = (
-            lax.dot_general(lora, dzx, TN, preferred_element_type=F32),
-            lax.dot_general(normed[r], mid, TN, preferred_element_type=F32),
-        )
-        dsmall = jnp.concatenate([dbc, ddt, mid], axis=1)
-
-        def part(first, last, dzx=dzx, dsmall=dsmall):
-            return dot(dzx[first:last], zx_weight, NT) + dot(dsmall[first:last], small_weight, NT)
-
-        grads[r] = part
-        if r == 1:
-            came = links.reduce_other(part)
-    grad_normed = links.reduce_own(grads[0], came)
-    in_up_total, in_down_total = [a + b for a, b in zip(*in_grads)]
-
+    grad_normed = links.reduce_own(in_chain.cover(after(whole_in, output)), came_in)
     scaled = grad_normed * norm_gain
     grad_tokens = (
         cotangent.astype(F32)
         + inv_rms * scaled
         - residual * inv_rms**3 * (jnp.sum(scaled * residual, axis=1, keepdims=True) / model)
     )
-    out_up_sum = lax.psum(up_total.astype(BF16), ("dp", "tensor")).astype(F32)
-    out_down_sum = lax.psum(down_total.astype(BF16), "dp").astype(F32)
-    in_down_sum = lax.psum(in_down_total.astype(BF16), ("dp", "tensor")).astype(F32)
-    in_up_sum = lax.psum(in_up_total.astype(BF16), "dp").astype(F32)
+    out_up_sum, out_down_sum = out_chain.finish()
+    in_down_sum, in_up_sum = in_chain.finish()
+    out_up_sum, in_up_sum = out_up_sum.T, in_up_sum.T
     return (
         output,
         grad_tokens,

time: 568 us -> 451 us (0.79)
  waiting for transfers between devices: 166 us -> 42.9 us
  matrix products: 186 us -> 148 us
  local copies, waits for them, and re-layouts: 41.2 us -> 61.6 us
  starting transfers between devices: 8.75 us -> 28 us
  other arithmetic: 34.7 us -> 51.4 us
  between operations: 19.3 us -> 6.3 us
    psum x2 -> x0, waiting for transfers between devices: 163 us -> none  [the longest x1 89.6 us: on_device(): lax.psum(in_down_total.astype(BF16), ('dp', 'tensor')).astype(F32)]
    dot_general x30 -> x22, matrix products: 163 us -> 116 us  [dot(): return lax.dot_general(a, b, dims, preferred_element_type=F32)]
    ppermute x0 -> x20, waiting for transfers between devices: none -> 34.8 us  [the longest x10 19.2 us: scatter_sum(): came = lax.ppermute(sent, axis, pairs).astype(F32)]
    ppermute x0 -> x20, starting transfers between devices: none -> 19.4 us  [the longest x10 13.1 us: scatter_sum(): came = lax.ppermute(sent, axis, pairs).astype(F32)]
    convert_element_type x2 -> x14, other arithmetic: 4.78 us -> 20.4 us  [the longest x2 8.44 us: reduce_other(): sent = self.reduce_near(whole).astype(BF16)]
    slice x2 -> x6, local copies, waits for them, and re-layouts: 1.52 us -> 12.8 us  [the longest x4 11.3 us: reduce_near(): second = self.near(whole[half:])]
    dot_general x8, matrix products: 22.5 us -> 31.9 us  [the longest x2 12.3 us: out_gradients(): lax.dot_general(lora_back, cots[row], TN, preferred_element_type=F32)]
    select_n x0 -> x16, other arithmetic: none -> 5.98 us  [gather_halves(): jnp.where(bit == 0, v, other)]
  transfers between devices with their start and end apart: 16 -> 34, of which waited for: 3 -> 14; matrix products, arithmetic and copies ran while one was open for 43% -> 41% of each run, Pallas kernels for 19% -> 24%
where the time goes in v2:
time: 451 us; the launch traced here: 444 us
  matrix products  148 us (33%)
  Pallas kernels  105 us (23%)
  local copies, waits for them, and re-layouts  61.6 us (14%)
  other arithmetic  51.4 us (11%)
  waiting for transfers between devices  42.9 us (10%)
  starting transfers between devices  28 us (6%)
  between operations  6.3 us (1%)
    dot_general x22, matrix products, dot(): return lax.dot_general(a, b, dims, preferred_element_type=F32)  116 us
    pallas_call x2, Pallas kernels, mixer_backward(): pl.pallas_call(functools.partial(backward_kernel, count, seq), grid_spec=...  68.6 us
    pallas_call x2, Pallas kernels, mixer_forward(): pl.pallas_call(functools.partial(forward_kernel, count), grid_spec=pltpu....  36.8 us
    unnamed x142, local copies, waits for them, and re-layouts  29.5 us
    ppermute x10, waiting for transfers between devices, scatter_sum(): came = lax.ppermute(sent, axis, pairs).astype(F32)  19.2 us
    ppermute x10, waiting for transfers between devices, gather_halves(): came = lax.ppermute(jnp.concatenate(arrays, axis=0), axis, pairs)  15.6 us
    ppermute x10, starting transfers between devices, scatter_sum(): came = lax.ppermute(sent, axis, pairs).astype(F32)  13.1 us
    dot_general x2, matrix products, out_gradients(): lax.dot_general(lora_back, cots[row], TN, preferred_element_type=F32)  12.3 us
  transfers between devices with their start and end apart: 34, of which 14 were waited for; matrix products, arithmetic and copies ran while one was open for 41% of the time, Pallas kernels for 24%

profile of v2, /device:TPU:0, one launch (start us, length us, event | category | flops | bytes accessed | tf_op | source)
XLA Modules:
  0.0 443.8 jit_solution(13025572433726897313)
XLA Ops:
  19.3 10.3 %copy.73 = bf16[256,8,2,1024]{3,1,2,0:T(8,128)(2,1)} copy(bf16[256,8,2,1024]{3,2,1,0:T(2,128)(2,1)} %bitcast.92) | data formatting | bytes 16777216
  33.9 5.5 %fusion.13.bc_ref.dt_ref.bch_ref = f32[1024,512]{1,0:T(8,128)S(1)} fusion(bf16[512,2048]{1,0:T(8,128)(2,1)} %collective-permute-done, bf16[512,2048]{1,0:T(8,128)(2,1)} %fusion.2, bf16[2048,16]{1,0:T(8,128)(2,1)} %copy.72, bf16[2048,128]{1,0:T(8,128)(2,1)} %copy.53, bf16[2048,256]{1,0:T(8,128)(2,1)S(1)} %copy-done.54), kind=kOutput, calls=%fused_computation.46 | convolution fusion | flops 2166358016 | bytes 7929856 | tf_op jit(solution)/shard_map/dot_general | solution.py:374
  40.8 13.4 %convolution_add_fusion.1.z_ref.x_ref.xh_ref = f32[1024,2048]{1,0:T(8,128)} fusion(f32[1024,2048]{1,0:T(8,128)S(1)} %fusion.85, bf16[2048,2048]{1,0:T(8,128)(2,1)S(1)} %bitcast.96, bf16[512,2048]{1,0:T(8,128)(2,1)} %collective-permute-done, bf16[512,2048]{1,0:T(8,128)(2,1)} %fusion.2), kind=kOutput, calls=%fused_computation.27 | convolution fusion | flops 8600420352 | bytes 29360128 | tf_op jit(solution)/shard_map/dot_general | solution.py:374
  54.2 18.4 %mixer_forward.2 = (f32[1024,1024]{1,0:T(8,128)}, bf16[1024,1024]{1,0:T(8,128)(2,1)}, f32[8,1024]{1,0:T(8,128)}, bf16[8,128,1024]{2,1,0:T(8,128)(2,1)}) custom-call(s32[5]{0:T(128)} %pad_add_fusion.ends, f32[1024,2048]{1,0:T(8,128)} %convolution_add_fusion.1.z_ref.x_ref.xh_ref, f32[1024,2048]{1,0:T(8,128)} %convolution_add_fusion.1.z_ref.x_ref.xh_ref, ...), custom_call_target="tpu_custom_call" | custom-call | flops 1258291200 | bytes 16777216 | tf_op jit(solution)/shard_map/mixer_forward/pallas_call | solution.py:297
  80.4 8.5 %multiply_reduce_fusion.1 = (f32[1024]{0:T(1024)S(1)}, f32[1024,1024]{1,0:T(8,128)}) fusion(bf16[1024,1024]{1,0:T(8,128)(2,1)S(1)} %copy-done.4, f32[1024,1024]{1,0:T(8,128)S(1)} %fusion.94, bf16[1024,2048]{1,0:T(8,128)(2,1)S(1)} %constant_dynamic-update-slice_fusion, bf16[1024,2048]{1,0:T(8,128)(2,1)} %param.31), kind=kOutput, calls=%fused_computation.23 | convolution fusion | flops 4299160576 | bytes 18878464 | tf_op jit(solution)/shard_map/dot_general | solution.py:374
  95.0 11.0 %convolution_add_fusion.z_ref.x_ref.xh_ref = f32[1024,2048]{1,0:T(8,128)} fusion(f32[1024,2048]{1,0:T(8,128)S(1)} %fusion.82, bf16[1024,2048]{1,0:T(8,128)(2,1)S(1)} %constant_dynamic-update-slice_fusion.2, bf16[2048,2048]{1,0:T(8,128)(2,1)S(1)} %bitcast.99), kind=kOutput, calls=%fused_computation.26 | convolution fusion | flops 8592031744 | bytes 29360128 | tf_op jit(solution)/shard_map/dot_general | solution.py:374
  105.9 18.4 %mixer_forward.3 = (f32[1024,1024]{1,0:T(8,128)}, bf16[1024,1024]{1,0:T(8,128)(2,1)}, f32[8,1024]{1,0:T(8,128)}, bf16[8,128,1024]{2,1,0:T(8,128)(2,1)}) custom-call(s32[5]{0:T(128)} %pad_add_fusion.1.ends, f32[1024,2048]{1,0:T(8,128)} %convolution_add_fusion.z_ref.x_ref.xh_ref, f32[1024,2048]{1,0:T(8,128)} %convolution_add_fusion.z_ref.x_ref.xh_ref, ...), custom_call_target="tpu_custom_call" | custom-call | flops 1258291200 | bytes 16777216 | tf_op jit(solution)/shard_map/mixer_forward/pallas_call | solution.py:297
  133.3 6.5 %multiply_reduce_fusion = (f32[1024]{0:T(1024)S(1)}, f32[1024,1024]{1,0:T(8,128)}) fusion(bf16[1024,1024]{1,0:T(8,128)(2,1)S(1)} %copy-done.7, f32[1024,1024]{1,0:T(8,128)S(1)} %fusion.95, bf16[1024,2048]{1,0:T(8,128)(2,1)S(1)} %constant_dynamic-update-slice_fusion.4, bf16[1024,2048]{1,0:T(8,128)(2,1)S(1)} %copy-done.52), kind=kOutput, calls=%fused_computation.22 | convolution fusion | flops 4299160576 | bytes 18878464 | tf_op jit(solution)/shard_map/dot_general | solution.py:374
  139.8 6.6 %fusion.96 = f32[1024,2048]{1,0:T(8,128)} fusion(bf16[1024,1024]{1,0:T(8,128)(2,1)S(1)} %copy-done.7, bf16[1024,2048]{1,0:T(8,128)(2,1)S(1)} %copy-done.52), kind=kOutput, calls=%fused_computation.264 | convolution fusion | flops 4294967296 | bytes 14680064 | tf_op jit(solution)/shard_map/dot_general | solution.py:374
  146.4 6.6 %add_convert_fusion.3 = bf16[1024,2048]{1,0:T(8,128)(2,1)} fusion(f32[1024,2048]{1,0:T(8,128)} %fusion.96, bf16[128,2048]{1,0:T(8,128)(2,1)S(1)} %bitcast.90, bf16[1024,1024]{1,0:T(8,128)(2,1)S(1)} %copy-done.7, bf16[1024,128]{0,1:T(8,128)(2,1)S(1)} %bitcast.105, s32[128]{0:T(128)S(1)} %and_select_fusion, s32[1024]{0:T(1024)S(1)} %select_reduce_fusion), kind=kOutput, calls=%fused_computation.3 | convolution fusion | flops 809893888 | bytes 15471104 | tf_op jit(solution)/shard_map/dot_general | solution.py:374
  164.6 6.0 %fusion.22 = f32[2048,128]{1,0:T(8,128)} fusion(bf16[1024,2048]{1,0:T(8,128)(2,1)} %copy-done.31, bf16[1024,1024]{1,0:T(8,128)(2,1)S(1)} %copy-done.7, bf16[1024,128]{0,1:T(8,128)(2,1)S(1)} %bitcast.106, f32[1024]{0:T(1024)S(1)} %bitcast.125, s32[128]{0:T(128)S(1)} %and_select_fusion, s32[1024]{0:T(1024)S(1)} %select_reduce_fusion), kind=kOutput, calls=%fused_computation.55 | convolution fusion | flops 805830656 | bytes 7610880 | tf_op jit(solution)/shard_map/dot_general | solution.py:630
  170.6 4.5 %add_convert_fusion.5 = bf16[512,2048]{1,0:T(8,128)(2,1)} fusion(bf16[512,2048]{1,0:T(8,128)(2,1)} %collective-permute-done.8, bf16[1024,2048]{1,0:T(8,128)(2,1)} %add_convert_fusion.3), kind=kLoop, calls=%fused_computation.21 | loop fusion | flops 4194304 | bytes 6291456 | tf_op jit(solution)/shard_map/convert_element_type | solution.py:430
  176.4 6.3 %convolution_add_fusion.4 = f32[2048,128]{1,0:T(8,128)} fusion(f32[2048,128]{1,0:T(8,128)} %fusion.22, bf16[1024,2048]{1,0:T(8,128)(2,1)} %copy-done.11, bf16[1024,1024]{1,0:T(8,128)(2,1)S(1)} %copy-done.5, bf16[1024,128]{0,1:T(8,128)(2,1)S(1)} %bitcast.107, f32[1024]{0:T(1024)S(1)} %bitcast.120, s32[128]{0:T(128)S(1)} %and_select_fusion, ...), kind=kOutput, calls=%fused_computation.30 | convolution fusion | flops 806092800 | bytes 8659456 | tf_op jit(solution)/shard_map/dot_general | solution.py:630
  189.0 34.4 %mixer_backward.2 = (bf16[1024,2048]{1,0:T(8,128)(2,1)}, bf16[1024,256]{1,0:T(8,128)(2,1)}, bf16[1024,128]{1,0:T(8,128)(2,1)}) custom-call(s32[5]{0:T(128)} %pad_add_fusion.1.ends, f32[1024,2048]{1,0:T(8,128)} %convolution_add_fusion.z_ref.x_ref.xh_ref, f32[1024,2048]{1,0:T(8,128)} %convolution_add_fusion.z_ref.x_ref.xh_ref, ...), custom_call_target="tpu_custom_call" | custom-call | flops 3145728000 | bytes 25165824 | tf_op jit(solution)/shard_map/mixer_backward/pallas_call | solution.py:340
  223.5 13.5 %fusion.97 = f32[1024,2048]{1,0:T(8,128)S(1)} fusion(bf16[1024,2048]{1,0:T(8,128)(2,1)} %get-tuple-element.78, bf16[2048,2048]{1,0:T(8,128)(2,1)} %bitcast.93), kind=kOutput, calls=%fused_computation.265 | convolution fusion | flops 8589934592 | bytes 20971520 | tf_op jit(solution)/shard_map/dot_general | solution.py:374
  250.7 4.5 %fusion.98 = f32[2048,128]{1,0:T(8,128)} fusion(bf16[1024,2048]{1,0:T(8,128)(2,1)} %copy-done.9, bf16[1024,128]{1,0:T(8,128)(2,1)} %copy-done.41), kind=kOutput, calls=%fused_computation.266 | convolution fusion | flops 536870912 | bytes 5505024 | tf_op jit(solution)/shard_map/dot_general | solution.py:643
  255.3 3.9 add_convert_fusion.4
  269.7 34.2 %mixer_backward.3 = (bf16[1024,2048]{1,0:T(8,128)(2,1)}, bf16[1024,256]{1,0:T(8,128)(2,1)}, bf16[1024,128]{1,0:T(8,128)(2,1)}) custom-call(s32[5]{0:T(128)} %pad_add_fusion.ends, f32[1024,2048]{1,0:T(8,128)} %convolution_add_fusion.1.z_ref.x_ref.xh_ref, f32[1024,2048]{1,0:T(8,128)} %convolution_add_fusion.1.z_ref.x_ref.xh_ref, ...), custom_call_target="tpu_custom_call" | custom-call | flops 3145728000 | bytes 25165824 | tf_op jit(solution)/shard_map/mixer_backward/pallas_call | solution.py:340
  309.5 5.1 %convolution_add_fusion.2 = f32[2048,128]{1,0:T(8,128)} fusion(f32[2048,128]{1,0:T(8,128)} %fusion.80, bf16[1024,2048]{1,0:T(8,128)(2,1)} %get-tuple-element.95, f32[1024,512]{1,0:T(8,128)} %copy-done.2, s32[128]{0:T(128)S(1)} %and_select_fusion, s32[1024]{0:T(1024)S(1)} %select_reduce_fusion.1), kind=kOutput, calls=%fused_computation.28 | convolution fusion | flops 537395200 | bytes 6558208 | tf_op jit(solution)/shard_map/dot_general | solution.py:642
  316.5 3.7 convolution_add_fusion.3
  320.7 11.0 %fusion.99 = f32[1024,2048]{1,0:T(8,128)} fusion(bf16[1024,2048]{1,0:T(8,128)(2,1)S(1)} %copy-done.17, bf16[2048,2048]{1,0:T(8,128)(2,1)S(1)} %bitcast.102), kind=kOutput, calls=%fused_computation.267 | convolution fusion | flops 8589934592 | bytes 20971520 | tf_op jit(solution)/shard_map/dot_general | solution.py:374
  331.8 6.3 %add_convert_fusion.1 = bf16[1024,2048]{1,0:T(8,128)(2,1)} fusion(f32[1024,2048]{1,0:T(8,128)} %fusion.99, bf16[1024,128]{1,0:T(8,128)(2,1)S(1)} %fusion.19, bf16[1024,128]{1,0:T(8,128)(2,1)S(1)} %copy-done.60, bf16[1024,256]{1,0:T(8,128)(2,1)S(1)} %copy-done.58, bf16[2048,16]{1,0:T(8,128)(2,1)S(1)} %copy-done.35, bf16[2048,128]{1,0:T(8,128)(2,1)S(1)} %copy-done.39, ...), kind=kOutput, calls=%fused_computation.1 | convolution fusion | flops 2165309440 | bytes 15269888 | tf_op jit(solution)/shard_map/dot_general | solution.py:374
  339.9 6.6 %fusion.100 = f32[1024,2048]{1,0:T(8,128)} fusion(bf16[1024,1024]{1,0:T(8,128)(2,1)S(1)} %copy-done.5, bf16[1024,2048]{1,0:T(8,128)(2,1)S(1)} %copy-done.53), kind=kOutput, calls=%fused_computation.268 | convolution fusion | flops 4294967296 | bytes 14680064 | tf_op jit(solution)/shard_map/dot_general | solution.py:374
  346.6 6.8 %add_convert_fusion = bf16[1024,2048]{1,0:T(8,128)(2,1)} fusion(f32[1024,2048]{1,0:T(8,128)} %fusion.100, bf16[128,2048]{1,0:T(8,128)(2,1)S(1)} %bitcast.91, bf16[1024,1024]{1,0:T(8,128)(2,1)S(1)} %copy-done.5, bf16[1024,128]{0,1:T(8,128)(2,1)S(1)} %bitcast.108, s32[128]{0:T(128)S(1)} %and_select_fusion, s32[1024]{0:T(1024)S(1)} %select_reduce_fusion.1), kind=kOutput, calls=%fused_computation | convolution fusion | flops 809893888 | bytes 15471104 | tf_op jit(solution)/shard_map/dot_general | solution.py:374
  367.1 8.4 %collective-permute-done.20 = bf16[1280,128]{1,0:T(8,128)(2,1)S(1)} collective-permute-done((bf16[1280,128]{1,0:T(8,128)(2,1)S(1)}, bf16[1280,128]{1,0:T(8,128)(2,1)S(1)}, u32[]{:S(2)}, u32[]{:S(2)}) %collective-permute-start.20) | collective-permute-done | bytes 327712 | tf_op jit(solution)/shard_map/ppermute | solution.py:508
  376.7 5.5 %fusion.3 = bf16[512,2048]{1,0:T(8,128)(2,1)} fusion(bf16[512,2048]{1,0:T(8,128)(2,1)S(1)} %copy-done.3, bf16[512,2048]{1,0:T(8,128)(2,1)} %collective-permute-done.9, bf16[512,2048]{1,0:T(8,128)(2,1)} %collective-permute-done.19, bf16[1024,2048]{1,0:T(8,128)(2,1)S(1)} %copy-done.6, f32[512]{0:T(512)S(1)} %bitcast.131), kind=kLoop, calls=%fused_computation.14 | loop fusion | flops 9437184 | bytes 10487808 | tf_op jit(solution)/shard_map/convert_element_type | solution.py:693
  384.0 4.6 %collective-permute-done.22 = bf16[640,128]{1,0:T(8,128)(2,1)S(1)} collective-permute-done((bf16[640,128]{1,0:T(8,128)(2,1)S(1)}, bf16[640,128]{1,0:T(8,128)(2,1)S(1)}, u32[]{:S(2)}, u32[]{:S(2)}) %collective-permute-start.22) | collective-permute-done | bytes 163872 | tf_op jit(solution)/shard_map/ppermute | solution.py:508
  391.5 4.8 %collective-permute-done.23 = bf16[320,128]{1,0:T(8,128)(2,1)S(1)} collective-permute-done((bf16[320,128]{1,0:T(8,128)(2,1)S(1)}, bf16[320,128]{1,0:T(8,128)(2,1)S(1)}, u32[]{:S(2)}, u32[]{:S(2)}) %collective-permute-start.23) | collective-permute-done | bytes 81952 | tf_op jit(solution)/shard_map/ppermute | solution.py:508
  397.5 5.8 %collective-permute-done.24 = bf16[320,128]{1,0:T(8,128)(2,1)} collective-permute-done((bf16[320,128]{1,0:T(8,128)(2,1)}, bf16[320,128]{1,0:T(8,128)(2,1)}, u32[]{:S(2)}, u32[]{:S(2)}) %collective-permute-start.24) | collective-permute-done | bytes 81952 | tf_op jit(solution)/shard_map/ppermute | solution.py:519
  405.3 4.9 %collective-permute-done.25 = bf16[640,128]{1,0:T(8,128)(2,1)S(1)} collective-permute-done((bf16[640,128]{1,0:T(8,128)(2,1)S(1)}, bf16[640,128]{1,0:T(8,128)(2,1)S(1)}, u32[]{:S(2)}, u32[]{:S(2)}) %collective-permute-start.25) | collective-permute-done | bytes 163872 | tf_op jit(solution)/shard_map/ppermute | solution.py:519
  433.6 4.3 fusion.6
  438.4 5.0 %fusion.5 = f32[512,2048]{1,0:T(8,128)} fusion(bf16[512,2048]{1,0:T(8,128)(2,1)S(1)} %copy-done.3, bf16[512,2048]{1,0:T(8,128)(2,1)S(1)} %copy-done.14, bf16[512,2048]{1,0:T(8,128)(2,1)} %collective-permute-done.14, bf16[512,2048]{1,0:T(8,128)(2,1)} %collective-permute-done.21, f32[512]{0:T(512)S(1)} %broadcast_multiply_fusion, f32[512]{0:T(512)S(1)} %copy-done.46, ...), kind=kLoop, calls=%fused_computation.16 | loop fusion | flops 13631488 | bytes 14694400 | tf_op jit(solution)/shard_map/sub | solution.py:697
  (348 shorter events, 142.2 us)
Async XLA Ops:
  7.0 26.9 %collective-permute-start = (bf16[512,2048]{1,0:T(8,128)(2,1)}, bf16[512,2048]{1,0:T(8,128)(2,1)}, u32[]{:S(2)}, u32[]{:S(2)}) collective-permute-start(bf16[512,2048]{1,0:T(8,128)(2,1)} %fusion.2), channel_id=1, source_target_pairs={{0,1},{1,0},{2,3},{3,2},{4,5},{5,4},{6,7},{7,6},{8,9},{9,8},{10,11... | collective-permute-start | bytes 6291464 | tf_op jit(solution)/shard_map/ppermute | solution.py:407
  7.5 65.4 %collective-permute-start.2 = (bf16[512,2048]{1,0:T(8,128)(2,1)}, bf16[512,2048]{1,0:T(8,128)(2,1)}, u32[]{:S(2)}, u32[]{:S(2)}) collective-permute-start(bf16[512,2048]{1,0:T(8,128)(2,1)} %fusion.2), channel_id=1, source_target_pairs={{0,2},{1,3},{2,0},{3,1},{4,6},{5,7},{6,4},{7,5},{8,10},{9,11},{10,... | collective-permute-start | bytes 6291464 | tf_op jit(solution)/shard_map/ppermute | solution.py:404
  10.0 65.0 %collective-permute-start.1 = (bf16[512,2048]{1,0:T(8,128)(2,1)S(1)}, bf16[512,2048]{1,0:T(8,128)(2,1)}, u32[]{:S(2)}, u32[]{:S(2)}) collective-permute-start(bf16[512,2048]{1,0:T(8,128)(2,1)S(1)} %copy-done.13), channel_id=1, source_target_pairs={{0,1},{1,0},{2,3},{3,2},{4,5},{5,4},{6,7},{7,6},{8,9},{9,8},{10,11... | collective-permute-start | bytes 6291464 | tf_op jit(solution)/shard_map/ppermute | solution.py:407
  72.6 51.8 %collective-permute-start.4 = (bf16[512,2048]{1,0:T(8,128)(2,1)S(1)}, bf16[512,2048]{1,0:T(8,128)(2,1)}, u32[]{:S(2)}, u32[]{:S(2)}) collective-permute-start(bf16[512,2048]{1,0:T(8,128)(2,1)S(1)} %copy-done.13), channel_id=1, source_target_pairs={{0,2},{1,3},{2,0},{3,1},{4,6},{5,7},{6,4},{7,5},{8,10},{9,11},{10,... | collective-permute-start | bytes 6291464 | tf_op jit(solution)/shard_map/ppermute | solution.py:404
  72.9 16.1 %collective-permute-start.3 = (bf16[512,2048]{1,0:T(8,128)(2,1)}, bf16[512,2048]{1,0:T(8,128)(2,1)S(1)}, u32[]{:S(2)}, u32[]{:S(2)}) collective-permute-start(bf16[512,2048]{1,0:T(8,128)(2,1)} %collective-permute-done.2), channel_id=1, source_target_pairs={{0,1},{1,0},{2,3},{3,2},{4,5},{5,4},{6,7},{7,6},{8,9},{9,8},{10,11... | collective-permute-start | bytes 6291464 | tf_op jit(solution)/shard_map/ppermute | solution.py:407
  124.3 4.4 collective-permute-start.5
  156.2 14.4 %collective-permute-start.8 = (bf16[512,2048]{1,0:T(8,128)(2,1)}, bf16[512,2048]{1,0:T(8,128)(2,1)}, u32[]{:S(2)}, u32[]{:S(2)}) collective-permute-start(bf16[512,2048]{1,0:T(8,128)(2,1)} %slice.220), channel_id=1, source_target_pairs={{0,1},{1,0},{2,3},{3,2},{4,5},{5,4},{6,7},{7,6},{8,9},{9,8},{10,11... | collective-permute-start | bytes 6291464 | tf_op jit(solution)/shard_map/ppermute | solution.py:407
  175.2 48.3 %collective-permute-start.9 = (bf16[512,2048]{1,0:T(8,128)(2,1)}, bf16[512,2048]{1,0:T(8,128)(2,1)}, u32[]{:S(2)}, u32[]{:S(2)}) collective-permute-start(bf16[512,2048]{1,0:T(8,128)(2,1)} %add_convert_fusion.5), channel_id=1, source_target_pairs={{0,2},{1,3},{2,0},{3,1},{4,6},{5,7},{6,4},{7,5},{8,10},{9,11},{10,... | collective-permute-start | bytes 6291464 | tf_op jit(solution)/shard_map/ppermute | solution.py:404
  183.9 4.3 collective-permute-start.10
  245.2 10.2 %collective-permute-start.11 = (bf16[512,2048]{1,0:T(8,128)(2,1)}, bf16[512,2048]{1,0:T(8,128)(2,1)}, u32[]{:S(2)}, u32[]{:S(2)}) collective-permute-start(bf16[512,2048]{1,0:T(8,128)(2,1)} %slice.223), channel_id=1, source_target_pairs={{0,1},{1,0},{2,3},{3,2},{4,5},{5,4},{6,7},{7,6},{8,9},{9,8},{10,11... | collective-permute-start | bytes 6291464 | tf_op jit(solution)/shard_map/ppermute | solution.py:407
  249.8 5.5 %collective-permute-start.12 = (bf16[512,128]{1,0:T(8,128)(2,1)S(1)}, bf16[512,128]{1,0:T(8,128)(2,1)S(1)}, u32[]{:S(2)}, u32[]{:S(2)}) collective-permute-start(bf16[512,128]{1,0:T(8,128)(2,1)S(1)} %dynamic-slice_convert_fusion.6), channel_id=1, source_target_pairs={{0,2},{1,3},{2,0},{3,1},{4,6},{5,7},{6,4},{7,5},{8,10},{9,11},{10,... | collective-permute-start | bytes 393224 | tf_op jit(solution)/shard_map/ppermute | solution.py:508
  259.2 47.5 %collective-permute-start.14 = (bf16[512,2048]{1,0:T(8,128)(2,1)}, bf16[512,2048]{1,0:T(8,128)(2,1)}, u32[]{:S(2)}, u32[]{:S(2)}) collective-permute-start(bf16[512,2048]{1,0:T(8,128)(2,1)} %add_convert_fusion.4), channel_id=1, source_target_pairs={{0,2},{1,3},{2,0},{3,1},{4,6},{5,7},{6,4},{7,5},{8,10},{9,11},{10,... | collective-permute-start | bytes 6291464 | tf_op jit(solution)/shard_map/ppermute | solution.py:404
  260.3 6.3 %collective-permute-start.13 = (bf16[768,128]{1,0:T(8,128)(2,1)S(1)}, bf16[768,128]{1,0:T(8,128)(2,1)S(1)}, u32[]{:S(2)}, u32[]{:S(2)}) collective-permute-start(bf16[768,128]{1,0:T(8,128)(2,1)S(1)} %pad_maximum_fusion.11), channel_id=1, source_target_pairs={{0,4},{4,0},{8,12},{12,8},{16,20},{20,16},{24,28},{28,24},{1,5},{5... | collective-permute-start | bytes 589832 | tf_op jit(solution)/shard_map/ppermute | solution.py:508
  268.2 35.8 %collective-permute-start.15 = (bf16[384,128]{1,0:T(8,128)(2,1)}, bf16[384,128]{1,0:T(8,128)(2,1)}, u32[]{:S(2)}, u32[]{:S(2)}) collective-permute-start(bf16[384,128]{1,0:T(8,128)(2,1)} %pad_maximum_fusion.19), channel_id=1, source_target_pairs={{0,8},{4,12},{8,0},{12,4},{16,24},{20,28},{24,16},{28,20},{1,9},{5... | collective-permute-start | bytes 294920 | tf_op jit(solution)/shard_map/ppermute | solution.py:508
  306.8 9.2 %collective-permute-start.16 = (bf16[192,128]{1,0:T(8,128)(2,1)S(1)}, bf16[192,128]{1,0:T(8,128)(2,1)S(1)}, u32[]{:S(2)}, u32[]{:S(2)}) collective-permute-start(bf16[192,128]{1,0:T(8,128)(2,1)S(1)} %pad_maximum_fusion.26), channel_id=1, source_target_pairs={{0,16},{4,20},{8,24},{12,28},{16,0},{20,4},{24,8},{28,12},{1,17},{... | collective-permute-start | bytes 147464 | tf_op jit(solution)/shard_map/ppermute | solution.py:508
  316.0 41.7 %collective-permute-start.29 = (bf16[192,128]{1,0:T(8,128)(2,1)S(1)}, bf16[192,128]{1,0:T(8,128)(2,1)}, u32[]{:S(2)}, u32[]{:S(2)}) collective-permute-start(bf16[192,128]{1,0:T(8,128)(2,1)S(1)} %pad_maximum_fusion.27), channel_id=1, source_target_pairs={{0,16},{4,20},{8,24},{12,28},{16,0},{20,4},{24,8},{28,12},{1,17},{... | collective-permute-start | bytes 147464 | tf_op jit(solution)/shard_map/ppermute | solution.py:519
  320.3 17.8 %collective-permute-start.17 = (bf16[1024,128]{1,0:T(8,128)(2,1)S(1)}, bf16[1024,128]{1,0:T(8,128)(2,1)S(1)}, u32[]{:S(2)}, u32[]{:S(2)}) collective-permute-start(bf16[1024,128]{1,0:T(8,128)(2,1)S(1)} %dynamic-slice_convert_fusion.1), channel_id=1, source_target_pairs={{0,1},{1,0},{2,3},{3,2},{4,5},{5,4},{6,7},{7,6},{8,9},{9,8},{10,11... | collective-permute-start | bytes 786440 | tf_op jit(solution)/shard_map/ppermute | solution.py:508
  338.8 14.5 %collective-permute-start.18 = (bf16[512,128]{1,0:T(8,128)(2,1)}, bf16[512,128]{1,0:T(8,128)(2,1)}, u32[]{:S(2)}, u32[]{:S(2)}) collective-permute-start(bf16[512,128]{1,0:T(8,128)(2,1)} %dynamic-slice_convert_fusion.4), channel_id=1, source_target_pairs={{0,2},{1,3},{2,0},{3,1},{4,6},{5,7},{6,4},{7,5},{8,10},{9,11},{10,... | collective-permute-start | bytes 393224 | tf_op jit(solution)/shard_map/ppermute | solution.py:508
  357.6 19.1 %collective-permute-start.19 = (bf16[512,2048]{1,0:T(8,128)(2,1)}, bf16[512,2048]{1,0:T(8,128)(2,1)}, u32[]{:S(2)}, u32[]{:S(2)}) collective-permute-start(bf16[512,2048]{1,0:T(8,128)(2,1)} %slice.187), channel_id=1, source_target_pairs={{0,1},{1,0},{2,3},{3,2},{4,5},{5,4},{6,7},{7,6},{8,9},{9,8},{10,11... | collective-permute-start | bytes 6291464 | tf_op jit(solution)/shard_map/ppermute | solution.py:407
  359.6 5.2 %collective-permute-start.30 = (bf16[384,128]{1,0:T(8,128)(2,1)S(1)}, bf16[384,128]{1,0:T(8,128)(2,1)S(1)}, u32[]{:S(2)}, u32[]{:S(2)}) collective-permute-start(bf16[384,128]{1,0:T(8,128)(2,1)S(1)} %pad_maximum_fusion.20), channel_id=1, source_target_pairs={{0,8},{4,12},{8,0},{12,4},{16,24},{20,28},{24,16},{28,20},{1,9},{5... | collective-permute-start | bytes 294920 | tf_op jit(solution)/shard_map/ppermute | solution.py:519
  364.9 10.6 %collective-permute-start.20 = (bf16[1280,128]{1,0:T(8,128)(2,1)S(1)}, bf16[1280,128]{1,0:T(8,128)(2,1)S(1)}, u32[]{:S(2)}, u32[]{:S(2)}) collective-permute-start(bf16[1280,128]{1,0:T(8,128)(2,1)S(1)} %pad_maximum_fusion.6), channel_id=1, source_target_pairs={{0,4},{4,0},{8,12},{12,8},{16,20},{20,16},{24,28},{28,24},{1,5},{5... | collective-permute-start | bytes 983048 | tf_op jit(solution)/shard_map/ppermute | solution.py:508
  366.5 17.5 %collective-permute-start.31 = (bf16[768,128]{1,0:T(8,128)(2,1)S(1)}, bf16[768,128]{1,0:T(8,128)(2,1)S(1)}, u32[]{:S(2)}, u32[]{:S(2)}) collective-permute-start(bf16[768,128]{1,0:T(8,128)(2,1)S(1)} %pad_maximum_fusion.12), channel_id=1, source_target_pairs={{0,4},{4,0},{8,12},{12,8},{16,20},{20,16},{24,28},{28,24},{1,5},{5... | collective-permute-start | bytes 589832 | tf_op jit(solution)/shard_map/ppermute | solution.py:519
  382.3 6.3 %collective-permute-start.22 = (bf16[640,128]{1,0:T(8,128)(2,1)S(1)}, bf16[640,128]{1,0:T(8,128)(2,1)S(1)}, u32[]{:S(2)}, u32[]{:S(2)}) collective-permute-start(bf16[640,128]{1,0:T(8,128)(2,1)S(1)} %pad_maximum_fusion.13), channel_id=1, source_target_pairs={{0,8},{4,12},{8,0},{12,4},{16,24},{20,28},{24,16},{28,20},{1,9},{5... | collective-permute-start | bytes 491528 | tf_op jit(solution)/shard_map/ppermute | solution.py:508
  388.7 7.6 %collective-permute-start.23 = (bf16[320,128]{1,0:T(8,128)(2,1)S(1)}, bf16[320,128]{1,0:T(8,128)(2,1)S(1)}, u32[]{:S(2)}, u32[]{:S(2)}) collective-permute-start(bf16[320,128]{1,0:T(8,128)(2,1)S(1)} %pad_maximum_fusion.21), channel_id=1, source_target_pairs={{0,16},{4,20},{8,24},{12,28},{16,0},{20,4},{24,8},{28,12},{1,17},{... | collective-permute-start | bytes 245768 | tf_op jit(solution)/shard_map/ppermute | solution.py:508
  390.5 14.6 %collective-permute-start.32 = (bf16[512,128]{1,0:T(8,128)(2,1)S(1)}, bf16[512,128]{1,0:T(8,128)(2,1)S(1)}, u32[]{:S(2)}, u32[]{:S(2)}) collective-permute-start(bf16[512,128]{1,0:T(8,128)(2,1)S(1)} %pad_maximum_fusion.18), channel_id=1, source_target_pairs={{0,2},{1,3},{2,0},{3,1},{4,6},{5,7},{6,4},{7,5},{8,10},{9,11},{10,... | collective-permute-start | bytes 393224 | tf_op jit(solution)/shard_map/ppermute | solution.py:519
  397.0 6.2 %collective-permute-start.24 = (bf16[320,128]{1,0:T(8,128)(2,1)}, bf16[320,128]{1,0:T(8,128)(2,1)}, u32[]{:S(2)}, u32[]{:S(2)}) collective-permute-start(bf16[320,128]{1,0:T(8,128)(2,1)} %pad_maximum_fusion.22), channel_id=1, source_target_pairs={{0,16},{4,20},{8,24},{12,28},{16,0},{20,4},{24,8},{28,12},{1,17},{... | collective-permute-start | bytes 245768 | tf_op jit(solution)/shard_map/ppermute | solution.py:519
  404.8 5.4 %collective-permute-start.25 = (bf16[640,128]{1,0:T(8,128)(2,1)S(1)}, bf16[640,128]{1,0:T(8,128)(2,1)S(1)}, u32[]{:S(2)}, u32[]{:S(2)}) collective-permute-start(bf16[640,128]{1,0:T(8,128)(2,1)S(1)} %pad_maximum_fusion.14), channel_id=1, source_target_pairs={{0,8},{4,12},{8,0},{12,4},{16,24},{20,28},{24,16},{28,20},{1,9},{5... | collective-permute-start | bytes 491528 | tf_op jit(solution)/shard_map/ppermute | solution.py:519
  405.2 10.7 %collective-permute-start.33 = (bf16[1024,128]{1,0:T(8,128)(2,1)S(1)}, bf16[1024,128]{1,0:T(8,128)(2,1)S(1)}, u32[]{:S(2)}, u32[]{:S(2)}) collective-permute-start(bf16[1024,128]{1,0:T(8,128)(2,1)S(1)} %pad_maximum_fusion.10), channel_id=1, source_target_pairs={{0,1},{1,0},{2,3},{3,2},{4,5},{5,4},{6,7},{7,6},{8,9},{9,8},{10,11... | collective-permute-start | bytes 786440 | tf_op jit(solution)/shard_map/ppermute | solution.py:519
  410.3 7.1 %collective-permute-start.26 = (bf16[1280,128]{1,0:T(8,128)(2,1)S(1)}, bf16[1280,128]{1,0:T(8,128)(2,1)S(1)}, u32[]{:S(2)}, u32[]{:S(2)}) collective-permute-start(bf16[1280,128]{1,0:T(8,128)(2,1)S(1)} %pad_maximum_fusion.7), channel_id=1, source_target_pairs={{0,4},{4,0},{8,12},{12,8},{16,20},{20,16},{24,28},{28,24},{1,5},{5... | collective-permute-start | bytes 983048 | tf_op jit(solution)/shard_map/ppermute | solution.py:519
  415.9 17.7 %collective-permute-start.21 = (bf16[512,2048]{1,0:T(8,128)(2,1)}, bf16[512,2048]{1,0:T(8,128)(2,1)}, u32[]{:S(2)}, u32[]{:S(2)}) collective-permute-start(bf16[512,2048]{1,0:T(8,128)(2,1)} %slice.191), channel_id=1, source_target_pairs={{0,1},{1,0},{2,3},{3,2},{4,5},{5,4},{6,7},{7,6},{8,9},{9,8},{10,11... | collective-permute-start | bytes 6291464 | tf_op jit(solution)/shard_map/ppermute | solution.py:407
  418.2 5.0 %collective-permute-start.27 = (bf16[512,128]{1,0:T(8,128)(2,1)S(1)}, bf16[512,128]{1,0:T(8,128)(2,1)S(1)}, u32[]{:S(2)}, u32[]{:S(2)}) collective-permute-start(bf16[512,128]{1,0:T(8,128)(2,1)S(1)} %pad_maximum_fusion.16), channel_id=1, source_target_pairs={{0,2},{1,3},{2,0},{3,1},{4,6},{5,7},{6,4},{7,5},{8,10},{9,11},{10,... | collective-permute-start | bytes 393224 | tf_op jit(solution)/shard_map/ppermute | solution.py:519
  423.4 7.8 %collective-permute-start.28 = (bf16[1024,128]{1,0:T(8,128)(2,1)S(1)}, bf16[1024,128]{1,0:T(8,128)(2,1)}, u32[]{:S(2)}, u32[]{:S(2)}) collective-permute-start(bf16[1024,128]{1,0:T(8,128)(2,1)S(1)} %pad_maximum_fusion.8), channel_id=1, source_target_pairs={{0,1},{1,0},{2,3},{3,2},{4,5},{5,4},{6,7},{7,6},{8,9},{9,8},{10,11... | collective-permute-start | bytes 786440 | tf_op jit(solution)/shard_map/ppermute | solution.py:519
  (70 other events, 535.3 us)

commit v3 on v2

--- a/solution.py
+++ b/solution.py
@@ -6,6 +6,7 @@
 from jax.experimental import pallas as pl
 from jax.experimental.pallas import tpu as pltpu
 from jax.sharding import PartitionSpec as P
+
 
 F32, BF16 = jnp.float32, jnp.bfloat16
 L = 128
@@ -91,11 +92,13 @@
 
 
 def forward_kernel(
-    count, ends, z_ref, x_ref, bc_ref, dt_ref, taps_ref, bct_ref, head_ref, chan_ref,
+    count, ends, z_ref, x_ref, bc_ref, dt_ref, sel_ref, down_ref,
+    taps_ref, bct_ref, head_ref, chan_ref,
     y_ref, g_ref, sum_ref, st_ref, state, xprev, bcprev,
 ):
     c = pl.program_id(0)
-    pairs = x_ref.shape[1] // 128
+    width = x_ref.shape[1]
+    pairs = width // 128
 
     @pl.when(c == 0)
     def _():
@@ -159,14 +162,15 @@
     ones = jnp.ones((8, 128), BF16)
     sq_row = sum(mm(ones, part, NT) for part in split3(squares))
     sum_ref[...] = sq_row
+    g_ref[:, width:] = (mm(g_ref[:, :width], down_ref[...]) * sel_ref[...]).astype(BF16)
     xprev[...] = x_ref[L - HALO :, :]
     bcprev[...] = bc_ref[L - HALO :, :]
 
 
 def backward_kernel(
     count, seq, ends, z_ref, x_ref, xh_ref, bc_ref, bch_ref, dt_ref, gm_ref, y_ref, st_ref, rk_ref,
-    taps_ref, bct_ref, head_ref, chan_ref,
-    dzx_ref, dbc_ref, ddt_ref, dstate, dnext, dbnext, ends_row,
+    lora_ref, nb_ref, sel_ref, up_ref, taps_ref, bct_ref, head_ref, chan_ref,
+    dzx_ref, inup_ref, indown_ref, dstate, dnext, dbnext, ends_row,
 ):
     g = pl.program_id(0)
     c = pl.num_programs(0) - 1 - g
@@ -179,6 +183,8 @@
         dnext[...] = jnp.zeros_like(dnext)
         dbnext[...] = jnp.zeros_like(dbnext)
         ends_row[...] = jnp.zeros_like(ends_row)
+        inup_ref[...] = jnp.zeros_like(inup_ref)
+        indown_ref[...] = jnp.zeros_like(indown_ref)
 
     t0 = c * L
     rows, cols, row_start, col_start, last_start = chunk_geometry(t0, ends, count)
@@ -279,32 +285,44 @@
         cut = slice(half * 128, half * 128 + 128)
         dpre = grad * slope
         ext = jnp.concatenate([dpre, dbnext[:, cut]], axis=0)
-        dbc_ref[:, cut] = conv_back(ext, bct_ref[:, cut], ok).astype(BF16)
+        place = slice(2 * width + half * 128, 2 * width + half * 128 + 128)
+        dzx_ref[:, place] = conv_back(ext, bct_ref[:, cut], ok).astype(BF16)
         dbnext[:, cut] = dpre[:HALO]
     d_cum = d_cum + jnp.where(sub == L - 1, ends_row[0:1, :], 0.0)
     ends_row[...] = d_end
     d_decay = sum(mm(up_mask, part) for part in split3(d_cum))
-    ddt_ref[...] = ((d_dt + head_ref[1:2] * d_decay) * sigmoid(raw)).astype(BF16)
-
-
-def mixer_forward(ends, zx, small, taps, bctaps, heads, chans):
-    seq, width = zx.shape[0], zx.shape[1] // 2
+    d_raw = (d_dt + head_ref[1:2] * d_decay) * sigmoid(raw)
+    dzx_ref[:, 2 * width + 256 : 2 * width + 384] = d_raw.astype(BF16)
+    mid = mm(dzx_ref[:, : 2 * width], up_ref[...], NT) * sel_ref[...]
+    dzx_ref[:, 2 * width + 384 :] = mid.astype(BF16)
+    mid_turn = mid.T.astype(BF16)
+    lora_turn = lora_ref[...].astype(F32).T.astype(BF16)
+    for k in range(0, 2 * width, 256):
+        cut = slice(k, k + 256)
+        inup_ref[:, cut] += mm(lora_turn, dzx_ref[:, cut])
+    for k in range(0, nb_ref.shape[1], 256):
+        cut = slice(k, k + 256)
+        indown_ref[:, cut] += mm(mid_turn, nb_ref[:, cut])
+
+
+def mixer_forward(ends, zx, small, select, out_down, taps, bctaps, heads, chans):
+    seq, width = zx.shape[0], chans.shape[1]
     count = ends.shape[0] - 1
     chunks = seq // L
     place = lambda c, e: lax.rem(c + e[count] * (chunks // 2), chunks)
     fixed = lambda shape: pl.BlockSpec(shape, lambda c, e: (0,) * len(shape))
-    blk = lambda w, j=0: pl.BlockSpec((L, w), lambda c, e: (place(c, e), j))
+    blk = lambda w, first=0: pl.BlockSpec((L, w), lambda c, e: (place(c, e), first // w))
     return pl.pallas_call(
         functools.partial(forward_kernel, count),
         grid_spec=pltpu.PrefetchScalarGridSpec(
             num_scalar_prefetch=1,
             grid=(chunks,),
             in_specs=[
-                blk(width, 0), blk(width, 1), blk(256, 0), blk(128, 2),
+                blk(width), blk(width, width), blk(256), blk(128, 256), blk(128), fixed((width, 128)),
                 fixed((5, width)), fixed((5, 256)), fixed((2, 128)), fixed((2, width)),
             ],
             out_specs=[
-                blk(width), blk(width), pl.BlockSpec((8, L), lambda c, e: (0, place(c, e))),
+                blk(width), blk(width + 128), pl.BlockSpec((8, L), lambda c, e: (0, place(c, e))),
                 pl.BlockSpec((1, 128, width), lambda c, e: (c, 0, 0)),
             ],
             scratch_shapes=[
@@ -313,7 +331,7 @@
         ),
         out_shape=[
             jax.ShapeDtypeStruct((seq, width), F32),
-            jax.ShapeDtypeStruct((seq, width), BF16),
+            jax.ShapeDtypeStruct((seq, width + 128), BF16),
             jax.ShapeDtypeStruct((8, seq), F32),
             jax.ShapeDtypeStruct((chunks, 128, width), BF16),
         ],
@@ -322,20 +340,21 @@
             flops=seq * width * 1200, bytes_accessed=seq * width * 16, transcendentals=seq * width * 6
         ),
         name="mixer_forward",
-    )(ends, zx, zx, small, small, taps, bctaps, heads, chans)
-
-
-def mixer_backward(ends, zx, small, gm, y, states, rk, taps, bctaps, heads, chans):
+    )(ends, zx, zx, small, small, select, out_down, taps, bctaps, heads, chans)
+
+
+def mixer_backward(ends, zx, small, gm, y, states, rk, lora, normed, select, in_up, taps, bctaps, heads, chans):
     seq, width = gm.shape
+    model = normed.shape[1]
     count = ends.shape[0] - 1
     chunks = seq // L
     last = chunks - 1
     step = L // HALO
     place = lambda c, e: lax.rem(c + e[count] * (chunks // 2), chunks)
     fixed = lambda shape: pl.BlockSpec(shape, lambda g, e: (0,) * len(shape))
-    blk = lambda w, j=0: pl.BlockSpec((L, w), lambda g, e: (place(last - g, e), j))
-    halo = lambda w, j=0: pl.BlockSpec(
-        (HALO, w), lambda g, e: (place(jnp.maximum(last - g - 1, 0), e) * step + step - 1, j)
+    blk = lambda w, first=0: pl.BlockSpec((L, w), lambda g, e: (place(last - g, e), first // w))
+    halo = lambda w, first=0: pl.BlockSpec(
+        (HALO, w), lambda g, e: (place(jnp.maximum(last - g - 1, 0), e) * step + step - 1, first // w)
     )
     return pl.pallas_call(
         functools.partial(backward_kernel, count, seq),
@@ -343,27 +362,31 @@
             num_scalar_prefetch=1,
             grid=(chunks,),
             in_specs=[
-                blk(width, 0), blk(width, 1), halo(width, 1), blk(256, 0), halo(256, 0), blk(128, 2),
-                blk(width), blk(width), pl.BlockSpec((1, 128, width), lambda g, e: (last - g, 0, 0)), blk(256),
+                blk(width), blk(width, width), halo(width, width), blk(256), halo(256), blk(128, 256), blk(width), blk(width),
+                pl.BlockSpec((1, 128, width), lambda g, e: (last - g, 0, 0)), blk(256),
+                blk(128), blk(model), blk(128), fixed((128, 2 * width)),
                 fixed((5, width)), fixed((5, 256)), fixed((2, 128)), fixed((2, width)),
             ],
-            out_specs=[blk(2 * width), blk(256), blk(128)],
+            out_specs=[blk(2 * width + 512), fixed((128, 2 * width)), fixed((128, model))],
             scratch_shapes=[
                 pltpu.VMEM((128, width), F32), pltpu.VMEM((HALO, width), F32), pltpu.VMEM((HALO, 256), F32),
                 pltpu.VMEM((8, 128), F32),
             ],
         ),
         out_shape=[
-            jax.ShapeDtypeStruct((seq, 2 * width), BF16),
-            jax.ShapeDtypeStruct((seq, 256), BF16),
-            jax.ShapeDtypeStruct((seq, 128), BF16),
+            jax.ShapeDtypeStruct((seq, 2 * width + 512), BF16),
+            jax.ShapeDtypeStruct((128, 2 * width), F32),
+            jax.ShapeDtypeStruct((128, model), F32),
         ],
         compiler_params=pltpu.CompilerParams(dimension_semantics=("arbitrary",)),
         cost_estimate=pl.CostEstimate(
             flops=seq * width * 3000, bytes_accessed=seq * width * 24, transcendentals=seq * width * 8
         ),
         name="mixer_backward",
-    )(ends, zx, zx, zx, small, small, small, gm, y, states, rk, taps, bctaps, heads, chans)
+    )(
+        ends, zx, zx, zx, small, small, small, gm, y, states, rk, lora, normed, select, in_up,
+        taps, bctaps, heads, chans,
+    )
 
 
 EPS = 1e-05
@@ -374,7 +397,7 @@
     return lax.dot_general(a, b, dims, preferred_element_type=F32)
 
 
-def row_places(own_row, core, flipped):
+def row_places(core, flipped):
     shift = core * (ROW_LEN // 2) if flipped else 0
     return jnp.remainder(jnp.arange(ROW_LEN, dtype=jnp.int32) + shift, ROW_LEN)
 
@@ -486,50 +509,64 @@
     return lax.optimization_barrier((v,) + done)[0]
 
 
-def exchange_steps(axis):
+def exchange_steps(axis, wide):
     size = lax.axis_size(axis)
     assert size & (size - 1) == 0
-    steps, mask = [], 1
-    while mask < size:
-        bit = (lax.axis_index(axis) // mask) % 2
-        steps.append((axis, bit, [(i, i ^ mask) for i in range(size)]))
-        mask *= 2
+    steps, base = [], 1
+    while base < size:
+        ways = 4 if wide and base > 1 and size >= 4 * base else 2
+        digit = (lax.axis_index(axis) // base) % ways
+        pairs = [[(i, i ^ (a * base)) for i in range(size)] for a in range(1, ways)]
+        steps.append((axis, digit, pairs))
+        base *= ways
     return steps
 
 
-def half_of(v, which):
-    size = v.shape[0] // 2
+def piece_of(v, which, ways):
+    size = v.shape[0] // ways
     return lax.dynamic_slice_in_dim(v, which * size, size, 0)
 
 
 def scatter_sum(arrays, step):
-    axis, bit, pairs = step
-    sent = jnp.concatenate([half_of(v, 1 - bit) for v in arrays], axis=0).astype(BF16)
-    came = lax.ppermute(sent, axis, pairs).astype(F32)
+    axis, digit, pairs = step
+    ways = len(pairs) + 1
+    came = []
+    for a in range(1, ways):
+        sent = jnp.concatenate([piece_of(v, digit ^ a, ways) for v in arrays], axis=0)
+        came.append(lax.ppermute(sent.astype(BF16), axis, pairs[a - 1]))
     sums, first = [], 0
     for v in arrays:
-        size = v.shape[0] // 2
-        sums.append(half_of(v, bit) + came[first : first + size])
+        size = v.shape[0] // ways
+        total = piece_of(v, digit, ways)
+        for block in came:
+            total = total + block[first : first + size].astype(F32)
+        sums.append(total)
         first += size
     return sums
 
 
-def gather_halves(arrays, step):
-    axis, bit, pairs = step
-    came = lax.ppermute(jnp.concatenate(arrays, axis=0), axis, pairs)
+def gather_pieces(arrays, step):
+    axis, digit, pairs = step
+    ways = len(pairs) + 1
+    sent = jnp.concatenate(arrays, axis=0)
+    blocks = [sent] + [lax.ppermute(sent, axis, pairs[a - 1]) for a in range(1, ways)]
     wholes, first = [], 0
     for v in arrays:
-        other = came[first : first + v.shape[0]]
+        parts = [block[first : first + v.shape[0]] for block in blocks]
         first += v.shape[0]
-        wholes.append(
-            jnp.concatenate([jnp.where(bit == 0, v, other), jnp.where(bit == 0, other, v)], axis=0)
-        )
+        placed = []
+        for q in range(ways):
+            value = parts[q]
+            for d in range(1, ways):
+                value = jnp.where(digit == d, parts[q ^ d], value)
+            placed.append(value)
+        wholes.append(jnp.concatenate(placed, axis=0))
     return wholes
 
 
 class FactorSum:
     def __init__(self, shared, split):
-        self.near, self.far = exchange_steps("tensor"), exchange_steps("dp")
+        self.near, self.far = exchange_steps("tensor", False), exchange_steps("dp", True)
         self.arrays, self.split, self.done = [shared], split, 0
 
     def hop(self):
@@ -545,7 +582,7 @@
         if at < near + far:
             self.arrays = scatter_sum(self.arrays, steps[at])
         else:
-            self.arrays = gather_halves(self.arrays, steps[total - 1 - at])
+            self.arrays = gather_pieces(self.arrays, steps[total - 1 - at])
         self.done += 1
         if self.done == near + 2 * far:
             self.split = self.arrays[1]
@@ -583,11 +620,13 @@
     zx_weight = zx_weight.reshape(model, 2 * width)
     pad = lambda v: jnp.pad(v, ((0, 0), (0, 128 - heads_here)))
     small_weight = jnp.concatenate([state_weight, pad(step_weight), in_down], axis=1)
+    proj_weight = jnp.concatenate([zx_weight, small_weight], axis=1)
+    back_weight = jnp.concatenate([out_weight, out_up], axis=0)
     heads = jnp.concatenate([pad(head_values[0:1]), pad(-jnp.exp(head_values[1:2]))], axis=0)
     chans = jnp.stack([jnp.repeat(head_values[2], HEAD), gated_gain])
     columns = jnp.arange(reduced, dtype=jnp.int32) // rank
 
-    places = row_places(links.own_row, links.core, links.flipped)
+    places = row_places(links.core, links.flipped)
     turn = (links.core if links.flipped else 0) * jnp.ones((1,), jnp.int32)
     base = lax.axis_index("dp") * rows
     row_data = []
@@ -608,43 +647,38 @@
         ends, select = row_data[row]
         small = dot(nb, small_weight)
         lora = (small[:, 384:] * select).astype(BF16)
-        zx = dot(nb, zx_weight) + dot(lora, in_up)
-        y, gained, squares, states = mixer_forward(ends, zx, small, conv_taps, state_taps, heads, chans)
+        zx = dot(nb, proj_weight[:, : 2 * width]) + dot(lora, in_up)
+        y, gained, squares, states = mixer_forward(
+            ends, zx, small, select, out_down, conv_taps, state_taps, heads, chans
+        )
         return small, lora, zx, y, gained, squares, states
 
     def cotangents(row, cot, gained):
         low = (dot(cot, out_up, NT) * row_data[row][1]).astype(BF16)
         grad = dot(cot, out_weight, NT) + dot(low, out_down, NT)
-        return low, grad, jnp.sum(grad * gained.astype(F32), axis=1)
-
-    def project_out(row, gained):
-        low = (dot(gained, out_down) * row_data[row][1]).astype(BF16)
-        return (dot(gained, out_weight) + dot(low, out_up)).astype(BF16)
+        return low, grad, jnp.sum(grad * gained[:, :width].astype(F32), axis=1)
+
+    def project_out(gained):
+        return dot(gained, back_weight).astype(BF16)
 
     def out_gradients(row, low, gained, scale):
-        select = row_data[row][1]
         scaled_low = (low.astype(F32) * scale[:, None]).astype(BF16)
-        lora_back = (dot(gained, out_down) * select * scale[:, None]).astype(BF16)
+        lora_back = (gained[:, width:].astype(F32) * scale[:, None]).astype(BF16)
         return (
-            lax.dot_general(gained, scaled_low, TN, preferred_element_type=F32),
-            lax.dot_general(lora_back, cots[row], TN, preferred_element_type=F32),
+            lax.dot_general(gained[:, :width], scaled_low, TN, preferred_element_type=F32),
+            lax.dot_general(cots[row], lora_back, TN, preferred_element_type=F32),
         )
 
     def backward(row, gm):
         ends, select = row_data[row]
-        small, lora, zx, y, gained, _, states = fw[row]
+        small, lora, zx, y, _, _, states = fw[row]
         return mixer_backward(
-            ends, zx, small, gm, y, states, rks[row], conv_taps, state_taps, heads, chans
+            ends, zx, small, gm, y, states, rks[row], lora, normed[row], select, in_up,
+            conv_taps, state_taps, heads, chans,
         )
 
-    def in_gradients(row, dzx, mid):
-        return (
-            lax.dot_general(dzx, fw[row][1], TN, preferred_element_type=F32),
-            lax.dot_general(normed[row], mid, TN, preferred_element_type=F32),
-        )
-
-    def project_in(row, dzx, dsmall):
-        return (dot(dzx, zx_weight, NT) + dot(dsmall, small_weight, NT)).astype(BF16)
+    def project_in(ext):
+        return dot(ext, proj_weight, NT).astype(BF16)
 
     fw = [forward(0, normed[0]), None]
     came_cot = links.send_other(after(cotangent, fw[0][4]))
@@ -654,7 +688,7 @@
     back[1] = cotangents(1, cots[1], fw[1][4])
     stats = [jnp.stack([fw[r][5][0], back[r][2]]) for r in range(2)]
     stats = links.sum_stats(stats[0], stats[1])
-    sent_out, came_out = links.reduce_other(project_out(1, after(fw[1][4], back[1][2])))
+    sent_out, came_out = links.reduce_other(project_out(after(fw[1][4], back[1][2])))
     inv, rks = [], []
     for r in range(2):
         scale = lax.rsqrt(stats[r][0] / inner + EPS)
@@ -669,38 +703,34 @@
     grads_1 = out_gradients(1, back[1][0], fw[1][4], inv[1])
     grads_0 = out_gradients(0, back[0][0], fw[0][4], inv[0])
     down_total, up_total = [a + b for a, b in zip(grads_0, grads_1)]
-    out_chain = FactorSum(up_total.T, down_total)
-
-    gm_1 = after(out_chain.cover(back[1][1]), sent_out, down_total)
-    dzx_1, dbc_1, ddt_1 = backward(1, gm_1)
-    dzx_1 = out_chain.cover(after(dzx_1, came_out))
-    mid_1 = (dot(dzx_1, in_up, NT) * row_data[1][1]).astype(BF16)
-    sent_in, came_in = links.reduce_other(project_in(1, dzx_1, jnp.concatenate([dbc_1, ddt_1, mid_1], axis=1)))
-    in_1 = in_gradients(1, out_chain.cover(after(dzx_1, sent_in)), mid_1)
-    gm_0 = out_chain.cover(after(back[0][1], sent_in, *in_1))
-    dzx_0, dbc_0, ddt_0 = backward(0, gm_0)
-    dzx_0 = out_chain.cover(after(dzx_0, came_in))
-    mid_0 = (dot(dzx_0, in_up, NT) * row_data[0][1]).astype(BF16)
-    in_0 = in_gradients(0, dzx_0, out_chain.cover(mid_0))
-    in_up_total, in_down_total = [a + b for a, b in zip(in_1, in_0)]
+    out_up_sum = lax.psum(up_total.astype(BF16), ("dp", "tensor"))
+    out_down_sum = lax.psum(down_total.astype(BF16), "dp")
+
+    gm_1 = after(back[1][1], sent_out, down_total, up_total)
+    ext_1, *in_1 = backward(1, gm_1)
+    sent_in, came_in = links.reduce_other(project_in(after(ext_1, came_out)))
+    gm_0 = after(back[0][1], sent_in)
+    ext_0, *in_0 = backward(0, gm_0)
+    ext_0 = after(ext_0, came_in)
+    in_up_total, in_down_total = [(a + b).T for a, b in zip(in_1, in_0)]
     in_chain = FactorSum(in_down_total, in_up_total)
 
-    dzx_0 = after(in_chain.cover(dzx_0), in_up_total)
-    whole_in = project_in(0, dzx_0, jnp.concatenate([dbc_0, ddt_0, mid_0], axis=1))
-    gained_0 = after(in_chain.cover(fw[0][4]), whole_in)
-    whole_out = project_out(0, gained_0)
-    out_sum = links.reduce_own(in_chain.cover(whole_out), came_out)
+    whole_out = project_out(in_chain.cover(after(fw[0][4], ext_0)))
+    whole_in = project_in(in_chain.cover(after(ext_0, whole_out)))
+    out_sum = links.reduce_own(whole_out, in_chain.cover(after(came_out, whole_in)))
     output = (residual + links.mine(inv[0])[:, None] * out_sum).astype(BF16)
-    grad_normed = links.reduce_own(in_chain.cover(after(whole_in, output)), came_in)
+    grad_normed = links.reduce_own(whole_in, in_chain.cover(after(came_in, output)))
     scaled = grad_normed * norm_gain
     grad_tokens = (
         cotangent.astype(F32)
         + inv_rms * scaled
         - residual * inv_rms**3 * (jnp.sum(scaled * residual, axis=1, keepdims=True) / model)
     )
-    out_up_sum, out_down_sum = out_chain.finish()
+    grad_tokens = in_chain.cover(grad_tokens)
     in_down_sum, in_up_sum = in_chain.finish()
-    out_up_sum, in_up_sum = out_up_sum.T, in_up_sum.T
+    out_down_sum = after(out_down_sum, in_down_sum)
+    out_up_sum, out_down_sum = out_up_sum.T.astype(F32), out_down_sum.astype(F32)
+    in_up_sum = in_up_sum.T
     return (
         output,
         grad_tokens,

time: 451 us -> 601 us (1.33)
  waiting for transfers between devices: 42.9 us -> 228 us
  matrix products: 148 us -> 109 us
  Pallas kernels: 105 us -> 120 us
  local copies, waits for them, and re-layouts: 61.6 us -> 46.9 us
  between operations: 6.3 us -> 19.3 us
    psum x0 -> x2, waiting for transfers between devices: none -> 192 us  [the longest x1 121 us: on_device(): out_up_sum = lax.psum(up_total.astype(BF16), ('dp', 'tensor'))]
    dot_general x8 -> x4, matrix products: 31.9 us -> 8.5 us  [the longest x2 5.86 us: out_gradients(): lax.dot_general(cots[row], lora_back, TN, preferred_element_type=F32)]
    dot_general x22 -> x16, matrix products: 116 us -> 100 us  [dot(): return lax.dot_general(a, b, dims, preferred_element_type=F32)]
    pallas_call x2, Pallas kernels: 68.6 us -> 80.3 us  [mixer_backward(): pl.pallas_call(functools.partial(backward_kernel, count, seq), grid_spec=...]
    ppermute x20 -> x12, waiting for transfers between devices: 34.8 us -> 24.5 us  [the longest x6 13.3 us: gather_pieces(): lax.ppermute(sent, axis, pairs[a - 1])]
    slice x4, local copies, waits for them, and re-layouts: 11.3 us -> 5.17 us  [reduce_near(): second = self.near(whole[half:])]
    ppermute x20 -> x12, starting transfers between devices: 19.4 us -> 14.9 us  [the longest x6 7.68 us: gather_pieces(): lax.ppermute(sent, axis, pairs[a - 1])]
    unnamed x142 -> x114, local copies, waits for them, and re-layouts: 29.5 us -> 29.2 us
  transfers between devices with their start and end apart: 34 -> 28, of which waited for: 14 -> 13; matrix products, arithmetic and copies ran while one was open for 41% -> 24% of each run, Pallas kernels for 24% -> 20%
where the time goes in v3:
time: 601 us; the launch traced here: 593 us
  waiting for transfers between devices  228 us (38%)
  Pallas kernels  120 us (20%)
  matrix products  109 us (18%)
  local copies, waits for them, and re-layouts  46.9 us (8%)
  other arithmetic  46.8 us (8%)
  starting transfers between devices  23.1 us (4%)
  between operations  19.3 us (3%)
    psum x1, waiting for transfers between devices, on_device(): out_up_sum = lax.psum(up_total.astype(BF16), ('dp', 'tensor'))  121 us
    dot_general x16, matrix products, dot(): return lax.dot_general(a, b, dims, preferred_element_type=F32)  100 us
    pallas_call x2, Pallas kernels, mixer_backward(): pl.pallas_call(functools.partial(backward_kernel, count, seq), grid_spec=...  80.3 us
    psum x1, waiting for transfers between devices, on_device(): out_down_sum = lax.psum(down_total.astype(BF16), 'dp')  71.3 us
    pallas_call x2, Pallas kernels, mixer_forward(): pl.pallas_call(functools.partial(forward_kernel, count), grid_spec=pltpu....  39.4 us
    unnamed x114, local copies, waits for them, and re-layouts  29.2 us
    ppermute x6, waiting for transfers between devices, gather_pieces(): lax.ppermute(sent, axis, pairs[a - 1])  13.3 us
  transfers between devices with their start and end apart: 28, of which 13 were waited for; matrix products, arithmetic and copies ran while one was open for 24% of the time, Pallas kernels for 20%

profile of v3, /device:TPU:0, one launch (start us, length us, event | category | flops | bytes accessed | tf_op | source)
XLA Modules:
  0.0 592.7 jit_solution(17747133582082093603)
XLA Ops:
  10.1 3.5 fusion.2
  26.1 10.4 %copy.61 = bf16[256,8,2,1024]{3,1,2,0:T(8,128)(2,1)} copy(bf16[256,8,2,1024]{3,2,1,0:T(2,128)(2,1)} %bitcast.74) | data formatting | bytes 16777216
  43.3 4.6 fusion.17.bc_ref.dt_ref.bch_ref
  49.5 15.1 %convolution_add_fusion.1.z_ref.x_ref.xh_ref = f32[1024,2048]{1,0:T(8,128)} fusion(f32[1024,2048]{1,0:T(8,128)S(1)} %fusion.49, bf16[2048,2048]{1,0:T(8,128)(2,1)} %bitcast.75, bf16[512,2048]{1,0:T(8,128)(2,1)} %collective-permute-done, bf16[512,2048]{1,0:T(8,128)(2,1)} %fusion.2), kind=kOutput, calls=%fused_computation.21 | convolution fusion | flops 8600420352 | bytes 29360128 | tf_op jit(solution)/shard_map/dot_general | solution.py:397
  64.6 19.7 %mixer_forward.2 = (f32[1024,1024]{1,0:T(8,128)}, bf16[1024,1152]{1,0:T(8,128)(2,1)}, f32[8,1024]{1,0:T(8,128)}, bf16[8,128,1024]{2,1,0:T(8,128)(2,1)}) custom-call(s32[5]{0:T(128)} %pad_add_fusion.ends, f32[1024,2048]{1,0:T(8,128)} %convolution_add_fusion.1.z_ref.x_ref.xh_ref, f32[1024,2048]{1,0:T(8,128)} %convolution_add_fusion.1.z_ref.x_ref.xh_ref, ...), custom_call_target="tpu_custom_call" | custom-call | flops 1258291200 | bytes 16777216 | tf_op jit(solution)/shard_map/mixer_forward/pallas_call | solution.py:315
  93.3 6.4 %multiply_reduce_fusion.1 = (f32[1024]{0:T(1024)S(1)}, f32[1024,1024]{1,0:T(8,128)}) fusion(bf16[1024,1152]{1,0:T(8,128)(2,1)S(1)} %copy-done.33, f32[1024,1024]{1,0:T(8,128)S(1)} %fusion.50, bf16[1024,2048]{1,0:T(8,128)(2,1)S(1)} %constant_dynamic-update-slice_fusion, bf16[1024,2048]{1,0:T(8,128)(2,1)S(1)} %copy-done.45), kind=kOutput, calls=%fused_computation.19 | convolution fusion | flops 4299160576 | bytes 18878464 | tf_op jit(solution)/shard_map/dot_general | solution.py:397
  105.9 13.2 %convolution_add_fusion.z_ref.x_ref.xh_ref = f32[1024,2048]{1,0:T(8,128)} fusion(f32[1024,2048]{1,0:T(8,128)S(1)} %fusion.51, bf16[1024,2048]{1,0:T(8,128)(2,1)S(1)} %constant_dynamic-update-slice_fusion.2.nb_ref, bf16[2048,2048]{1,0:T(8,128)(2,1)} %bitcast.76), kind=kOutput, calls=%fused_computation.20 | convolution fusion | flops 8592031744 | bytes 29360128 | tf_op jit(solution)/shard_map/dot_general | solution.py:397
  119.1 19.7 %mixer_forward.3 = (f32[1024,1024]{1,0:T(8,128)}, bf16[1024,1152]{1,0:T(8,128)(2,1)}, f32[8,1024]{1,0:T(8,128)}, bf16[8,128,1024]{2,1,0:T(8,128)(2,1)}) custom-call(s32[5]{0:T(128)} %pad_add_fusion.1.ends, f32[1024,2048]{1,0:T(8,128)} %convolution_add_fusion.z_ref.x_ref.xh_ref, f32[1024,2048]{1,0:T(8,128)} %convolution_add_fusion.z_ref.x_ref.xh_ref, ...), custom_call_target="tpu_custom_call" | custom-call | flops 1258291200 | bytes 16777216 | tf_op jit(solution)/shard_map/mixer_forward/pallas_call | solution.py:315
  147.8 6.5 %multiply_reduce_fusion = (f32[1024]{0:T(1024)S(1)}, f32[1024,1024]{1,0:T(8,128)}) fusion(bf16[1024,1152]{1,0:T(8,128)(2,1)S(1)} %copy-done.36, f32[1024,1024]{1,0:T(8,128)S(1)} %fusion.52, bf16[1024,2048]{1,0:T(8,128)(2,1)S(1)} %constant_dynamic-update-slice_fusion.4, bf16[1024,2048]{1,0:T(8,128)(2,1)S(1)} %copy-done.46), kind=kOutput, calls=%fused_computation.18 | convolution fusion | flops 4299160576 | bytes 18878464 | tf_op jit(solution)/shard_map/dot_general | solution.py:397
  154.3 5.8 convolution_convert_fusion.3
  165.7 2.5 collective-permute-done.7
  174.5 3.2 fusion.20
  178.0 2.7 convolution_add_fusion.2
  180.7 40.3 %mixer_backward.2 = (bf16[1024,2560]{1,0:T(8,128)(2,1)}, f32[128,2048]{1,0:T(8,128)}, f32[128,2048]{1,0:T(8,128)}) custom-call(s32[5]{0:T(128)} %pad_add_fusion.1.ends, f32[1024,2048]{1,0:T(8,128)} %convolution_add_fusion.z_ref.x_ref.xh_ref, f32[1024,2048]{1,0:T(8,128)} %convolution_add_fusion.z_ref.x_ref.xh_ref, ...), custom_call_target="tpu_custom_call" | custom-call | flops 3145728000 | bytes 25165824 | tf_op jit(solution)/shard_map/mixer_backward/pallas_call | solution.py:359
  221.1 15.2 %convolution_convert_fusion.1 = bf16[1024,2048]{1,0:T(8,128)(2,1)S(1)} fusion(bf16[1024,2560]{1,0:T(8,128)(2,1)} %get-tuple-element.58, bf16[2048,128]{1,0:T(8,128)(2,1)S(1)} %copy-done.27, bf16[2048,128]{1,0:T(8,128)(2,1)S(1)} %copy-done.30, bf16[2048,256]{1,0:T(8,128)(2,1)} %param.25, bf16[2048,2048]{1,0:T(8,128)(2,1)} %bitcast.77), kind=kOutput, calls=%fused_computation.23 | convolution fusion | flops 10781458432 | bytes 19922944 | tf_op jit(solution)/shard_map/dot_general | solution.py:397
  236.5 4.1 collective-permute-done.10
  243.6 4.8 pad_maximum_fusion.2.nb_ref
  249.9 39.9 %mixer_backward.3 = (bf16[1024,2560]{1,0:T(8,128)(2,1)}, f32[128,2048]{1,0:T(8,128)}, f32[128,2048]{1,0:T(8,128)}) custom-call(s32[5]{0:T(128)} %pad_add_fusion.ends, f32[1024,2048]{1,0:T(8,128)} %convolution_add_fusion.1.z_ref.x_ref.xh_ref, f32[1024,2048]{1,0:T(8,128)} %convolution_add_fusion.1.z_ref.x_ref.xh_ref, ...), custom_call_target="tpu_custom_call" | custom-call | flops 3145728000 | bytes 25165824 | tf_op jit(solution)/shard_map/mixer_backward/pallas_call | solution.py:359
  292.9 9.1 %convolution_convert_fusion.2 = bf16[1024,2048]{1,0:T(8,128)(2,1)S(1)} fusion(bf16[1024,1152]{1,0:T(8,128)(2,1)S(1)} %copy-done.35, bf16[128,2048]{1,0:T(8,128)(2,1)S(1)} %bitcast.114, bf16[1024,2048]{1,0:T(8,128)(2,1)} %param.31), kind=kOutput, calls=%fused_computation.24 | convolution fusion | flops 4843372544 | bytes 11272192 | tf_op jit(solution)/shard_map/dot_general | solution.py:397
  306.1 15.6 %convolution_convert_fusion = bf16[1024,2048]{1,0:T(8,128)(2,1)} fusion(bf16[1024,2560]{1,0:T(8,128)(2,1)} %get-tuple-element.70, bf16[2048,128]{1,0:T(8,128)(2,1)} %copy.46, bf16[2048,128]{1,0:T(8,128)(2,1)} %copy-done.28, bf16[2048,256]{1,0:T(8,128)(2,1)} %param.25, bf16[2048,2048]{1,0:T(8,128)(2,1)S(1)} %bitcast.80), kind=kOutput, calls=%fused_computation.22 | convolution fusion | flops 10781458432 | bytes 19922944 | tf_op jit(solution)/shard_map/dot_general | solution.py:397
  325.8 3.3 slice.214
  329.2 5.3 collective-permute-done.16
  336.4 5.7 fusion.3
  342.3 2.6 collective-permute-start.18
  346.9 4.7 collective-permute-done.18
  354.1 4.3 fusion.6
  359.3 4.7 fusion.5
  369.1 3.4 collective-permute-done.21
  372.6 3.5 collective-permute-done.20
  378.7 6.3 %collective-permute-done.23 = bf16[1280,128]{0,1:T(8,128)(2,1)S(1)} collective-permute-done((bf16[1280,128]{0,1:T(8,128)(2,1)S(1)}, bf16[1280,128]{0,1:T(8,128)(2,1)S(1)}, u32[]{:S(2)}, u32[]{:S(2)}) %collective-permute-start.23) | collective-permute-done | bytes 327712 | tf_op jit(solution)/shard_map/ppermute | solution.py:552
  386.2 120.8 %all-reduce.8.cloned.1.call-done = bf16[8,16,2048]{2,1,0:T(8,128)(2,1)} async-done(((bf16[8,16,2048]{2,1,0:T(8,128)(2,1)}), bf16[8,16,2048]{2,1,0:T(8,128)(2,1)}) %all-reduce.8.cloned.1.call-update) | async-done | bytes 524304 | tf_op jit(solution)/shard_map/psum | solution.py:706
  509.1 71.3 %all-reduce.6.cloned.1.call-done = bf16[1024,128]{1,0:T(8,128)(2,1)} async-done(((bf16[1024,128]{1,0:T(8,128)(2,1)}), bf16[1024,128]{1,0:T(8,128)(2,1)}) %all-reduce.6.cloned.1.call-update) | async-done | bytes 262160 | tf_op jit(solution)/shard_map/psum | solution.py:707
  (256 shorter events, 95.0 us)
Async XLA Ops:
  7.3 499.7 %all-reduce.8.cloned.1.call-start = ((), (), s32[]{:S(2)}) async-start(), calls=%async_computation.1 | async-start | bytes 1048576 | tf_op jit(solution)/shard_map/psum | solution.py:706
  13.6 29.7 %collective-permute-start = (bf16[512,2048]{1,0:T(8,128)(2,1)}, bf16[512,2048]{1,0:T(8,128)(2,1)}, u32[]{:S(2)}, u32[]{:S(2)}) collective-permute-start(bf16[512,2048]{1,0:T(8,128)(2,1)} %fusion.2), channel_id=1, source_target_pairs={{0,1},{1,0},{2,3},{3,2},{4,5},{5,4},{6,7},{7,6},{8,9},{9,8},{10,11... | collective-permute-start | bytes 6291464 | tf_op jit(solution)/shard_map/ppermute | solution.py:430
  14.1 70.6 %collective-permute-start.2 = (bf16[512,2048]{1,0:T(8,128)(2,1)}, bf16[512,2048]{1,0:T(8,128)(2,1)}, u32[]{:S(2)}, u32[]{:S(2)}) collective-permute-start(bf16[512,2048]{1,0:T(8,128)(2,1)} %fusion.2), channel_id=1, source_target_pairs={{0,2},{1,3},{2,0},{3,1},{4,6},{5,7},{6,4},{7,5},{8,10},{9,11},{10,... | collective-permute-start | bytes 6291464 | tf_op jit(solution)/shard_map/ppermute | solution.py:427
  16.6 70.2 %collective-permute-start.1 = (bf16[512,2048]{1,0:T(8,128)(2,1)S(1)}, bf16[512,2048]{1,0:T(8,128)(2,1)}, u32[]{:S(2)}, u32[]{:S(2)}) collective-permute-start(bf16[512,2048]{1,0:T(8,128)(2,1)S(1)} %copy-done.10), channel_id=1, source_target_pairs={{0,1},{1,0},{2,3},{3,2},{4,5},{5,4},{6,7},{7,6},{8,9},{9,8},{10,11... | collective-permute-start | bytes 6291464 | tf_op jit(solution)/shard_map/ppermute | solution.py:430
  26.1 78.5 %copy-start.3 = (bf16[16,8,2,1024]{3,1,2,0:T(8,128)(2,1)}, bf16[16,8,2,1024]{3,1,2,0:T(8,128)(2,1)S(1)}, u32[]{:S(2)}) copy-start(bf16[16,8,2,1024]{3,1,2,0:T(8,128)(2,1)S(1)} %copy.62) | copy-start | bytes 1572868
  84.3 54.5 %collective-permute-start.4 = (bf16[512,2048]{1,0:T(8,128)(2,1)S(1)}, bf16[512,2048]{1,0:T(8,128)(2,1)}, u32[]{:S(2)}, u32[]{:S(2)}) collective-permute-start(bf16[512,2048]{1,0:T(8,128)(2,1)S(1)} %copy-done.10), channel_id=1, source_target_pairs={{0,2},{1,3},{2,0},{3,1},{4,6},{5,7},{6,4},{7,5},{8,10},{9,11},{10,... | collective-permute-start | bytes 6291464 | tf_op jit(solution)/shard_map/ppermute | solution.py:427
  84.6 15.1 %collective-permute-start.3 = (bf16[512,2048]{1,0:T(8,128)(2,1)}, bf16[512,2048]{1,0:T(8,128)(2,1)S(1)}, u32[]{:S(2)}, u32[]{:S(2)}) collective-permute-start(bf16[512,2048]{1,0:T(8,128)(2,1)} %collective-permute-done.2), channel_id=1, source_target_pairs={{0,1},{1,0},{2,3},{3,2},{4,5},{5,4},{6,7},{7,6},{8,9},{9,8},{10,11... | collective-permute-start | bytes 6291464 | tf_op jit(solution)/shard_map/ppermute | solution.py:430
  138.8 4.4 collective-permute-start.5
  160.2 8.1 %collective-permute-start.8 = (bf16[512,2048]{1,0:T(8,128)(2,1)S(1)}, bf16[512,2048]{1,0:T(8,128)(2,1)S(1)}, u32[]{:S(2)}, u32[]{:S(2)}) collective-permute-start(bf16[512,2048]{1,0:T(8,128)(2,1)S(1)} %slice.203), channel_id=1, source_target_pairs={{0,1},{1,0},{2,3},{3,2},{4,5},{5,4},{6,7},{7,6},{8,9},{9,8},{10,11... | collective-permute-start | bytes 6291464 | tf_op jit(solution)/shard_map/ppermute | solution.py:430
  162.2 2.3 collective-permute-start.6
  164.5 3.8 collective-permute-start.7
  169.1 51.9 %collective-permute-start.9 = (bf16[512,2048]{1,0:T(8,128)(2,1)S(1)}, bf16[512,2048]{1,0:T(8,128)(2,1)}, u32[]{:S(2)}, u32[]{:S(2)}) collective-permute-start(bf16[512,2048]{1,0:T(8,128)(2,1)S(1)} %add_convert_fusion.1), channel_id=1, source_target_pairs={{0,2},{1,3},{2,0},{3,1},{4,6},{5,7},{6,4},{7,5},{8,10},{9,11},{10,... | collective-permute-start | bytes 6291464 | tf_op jit(solution)/shard_map/ppermute | solution.py:427
  180.7 40.3 %copy-start.27 = (bf16[2048,128]{1,0:T(8,128)(2,1)S(1)}, bf16[2048,128]{1,0:T(8,128)(2,1)}, u32[]{:S(2)}) copy-start(bf16[2048,128]{1,0:T(8,128)(2,1)} %copy.46) | copy-start | bytes 1572868
  180.7 40.3 %copy-start.30 = (bf16[2048,128]{1,0:T(8,128)(2,1)S(1)}, bf16[2048,128]{1,0:T(8,128)(2,1)}, u32[]{:S(2)}) copy-start(bf16[2048,128]{1,0:T(8,128)(2,1)} %copy-done.28) | copy-start | bytes 1572868
  236.4 4.2 collective-permute-start.10
  242.8 49.4 %collective-permute-start.11 = (bf16[512,2048]{1,0:T(8,128)(2,1)}, bf16[512,2048]{1,0:T(8,128)(2,1)S(1)}, u32[]{:S(2)}, u32[]{:S(2)}) collective-permute-start(bf16[512,2048]{1,0:T(8,128)(2,1)} %add_convert_fusion), channel_id=1, source_target_pairs={{0,2},{1,3},{2,0},{3,1},{4,6},{5,7},{6,4},{7,5},{8,10},{9,11},{10,... | collective-permute-start | bytes 6291464 | tf_op jit(solution)/shard_map/ppermute | solution.py:427
  292.2 12.4 %collective-permute-start.13 = (bf16[1024,128]{0,1:T(8,128)(2,1)S(1)}, bf16[1024,128]{0,1:T(8,128)(2,1)S(1)}, u32[]{:S(2)}, u32[]{:S(2)}) collective-permute-start(bf16[1024,128]{0,1:T(8,128)(2,1)S(1)} %dynamic-slice_convert_fusion.1), channel_id=1, source_target_pairs={{0,1},{1,0},{2,3},{3,2},{4,5},{5,4},{6,7},{7,6},{8,9},{9,8},{10,11... | collective-permute-start | bytes 786440 | tf_op jit(solution)/shard_map/ppermute | solution.py:536
  304.6 31.7 %collective-permute-start.12 = (bf16[512,2048]{1,0:T(8,128)(2,1)}, bf16[512,2048]{1,0:T(8,128)(2,1)}, u32[]{:S(2)}, u32[]{:S(2)}) collective-permute-start(bf16[512,2048]{1,0:T(8,128)(2,1)} %slice.212), channel_id=1, source_target_pairs={{0,1},{1,0},{2,3},{3,2},{4,5},{5,4},{6,7},{7,6},{8,9},{9,8},{10,11... | collective-permute-start | bytes 6291464 | tf_op jit(solution)/shard_map/ppermute | solution.py:430
  304.8 16.9 %collective-permute-start.14 = (bf16[512,128]{0,1:T(8,128)(2,1)S(1)}, bf16[512,128]{0,1:T(8,128)(2,1)S(1)}, u32[]{:S(2)}, u32[]{:S(2)}) collective-permute-start(bf16[512,128]{0,1:T(8,128)(2,1)S(1)} %dynamic-slice_convert_fusion.2), channel_id=1, source_target_pairs={{0,2},{1,3},{2,0},{3,1},{4,6},{5,7},{6,4},{7,5},{8,10},{9,11},{10,... | collective-permute-start | bytes 393224 | tf_op jit(solution)/shard_map/ppermute | solution.py:536
  324.3 10.2 %collective-permute-start.16 = (bf16[1280,128]{0,1:T(8,128)(2,1)}, bf16[1280,128]{0,1:T(8,128)(2,1)}, u32[]{:S(2)}, u32[]{:S(2)}) collective-permute-start(bf16[1280,128]{0,1:T(8,128)(2,1)} %pad_maximum_fusion.12), channel_id=1, source_target_pairs={{0,4},{4,0},{8,12},{12,8},{16,20},{20,16},{24,28},{28,24},{1,5},{5... | collective-permute-start | bytes 983048 | tf_op jit(solution)/shard_map/ppermute | solution.py:536
  329.2 24.9 %collective-permute-start.15 = (bf16[512,2048]{1,0:T(8,128)(2,1)}, bf16[512,2048]{1,0:T(8,128)(2,1)}, u32[]{:S(2)}, u32[]{:S(2)}) collective-permute-start(bf16[512,2048]{1,0:T(8,128)(2,1)} %slice.214), channel_id=1, source_target_pairs={{0,1},{1,0},{2,3},{3,2},{4,5},{5,4},{6,7},{7,6},{8,9},{9,8},{10,11... | collective-permute-start | bytes 6291464 | tf_op jit(solution)/shard_map/ppermute | solution.py:430
  336.4 17.7 %copy-start.31 = (f32[2048]{0:T(1024)S(1)}, f32[2048]{0:T(1024)}, u32[]{:S(2)}) copy-start(f32[2048]{0:T(1024)} %param.23) | copy-start | bytes 24580
  342.3 9.3 %collective-permute-start.18 = (bf16[320,128]{0,1:T(8,128)(2,1)S(1)}, bf16[320,128]{0,1:T(8,128)(2,1)S(1)}, u32[]{:S(2)}, u32[]{:S(2)}) collective-permute-start(bf16[320,128]{0,1:T(8,128)(2,1)S(1)} %pad_maximum_fusion.17), channel_id=1, source_target_pairs={{0,16},{4,20},{8,24},{12,28},{16,0},{20,4},{24,8},{28,12},{1,17},{... | collective-permute-start | bytes 245768 | tf_op jit(solution)/shard_map/ppermute | solution.py:536
  345.1 7.1 %collective-permute-start.19 = (bf16[320,128]{0,1:T(8,128)(2,1)S(1)}, bf16[320,128]{0,1:T(8,128)(2,1)S(1)}, u32[]{:S(2)}, u32[]{:S(2)}) collective-permute-start(bf16[320,128]{0,1:T(8,128)(2,1)S(1)} %pad_maximum_fusion.18), channel_id=1, source_target_pairs={{0,24},{4,28},{8,16},{12,20},{16,8},{20,12},{24,0},{28,4},{1,25},{... | collective-permute-start | bytes 245768 | tf_op jit(solution)/shard_map/ppermute | solution.py:536
  346.6 6.3 %collective-permute-start.17 = (bf16[320,128]{0,1:T(8,128)(2,1)S(1)}, bf16[320,128]{0,1:T(8,128)(2,1)S(1)}, u32[]{:S(2)}, u32[]{:S(2)}) collective-permute-start(bf16[320,128]{0,1:T(8,128)(2,1)S(1)} %pad_maximum_fusion.16), channel_id=1, source_target_pairs={{0,8},{4,12},{8,0},{12,4},{16,24},{20,28},{24,16},{28,20},{1,9},{5... | collective-permute-start | bytes 245768 | tf_op jit(solution)/shard_map/ppermute | solution.py:536
  364.1 5.0 collective-permute-start.22
  365.8 6.8 %collective-permute-start.21 = (bf16[320,128]{0,1:T(8,128)(2,1)S(1)}, bf16[320,128]{0,1:T(8,128)(2,1)S(1)}, u32[]{:S(2)}, u32[]{:S(2)}) collective-permute-start(bf16[320,128]{0,1:T(8,128)(2,1)S(1)} %pad_maximum_fusion.19), channel_id=1, source_target_pairs={{0,16},{4,20},{8,24},{12,28},{16,0},{20,4},{24,8},{28,12},{1,17},{... | collective-permute-start | bytes 245768 | tf_op jit(solution)/shard_map/ppermute | solution.py:552
  368.1 7.9 %collective-permute-start.20 = (bf16[320,128]{0,1:T(8,128)(2,1)S(1)}, bf16[320,128]{0,1:T(8,128)(2,1)S(1)}, u32[]{:S(2)}, u32[]{:S(2)}) collective-permute-start(bf16[320,128]{0,1:T(8,128)(2,1)S(1)} %pad_maximum_fusion.19), channel_id=1, source_target_pairs={{0,24},{4,28},{8,16},{12,20},{16,8},{20,12},{24,0},{28,4},{1,25},{... | collective-permute-start | bytes 245768 | tf_op jit(solution)/shard_map/ppermute | solution.py:552
  376.3 8.7 %collective-permute-start.23 = (bf16[1280,128]{0,1:T(8,128)(2,1)S(1)}, bf16[1280,128]{0,1:T(8,128)(2,1)S(1)}, u32[]{:S(2)}, u32[]{:S(2)}) collective-permute-start(bf16[1280,128]{0,1:T(8,128)(2,1)S(1)} %concatenate.104), channel_id=1, source_target_pairs={{0,4},{4,0},{8,12},{12,8},{16,20},{20,16},{24,28},{28,24},{1,5},{5... | collective-permute-start | bytes 983048 | tf_op jit(solution)/shard_map/ppermute | solution.py:552
  377.9 202.4 %all-reduce.6.cloned.1.call-start = ((), (), s32[]{:S(2)}) async-start(), calls=%async_computation | async-start | bytes 524288 | tf_op jit(solution)/shard_map/psum | solution.py:707
  385.2 197.1 %collective-permute-start.24 = (bf16[512,128]{0,1:T(8,128)(2,1)S(1)}, bf16[512,128]{0,1:T(8,128)(2,1)S(1)}, u32[]{:S(2)}, u32[]{:S(2)}) collective-permute-start(bf16[512,128]{0,1:T(8,128)(2,1)S(1)} %pad_maximum_fusion.15), channel_id=1, source_target_pairs={{0,2},{1,3},{2,0},{3,1},{4,6},{5,7},{6,4},{7,5},{8,10},{9,11},{10,... | collective-permute-start | bytes 393224 | tf_op jit(solution)/shard_map/ppermute | solution.py:552
  582.3 2.2 collective-permute-start.25
  (50 other events, 326.8 us)
Sparse Core Ops, SparseCore 0:
  378.1 128.8 all-reduce.7
  510.3 70.0 all-reduce.5

commit v4 on v3

--- a/solution.py
+++ b/solution.py
@@ -77,12 +77,21 @@
     return total
 
 
+def masked_sum(mask, v):
+    hi, mid, low = split3(v)
+    twice = jnp.concatenate([mask, mask], axis=1)
+    return mm(twice, jnp.concatenate([hi, mid], axis=0)) + mm(mask, low)
+
+
+def halves(v):
+    return jnp.concatenate(split2(v), axis=1)
+
+
 def step_terms(dt_raw, bias, rate, low_mask):
     raw = dt_raw + bias
     dt = jnp.maximum(raw, 0.0) + jnp.log1p(jnp.exp(-jnp.abs(raw)))
     decay = dt * rate
-    cum = sum(mm(low_mask, part) for part in split3(decay))
-    return raw, dt, cum
+    return raw, dt, masked_sum(low_mask, decay)
 
 
 def lane_pair(low, value, h):
@@ -268,11 +277,13 @@
         ds_new = (keep * jnp.exp(c_last)) * ds + mm(c_turn, dyc)
         dstate[:, cut] = ds_new
         both = jnp.sum(ds_new * st.astype(F32), axis=0, keepdims=True)
-        both = jnp.broadcast_to(both, (8, 128))
-        d_end = d_end + sum(mm(part, pick) for part in split2(both))
+        both = jnp.broadcast_to(both, (16, 128))
         v = dyb.astype(F32) * y - xb.astype(F32) * dxt
-        d_cum = d_cum + sum(mm(part, pick) for part in split2(v))
-        d_dt = d_dt + sum(mm(part, pick) for part in split2(dxt * xc))
+        stacked = jnp.concatenate([halves(v), halves(dxt * xc), halves(both)], axis=0)
+        sums = mm(stacked, jnp.concatenate([pick, pick], axis=0))
+        d_cum = d_cum + sums[:L]
+        d_dt = d_dt + sums[L : 2 * L]
+        d_end = d_end + sums[2 * L : 2 * L + 8]
         dpre = (skip * dyt + dt_both * dxt) * (sg + xc * (1.0 - sg))
         ext = jnp.concatenate([dpre, dnext[:, cut]], axis=0)
         dzx_ref[:, slice(width + p * 128, width + p * 128 + 128)] = conv_back(ext, taps, ok).astype(BF16)
@@ -290,7 +301,7 @@
         dbnext[:, cut] = dpre[:HALO]
     d_cum = d_cum + jnp.where(sub == L - 1, ends_row[0:1, :], 0.0)
     ends_row[...] = d_end
-    d_decay = sum(mm(up_mask, part) for part in split3(d_cum))
+    d_decay = masked_sum(up_mask, d_cum)
     d_raw = (d_dt + head_ref[1:2] * d_decay) * sigmoid(raw)
     dzx_ref[:, 2 * width + 256 : 2 * width + 384] = d_raw.astype(BF16)
     mid = mm(dzx_ref[:, : 2 * width], up_ref[...], NT) * sel_ref[...]
@@ -565,17 +576,20 @@
 
 
 class FactorSum:
-    def __init__(self, shared, split):
+    def __init__(self, shared, split, summed):
         self.near, self.far = exchange_steps("tensor", False), exchange_steps("dp", True)
-        self.arrays, self.split, self.done = [shared], split, 0
+        self.arrays, self.split, self.parked, self.done = [shared, summed], split, None, 0
 
     def hop(self):
         near, far = len(self.near), len(self.far)
+        if self.done < 2 * (near + far):
+            self.move(near, far)
+
+    def move(self, near, far):
         at, total = self.done, 2 * (near + far)
-        if at == total:
-            return
         if at == near:
-            self.arrays = self.arrays + [self.split]
+            self.parked = self.arrays[1].astype(BF16)
+            self.arrays = [self.arrays[0], self.split]
         if at == near + far:
             self.arrays = [v.astype(BF16) for v in self.arrays]
         steps = self.near + self.far
@@ -586,7 +600,7 @@
         self.done += 1
         if self.done == near + 2 * far:
             self.split = self.arrays[1]
-            self.arrays = self.arrays[:1]
+            self.arrays = [self.arrays[0], self.parked]
 
     def cover(self, v):
         v, *self.arrays = lax.optimization_barrier((v, *self.arrays))
@@ -596,7 +610,7 @@
     def finish(self):
         while self.done < 2 * (len(self.near) + len(self.far)):
             self.hop()
-        return self.arrays[0].astype(F32), self.split.astype(F32)
+        return self.arrays[0].astype(F32), self.split.astype(F32), self.arrays[1].astype(F32)
 
 
 def on_device(
@@ -640,7 +654,8 @@
     residual = tokens.astype(F32)
     inv_rms = lax.rsqrt(jnp.mean(residual * residual, axis=1, keepdims=True) + EPS)
     normed_here = (residual * inv_rms * norm_gain).astype(BF16)
-    normed = [links.gather_own(normed_here), links.gather_other(links.send_other(normed_here))]
+    came_normed = links.send_other(normed_here)
+    normed = [lax.optimization_barrier(links.gather_own(normed_here)), None]
     cots = [links.gather_own(cotangent), None]
 
     def forward(row, nb):
@@ -682,8 +697,10 @@
 
     fw = [forward(0, normed[0]), None]
     came_cot = links.send_other(after(cotangent, fw[0][4]))
-    back = [cotangents(0, after(cots[0], fw[0][4]), fw[0][4]), None]
-    fw[1] = forward(1, after(normed[1], back[0][1]))
+    cots[0] = after(cots[0], fw[0][4])
+    back = [cotangents(0, cots[0], fw[0][4]), None]
+    normed[1] = after(links.gather_other(after(came_normed, fw[0][4])), back[0][1])
+    fw[1] = forward(1, normed[1])
     cots[1] = links.gather_other(after(came_cot, fw[1][4]))
     back[1] = cotangents(1, cots[1], fw[1][4])
     stats = [jnp.stack([fw[r][5][0], back[r][2]]) for r in range(2)]
@@ -703,17 +720,16 @@
     grads_1 = out_gradients(1, back[1][0], fw[1][4], inv[1])
     grads_0 = out_gradients(0, back[0][0], fw[0][4], inv[0])
     down_total, up_total = [a + b for a, b in zip(grads_0, grads_1)]
-    out_up_sum = lax.psum(up_total.astype(BF16), ("dp", "tensor"))
-    out_down_sum = lax.psum(down_total.astype(BF16), "dp")
+    up_sum, out_down_sum = lax.psum((up_total.astype(BF16), down_total.astype(BF16)), "dp")
 
     gm_1 = after(back[1][1], sent_out, down_total, up_total)
     ext_1, *in_1 = backward(1, gm_1)
     sent_in, came_in = links.reduce_other(project_in(after(ext_1, came_out)))
     gm_0 = after(back[0][1], sent_in)
     ext_0, *in_0 = backward(0, gm_0)
-    ext_0 = after(ext_0, came_in)
+    ext_0, up_sum, out_down_sum = lax.optimization_barrier((after(ext_0, came_in), up_sum, out_down_sum))
     in_up_total, in_down_total = [(a + b).T for a, b in zip(in_1, in_0)]
-    in_chain = FactorSum(in_down_total, in_up_total)
+    in_chain = FactorSum(in_down_total, in_up_total, up_sum.astype(F32))
 
     whole_out = project_out(in_chain.cover(after(fw[0][4], ext_0)))
     whole_in = project_in(in_chain.cover(after(ext_0, whole_out)))
@@ -721,15 +737,10 @@
     output = (residual + links.mine(inv[0])[:, None] * out_sum).astype(BF16)
     grad_normed = links.reduce_own(whole_in, in_chain.cover(after(came_in, output)))
     scaled = grad_normed * norm_gain
-    grad_tokens = (
-        cotangent.astype(F32)
-        + inv_rms * scaled
-        - residual * inv_rms**3 * (jnp.sum(scaled * residual, axis=1, keepdims=True) / model)
-    )
-    grad_tokens = in_chain.cover(grad_tokens)
-    in_down_sum, in_up_sum = in_chain.finish()
-    out_down_sum = after(out_down_sum, in_down_sum)
-    out_up_sum, out_down_sum = out_up_sum.T.astype(F32), out_down_sum.astype(F32)
+    inner_sum = jnp.sum(scaled * residual, axis=1, keepdims=True) / model
+    grad_tokens = cotangent.astype(F32) + inv_rms * scaled - residual * inv_rms**3 * inner_sum
+    in_down_sum, in_up_sum, out_up_sum = in_chain.finish()
+    out_up_sum, out_down_sum = out_up_sum.T, out_down_sum.astype(F32)
     in_up_sum = in_up_sum.T
     return (
         output,

time: 601 us -> 425 us (0.71)
  the two profiles are of different devices: /device:TPU:0 before, /device:TPU:9 now
where the time goes in v4:
time: 425 us; the launch traced here: 417 us
  Pallas kernels  114 us (27%)
  matrix products  98.8 us (23%)
  waiting for transfers between devices  70 us (16%)
  other arithmetic  51.8 us (12%)
  local copies, waits for them, and re-layouts  38.3 us (9%)
  starting transfers between devices  23.8 us (6%)
  between operations  19.4 us (5%)
    dot_general x16, matrix products, dot(): return lax.dot_general(a, b, dims, preferred_element_type=F32)  93.6 us
    pallas_call x2, Pallas kernels, mixer_backward(): pl.pallas_call(functools.partial(backward_kernel, count, seq), grid_spec=...  74.9 us
    pallas_call x2, Pallas kernels, mixer_forward(): pl.pallas_call(functools.partial(forward_kernel, count), grid_spec=pltpu....  39.5 us
    psum x1, waiting for transfers between devices, on_device(): lax.psum((up_total.astype(BF16), down_total.astype(BF16)), 'dp')  29.1 us
    unnamed x114, local copies, waits for them, and re-layouts  21.7 us
    ppermute x6, waiting for transfers between devices, gather_pieces(): lax.ppermute(sent, axis, pairs[a - 1])  14.8 us
    ppermute x6, waiting for transfers between devices, scatter_sum(): came.append(lax.ppermute(sent.astype(BF16), axis, pairs[a - 1]))  9.22 us
    ppermute x5, waiting for transfers between devices, far(): return lax.ppermute(v, 'tensor', self.across)  8.74 us
  transfers between devices with their start and end apart: 27, of which 13 were waited for; matrix products, arithmetic and copies ran while one was open for 31% of the time, Pallas kernels for 27%

profile of v4, /device:TPU:9, one launch (start us, length us, event | category | flops | bytes accessed | tf_op | source)
XLA Modules:
  0.0 416.5 jit_solution(11572390927234304238)
XLA Ops:
  10.1 3.5 fusion.2
  25.0 10.4 %copy.69 = bf16[256,8,2,1024]{3,1,2,0:T(8,128)(2,1)} copy(bf16[256,8,2,1024]{3,2,1,0:T(2,128)(2,1)} %bitcast.76) | data formatting | bytes 16777216
  40.8 2.6 pad_maximum_fusion.2.nb_ref
  43.5 2.3 fusion.17.bc_ref.dt_ref.bch_ref
  47.3 13.7 %convolution_add_fusion.1.z_ref.x_ref.xh_ref = f32[1024,2048]{1,0:T(8,128)} fusion(f32[1024,2048]{1,0:T(8,128)S(1)} %fusion.51, bf16[1024,2048]{1,0:T(8,128)(2,1)S(1)} %pad_maximum_fusion.2.nb_ref, bf16[2048,2048]{1,0:T(8,128)(2,1)} %bitcast.77), kind=kOutput, calls=%fused_computation.23 | convolution fusion | flops 8592031744 | bytes 29360128 | tf_op jit(solution)/shard_map/dot_general | solution.py:408
  61.0 19.7 %mixer_forward.2 = (f32[1024,1024]{1,0:T(8,128)}, bf16[1024,1152]{1,0:T(8,128)(2,1)}, f32[8,1024]{1,0:T(8,128)}, bf16[8,128,1024]{2,1,0:T(8,128)(2,1)}) custom-call(s32[5]{0:T(128)} %pad_add_fusion.ends, f32[1024,2048]{1,0:T(8,128)} %convolution_add_fusion.1.z_ref.x_ref.xh_ref, f32[1024,2048]{1,0:T(8,128)} %convolution_add_fusion.1.z_ref.x_ref.xh_ref, ...), custom_call_target="tpu_custom_call" | custom-call | flops 1258291200 | bytes 16777216 | tf_op jit(solution)/shard_map/mixer_forward/pallas_call | solution.py:326
  87.6 6.4 %multiply_reduce_fusion.1 = (f32[1024]{0:T(1024)S(1)}, f32[1024,1024]{1,0:T(8,128)}) fusion(bf16[1024,1152]{1,0:T(8,128)(2,1)S(1)} %copy-done.33, f32[1024,1024]{1,0:T(8,128)S(1)} %fusion.52, bf16[1024,2048]{1,0:T(8,128)(2,1)S(1)} %pad_maximum_fusion.3, bf16[1024,2048]{1,0:T(8,128)(2,1)S(1)} %copy-done.44), kind=kOutput, calls=%fused_computation.22 | convolution fusion | flops 4299160576 | bytes 18878464 | tf_op jit(solution)/shard_map/dot_general | solution.py:408
  96.4 2.3 fusion.16.bc_ref.dt_ref.bch_ref
  101.2 8.8 %fusion.53 = f32[1024,2048]{1,0:T(8,128)S(1)} fusion(bf16[1024,2048]{1,0:T(8,128)(2,1)S(1)} %pad_maximum_fusion.4.nb_ref, bf16[2048,2048]{1,0:T(8,128)(2,1)S(1)} %bitcast.82), kind=kOutput, calls=%fused_computation.186 | convolution fusion | flops 8589934592 | bytes 20971520 | tf_op jit(solution)/shard_map/dot_general | solution.py:408
  110.0 4.6 %convolution_add_fusion.z_ref.x_ref.xh_ref = f32[1024,2048]{1,0:T(8,128)} fusion(f32[1024,2048]{1,0:T(8,128)S(1)} %fusion.53, bf16[1024,128]{1,0:T(8,128)(2,1)S(1)} %fusion.19.lora_ref, bf16[128,2048]{1,0:T(8,128)(2,1)S(1)} %bitcast.73), kind=kOutput, calls=%fused_computation.7 | convolution fusion | flops 538968064 | bytes 17563648 | tf_op jit(solution)/shard_map/dot_general | solution.py:408
  114.6 19.8 %mixer_forward.3 = (f32[1024,1024]{1,0:T(8,128)}, bf16[1024,1152]{1,0:T(8,128)(2,1)}, f32[8,1024]{1,0:T(8,128)}, bf16[8,128,1024]{2,1,0:T(8,128)(2,1)}) custom-call(s32[5]{0:T(128)} %pad_add_fusion.1.ends, f32[1024,2048]{1,0:T(8,128)} %convolution_add_fusion.z_ref.x_ref.xh_ref, f32[1024,2048]{1,0:T(8,128)} %convolution_add_fusion.z_ref.x_ref.xh_ref, ...), custom_call_target="tpu_custom_call" | custom-call | flops 1258291200 | bytes 16777216 | tf_op jit(solution)/shard_map/mixer_forward/pallas_call | solution.py:326
  141.9 6.3 %multiply_reduce_fusion = (f32[1024]{0:T(1024)S(1)}, f32[1024,1024]{1,0:T(8,128)}) fusion(bf16[1024,1152]{1,0:T(8,128)(2,1)S(1)} %copy-done.35, f32[1024,1024]{1,0:T(8,128)S(1)} %fusion.54, bf16[1024,2048]{1,0:T(8,128)(2,1)S(1)} %constant_dynamic-update-slice_fusion, bf16[1024,2048]{1,0:T(8,128)(2,1)S(1)} %copy-done.45), kind=kOutput, calls=%fused_computation.21 | convolution fusion | flops 4299160576 | bytes 18878464 | tf_op jit(solution)/shard_map/dot_general | solution.py:408
  148.2 5.8 %convolution_convert_fusion.3 = bf16[1024,2048]{1,0:T(8,128)(2,1)S(1)} fusion(bf16[1024,1152]{1,0:T(8,128)(2,1)S(1)} %copy-done.35, bf16[128,2048]{1,0:T(8,128)(2,1)S(1)} %bitcast.118, bf16[1024,2048]{1,0:T(8,128)(2,1)S(1)} %copy-done.45), kind=kOutput, calls=%fused_computation.27 | convolution fusion | flops 4843372544 | bytes 11272192 | tf_op jit(solution)/shard_map/dot_general | solution.py:408
  158.8 2.4 collective-permute-done.7
  168.9 37.6 %mixer_backward.2 = (bf16[1024,2560]{1,0:T(8,128)(2,1)}, f32[128,2048]{1,0:T(8,128)}, f32[128,2048]{1,0:T(8,128)}) custom-call(s32[5]{0:T(128)} %pad_add_fusion.1.ends, f32[1024,2048]{1,0:T(8,128)} %convolution_add_fusion.z_ref.x_ref.xh_ref, f32[1024,2048]{1,0:T(8,128)} %convolution_add_fusion.z_ref.x_ref.xh_ref, ...), custom_call_target="tpu_custom_call" | custom-call | flops 3145728000 | bytes 25165824 | tf_op jit(solution)/shard_map/mixer_backward/pallas_call | solution.py:370
  208.0 15.2 %convolution_convert_fusion.1 = bf16[1024,2048]{1,0:T(8,128)(2,1)S(1)} fusion(bf16[1024,2560]{1,0:T(8,128)(2,1)} %get-tuple-element.63, bf16[2048,128]{1,0:T(8,128)(2,1)S(1)} %copy-done.25, bf16[2048,128]{1,0:T(8,128)(2,1)S(1)} %copy-done.29, bf16[2048,256]{1,0:T(8,128)(2,1)} %param.25, bf16[2048,2048]{1,0:T(8,128)(2,1)} %bitcast.78), kind=kOutput, calls=%fused_computation.25 | convolution fusion | flops 10781458432 | bytes 19922944 | tf_op jit(solution)/shard_map/dot_general | solution.py:408
  225.7 3.8 collective-permute-done.10
  233.2 37.3 %mixer_backward.3 = (bf16[1024,2560]{1,0:T(8,128)(2,1)}, f32[128,2048]{1,0:T(8,128)}, f32[128,2048]{1,0:T(8,128)}) custom-call(s32[5]{0:T(128)} %pad_add_fusion.ends, f32[1024,2048]{1,0:T(8,128)} %convolution_add_fusion.1.z_ref.x_ref.xh_ref, f32[1024,2048]{1,0:T(8,128)} %convolution_add_fusion.1.z_ref.x_ref.xh_ref, ...), custom_call_target="tpu_custom_call" | custom-call | flops 3145728000 | bytes 25165824 | tf_op jit(solution)/shard_map/mixer_backward/pallas_call | solution.py:370
  273.8 4.9 %collective-permute-done.11 = bf16[512,2048]{1,0:T(8,128)(2,1)S(1)} collective-permute-done((bf16[512,2048]{1,0:T(8,128)(2,1)}, bf16[512,2048]{1,0:T(8,128)(2,1)S(1)}, u32[]{:S(2)}, u32[]{:S(2)}) %collective-permute-start.11) | collective-permute-done | bytes 2097184 | tf_op jit(solution)/shard_map/ppermute | solution.py:438
  278.7 29.1 %all-reduce.6.cloned.1.call-done = (bf16[2048,128]{0,1:T(8,128)(2,1)}, bf16[1024,128]{1,0:T(8,128)(2,1)}) async-done(((bf16[2048,128]{0,1:T(8,128)(2,1)}, bf16[1024,128]{1,0:T(8,128)(2,1)}), (bf16[2048,128]{0,1:T(8,128)(2,1)}, bf16[1024,128]{1,0:T(8,128)(2,1)})) %all-reduce.6.cloned.1.call-update) | async-done | bytes 786448 | tf_op jit(solution)/shard_map/psum | solution.py:723
  310.1 2.3 collective-permute-start.13
  312.4 8.2 %convolution_convert_fusion.2 = bf16[1024,2048]{1,0:T(8,128)(2,1)S(1)} fusion(bf16[1024,1152]{1,0:T(8,128)(2,1)} %get-tuple-element.74, bf16[128,2048]{1,0:T(8,128)(2,1)} %bitcast.115, bf16[1024,2048]{1,0:T(8,128)(2,1)} %param.31), kind=kOutput, calls=%fused_computation.26 | convolution fusion | flops 4843372544 | bytes 11272192 | tf_op jit(solution)/shard_map/dot_general | solution.py:408
  325.5 15.0 %convolution_convert_fusion = bf16[1024,2048]{1,0:T(8,128)(2,1)} fusion(bf16[1024,2560]{1,0:T(8,128)(2,1)S(1)} %bitcast.114, bf16[2048,128]{1,0:T(8,128)(2,1)S(1)} %copy-done.26, bf16[2048,128]{1,0:T(8,128)(2,1)S(1)} %copy-done.30, bf16[2048,256]{1,0:T(8,128)(2,1)S(1)} %copy-done.48, bf16[2048,2048]{1,0:T(8,128)(2,1)} %bitcast.79), kind=kOutput, calls=%fused_computation.24 | convolution fusion | flops 10781458432 | bytes 19922944 | tf_op jit(solution)/shard_map/dot_general | solution.py:408
  342.5 7.9 %collective-permute-done.16 = bf16[1280,128]{0,1:T(8,128)(2,1)} collective-permute-done((bf16[1280,128]{0,1:T(8,128)(2,1)}, bf16[1280,128]{0,1:T(8,128)(2,1)}, u32[]{:S(2)}, u32[]{:S(2)}) %collective-permute-start.16) | collective-permute-done | bytes 327712 | tf_op jit(solution)/shard_map/ppermute | solution.py:547
  352.3 6.3 %fusion.3 = bf16[512,2048]{1,0:T(8,128)(2,1)} fusion(bf16[512,2048]{1,0:T(8,128)(2,1)S(1)} %copy-done.2, bf16[512,2048]{1,0:T(8,128)(2,1)} %collective-permute-done.9, bf16[512,2048]{1,0:T(8,128)(2,1)} %collective-permute-done.12, bf16[1024,2048]{1,0:T(8,128)(2,1)} %copy-done.13, f32[512]{0:T(512)S(1)} %bitcast.103), kind=kLoop, calls=%fused_computation.11 | loop fusion | flops 9437184 | bytes 10487808 | tf_op jit(solution)/shard_map/convert_element_type | solution.py:737
  362.8 3.2 slice.250
  365.9 2.3 collective-permute-start.15
  376.4 5.9 %collective-permute-done.20 = bf16[320,128]{0,1:T(8,128)(2,1)S(1)} collective-permute-done((bf16[320,128]{0,1:T(8,128)(2,1)S(1)}, bf16[320,128]{0,1:T(8,128)(2,1)S(1)}, u32[]{:S(2)}, u32[]{:S(2)}) %collective-permute-start.20) | collective-permute-done | bytes 81952 | tf_op jit(solution)/shard_map/ppermute | solution.py:563
  384.6 6.1 %collective-permute-done.23 = bf16[1280,128]{0,1:T(8,128)(2,1)S(1)} collective-permute-done((bf16[1280,128]{0,1:T(8,128)(2,1)S(1)}, bf16[1280,128]{0,1:T(8,128)(2,1)S(1)}, u32[]{:S(2)}, u32[]{:S(2)}) %collective-permute-start.23) | collective-permute-done | bytes 327712 | tf_op jit(solution)/shard_map/ppermute | solution.py:563
  394.4 4.3 %fusion.6 = f32[512]{0:T(512)S(1)} fusion(bf16[512,2048]{1,0:T(8,128)(2,1)S(1)} %copy-done.2, bf16[512,2048]{1,0:T(8,128)(2,1)} %copy-done.11, bf16[512,2048]{1,0:T(8,128)(2,1)} %collective-permute-done.15, f32[2048]{0:T(1024)S(1)} %copy-done.31, bf16[1024,2048]{1,0:T(8,128)(2,1)} %convolution_convert_fusion), kind=kLoop, calls=%fused_computation.14 | loop fusion | flops 9436672 | bytes 8398848 | tf_op jit(solution)/shard_map/reduce_sum | solution.py:740
  399.8 2.5 collective-permute-start.25
  402.3 4.7 %fusion.5 = f32[512,2048]{1,0:T(8,128)} fusion(bf16[512,2048]{1,0:T(8,128)(2,1)S(1)} %copy-done.2, bf16[512,2048]{1,0:T(8,128)(2,1)S(1)} %copy-done.10, bf16[512,2048]{1,0:T(8,128)(2,1)S(1)} %copy-done.12, bf16[512,2048]{1,0:T(8,128)(2,1)} %collective-permute-done.15, f32[512]{0:T(512)S(1)} %broadcast_multiply_fusion, f32[512]{0:T(512)S(1)} %copy-done.38, ...), kind=kLoop, calls=%fused_computation.13 | loop fusion | flops 13631488 | bytes 14694400 | tf_op jit(solution)/shard_map/sub | solution.py:741
  (260 shorter events, 92.1 us)
Async XLA Ops:
  7.3 300.5 %all-reduce.6.cloned.1.call-start = ((), (), s32[]{:S(2)}) async-start(), calls=%async_computation | async-start | bytes 1572864 | tf_op jit(solution)/shard_map/psum | solution.py:723
  13.6 27.2 %collective-permute-start = (bf16[512,2048]{1,0:T(8,128)(2,1)}, bf16[512,2048]{1,0:T(8,128)(2,1)}, u32[]{:S(2)}, u32[]{:S(2)}) collective-permute-start(bf16[512,2048]{1,0:T(8,128)(2,1)} %fusion.2), channel_id=1, source_target_pairs={{0,1},{1,0},{2,3},{3,2},{4,5},{5,4},{6,7},{7,6},{8,9},{9,8},{10,11... | collective-permute-start | bytes 6291464 | tf_op jit(solution)/shard_map/ppermute | solution.py:441
  14.3 66.4 %collective-permute-start.2 = (bf16[512,2048]{1,0:T(8,128)(2,1)}, bf16[512,2048]{1,0:T(8,128)(2,1)}, u32[]{:S(2)}, u32[]{:S(2)}) collective-permute-start(bf16[512,2048]{1,0:T(8,128)(2,1)} %fusion.2), channel_id=1, source_target_pairs={{0,2},{1,3},{2,0},{3,1},{4,6},{5,7},{6,4},{7,5},{8,10},{9,11},{10,... | collective-permute-start | bytes 6291464 | tf_op jit(solution)/shard_map/ppermute | solution.py:438
  15.5 65.5 %collective-permute-start.1 = (bf16[512,2048]{1,0:T(8,128)(2,1)S(1)}, bf16[512,2048]{1,0:T(8,128)(2,1)}, u32[]{:S(2)}, u32[]{:S(2)}) collective-permute-start(bf16[512,2048]{1,0:T(8,128)(2,1)S(1)} %copy-done.9), channel_id=1, source_target_pairs={{0,1},{1,0},{2,3},{3,2},{4,5},{5,4},{6,7},{7,6},{8,9},{9,8},{10,11... | collective-permute-start | bytes 6291464 | tf_op jit(solution)/shard_map/ppermute | solution.py:441
  25.0 85.0 %copy-start.7 = (bf16[16,8,2,1024]{3,1,2,0:T(8,128)(2,1)}, bf16[16,8,2,1024]{3,1,2,0:T(8,128)(2,1)S(1)}, u32[]{:S(2)}) copy-start(bf16[16,8,2,1024]{3,1,2,0:T(8,128)(2,1)S(1)} %copy.70) | copy-start | bytes 1572868
  80.7 13.3 %collective-permute-start.3 = (bf16[512,2048]{1,0:T(8,128)(2,1)}, bf16[512,2048]{1,0:T(8,128)(2,1)S(1)}, u32[]{:S(2)}, u32[]{:S(2)}) collective-permute-start(bf16[512,2048]{1,0:T(8,128)(2,1)} %collective-permute-done.2), channel_id=1, source_target_pairs={{0,1},{1,0},{2,3},{3,2},{4,5},{5,4},{6,7},{7,6},{8,9},{9,8},{10,11... | collective-permute-start | bytes 6291464 | tf_op jit(solution)/shard_map/ppermute | solution.py:441
  83.2 51.2 %collective-permute-start.4 = (bf16[512,2048]{1,0:T(8,128)(2,1)S(1)}, bf16[512,2048]{1,0:T(8,128)(2,1)}, u32[]{:S(2)}, u32[]{:S(2)}) collective-permute-start(bf16[512,2048]{1,0:T(8,128)(2,1)S(1)} %copy-done.9), channel_id=1, source_target_pairs={{0,2},{1,3},{2,0},{3,1},{4,6},{5,7},{6,4},{7,5},{8,10},{9,11},{10,... | collective-permute-start | bytes 6291464 | tf_op jit(solution)/shard_map/ppermute | solution.py:438
  134.4 4.4 %collective-permute-start.5 = (bf16[512,2048]{1,0:T(8,128)(2,1)}, bf16[512,2048]{1,0:T(8,128)(2,1)S(1)}, u32[]{:S(2)}, u32[]{:S(2)}) collective-permute-start(bf16[512,2048]{1,0:T(8,128)(2,1)} %collective-permute-done.4), channel_id=1, source_target_pairs={{0,1},{1,0},{2,3},{3,2},{4,5},{5,4},{6,7},{7,6},{8,9},{9,8},{10,11... | collective-permute-start | bytes 6291464 | tf_op jit(solution)/shard_map/ppermute | solution.py:441
  154.2 7.0 %collective-permute-start.8 = (bf16[512,2048]{1,0:T(8,128)(2,1)S(1)}, bf16[512,2048]{1,0:T(8,128)(2,1)S(1)}, u32[]{:S(2)}, u32[]{:S(2)}) collective-permute-start(bf16[512,2048]{1,0:T(8,128)(2,1)S(1)} %slice.235), channel_id=1, source_target_pairs={{0,1},{1,0},{2,3},{3,2},{4,5},{5,4},{6,7},{7,6},{8,9},{9,8},{10,11... | collective-permute-start | bytes 6291464 | tf_op jit(solution)/shard_map/ppermute | solution.py:441
  156.1 2.4 collective-permute-start.6
  158.5 2.7 collective-permute-start.7
  162.0 46.0 %collective-permute-start.9 = (bf16[512,2048]{1,0:T(8,128)(2,1)S(1)}, bf16[512,2048]{1,0:T(8,128)(2,1)}, u32[]{:S(2)}, u32[]{:S(2)}) collective-permute-start(bf16[512,2048]{1,0:T(8,128)(2,1)S(1)} %add_convert_fusion.1), channel_id=1, source_target_pairs={{0,2},{1,3},{2,0},{3,1},{4,6},{5,7},{6,4},{7,5},{8,10},{9,11},{10,... | collective-permute-start | bytes 6291464 | tf_op jit(solution)/shard_map/ppermute | solution.py:438
  168.9 39.1 %copy-start.25 = (bf16[2048,128]{1,0:T(8,128)(2,1)S(1)}, bf16[2048,128]{1,0:T(8,128)(2,1)}, u32[]{:S(2)}) copy-start(bf16[2048,128]{1,0:T(8,128)(2,1)} %copy.50) | copy-start | bytes 1572868
  168.9 39.1 %copy-start.29 = (bf16[2048,128]{1,0:T(8,128)(2,1)S(1)}, bf16[2048,128]{1,0:T(8,128)(2,1)}, u32[]{:S(2)}) copy-start(bf16[2048,128]{1,0:T(8,128)(2,1)} %copy-done.27) | copy-start | bytes 1572868
  223.4 6.1 %collective-permute-start.10 = (bf16[512,2048]{1,0:T(8,128)(2,1)S(1)}, bf16[512,2048]{1,0:T(8,128)(2,1)S(1)}, u32[]{:S(2)}, u32[]{:S(2)}) collective-permute-start(bf16[512,2048]{1,0:T(8,128)(2,1)S(1)} %slice.241), channel_id=1, source_target_pairs={{0,1},{1,0},{2,3},{3,2},{4,5},{5,4},{6,7},{7,6},{8,9},{9,8},{10,11... | collective-permute-start | bytes 6291464 | tf_op jit(solution)/shard_map/ppermute | solution.py:441
  231.5 47.1 %collective-permute-start.11 = (bf16[512,2048]{1,0:T(8,128)(2,1)}, bf16[512,2048]{1,0:T(8,128)(2,1)S(1)}, u32[]{:S(2)}, u32[]{:S(2)}) collective-permute-start(bf16[512,2048]{1,0:T(8,128)(2,1)} %add_convert_fusion), channel_id=1, source_target_pairs={{0,2},{1,3},{2,0},{3,1},{4,6},{5,7},{6,4},{7,5},{8,10},{9,11},{10,... | collective-permute-start | bytes 6291464 | tf_op jit(solution)/shard_map/ppermute | solution.py:438
  278.7 41.9 %copy-start.11 = (bf16[512,2048]{1,0:T(8,128)(2,1)}, bf16[512,2048]{1,0:T(8,128)(2,1)S(1)}, u32[]{:S(2)}) copy-start(bf16[512,2048]{1,0:T(8,128)(2,1)S(1)} %collective-permute-done.11) | copy-start | bytes 6291460
  310.1 13.8 %collective-permute-start.13 = (bf16[2048,128]{0,1:T(8,128)(2,1)S(1)}, bf16[2048,128]{0,1:T(8,128)(2,1)S(1)}, u32[]{:S(2)}, u32[]{:S(2)}) collective-permute-start(bf16[2048,128]{0,1:T(8,128)(2,1)S(1)} %pad_maximum_fusion.14), channel_id=1, source_target_pairs={{0,1},{1,0},{2,3},{3,2},{4,5},{5,4},{6,7},{7,6},{8,9},{9,8},{10,11... | collective-permute-start | bytes 1572872 | tf_op jit(solution)/shard_map/ppermute | solution.py:547
  323.7 28.5 %collective-permute-start.12 = (bf16[512,2048]{1,0:T(8,128)(2,1)}, bf16[512,2048]{1,0:T(8,128)(2,1)}, u32[]{:S(2)}, u32[]{:S(2)}) collective-permute-start(bf16[512,2048]{1,0:T(8,128)(2,1)} %slice.244), channel_id=1, source_target_pairs={{0,1},{1,0},{2,3},{3,2},{4,5},{5,4},{6,7},{7,6},{8,9},{9,8},{10,11... | collective-permute-start | bytes 6291464 | tf_op jit(solution)/shard_map/ppermute | solution.py:441
  324.2 16.3 %collective-permute-start.14 = (bf16[1024,128]{0,1:T(8,128)(2,1)S(1)}, bf16[1024,128]{0,1:T(8,128)(2,1)S(1)}, u32[]{:S(2)}, u32[]{:S(2)}) collective-permute-start(bf16[1024,128]{0,1:T(8,128)(2,1)S(1)} %pad_maximum_fusion.17), channel_id=1, source_target_pairs={{0,2},{1,3},{2,0},{3,1},{4,6},{5,7},{6,4},{7,5},{8,10},{9,11},{10,... | collective-permute-start | bytes 786440 | tf_op jit(solution)/shard_map/ppermute | solution.py:547
  341.4 9.0 %collective-permute-start.16 = (bf16[1280,128]{0,1:T(8,128)(2,1)}, bf16[1280,128]{0,1:T(8,128)(2,1)}, u32[]{:S(2)}, u32[]{:S(2)}) collective-permute-start(bf16[1280,128]{0,1:T(8,128)(2,1)} %pad_maximum_fusion.16), channel_id=1, source_target_pairs={{0,4},{4,0},{8,12},{12,8},{16,20},{20,16},{24,28},{28,24},{1,5},{5... | collective-permute-start | bytes 983048 | tf_op jit(solution)/shard_map/ppermute | solution.py:547
  358.8 9.4 %collective-permute-start.18 = (bf16[320,128]{0,1:T(8,128)(2,1)S(1)}, bf16[320,128]{0,1:T(8,128)(2,1)S(1)}, u32[]{:S(2)}, u32[]{:S(2)}) collective-permute-start(bf16[320,128]{0,1:T(8,128)(2,1)S(1)} %pad_maximum_fusion.24), channel_id=1, source_target_pairs={{0,16},{4,20},{8,24},{12,28},{16,0},{20,4},{24,8},{28,12},{1,17},{... | collective-permute-start | bytes 245768 | tf_op jit(solution)/shard_map/ppermute | solution.py:547
  360.3 9.3 %collective-permute-start.19 = (bf16[320,128]{0,1:T(8,128)(2,1)S(1)}, bf16[320,128]{0,1:T(8,128)(2,1)S(1)}, u32[]{:S(2)}, u32[]{:S(2)}) collective-permute-start(bf16[320,128]{0,1:T(8,128)(2,1)S(1)} %pad_maximum_fusion.25), channel_id=1, source_target_pairs={{0,24},{4,28},{8,16},{12,20},{16,8},{20,12},{24,0},{28,4},{1,25},{... | collective-permute-start | bytes 245768 | tf_op jit(solution)/shard_map/ppermute | solution.py:547
  361.1 8.5 %collective-permute-start.17 = (bf16[320,128]{0,1:T(8,128)(2,1)S(1)}, bf16[320,128]{0,1:T(8,128)(2,1)S(1)}, u32[]{:S(2)}, u32[]{:S(2)}) collective-permute-start(bf16[320,128]{0,1:T(8,128)(2,1)S(1)} %pad_maximum_fusion.23), channel_id=1, source_target_pairs={{0,8},{4,12},{8,0},{12,4},{16,24},{20,28},{24,16},{28,20},{1,9},{5... | collective-permute-start | bytes 245768 | tf_op jit(solution)/shard_map/ppermute | solution.py:547
  365.9 28.4 %collective-permute-start.15 = (bf16[512,2048]{1,0:T(8,128)(2,1)}, bf16[512,2048]{1,0:T(8,128)(2,1)}, u32[]{:S(2)}, u32[]{:S(2)}) collective-permute-start(bf16[512,2048]{1,0:T(8,128)(2,1)} %slice.250), channel_id=1, source_target_pairs={{0,1},{1,0},{2,3},{3,2},{4,5},{5,4},{6,7},{7,6},{8,9},{9,8},{10,11... | collective-permute-start | bytes 6291464 | tf_op jit(solution)/shard_map/ppermute | solution.py:441
  369.7 24.7 %copy-start.31 = (f32[2048]{0:T(1024)S(1)}, f32[2048]{0:T(1024)}, u32[]{:S(2)}) copy-start(f32[2048]{0:T(1024)} %param.23) | copy-start | bytes 24580
  370.9 3.5 collective-permute-start.22
  370.9 5.5 %collective-permute-start.21 = (bf16[320,128]{0,1:T(8,128)(2,1)S(1)}, bf16[320,128]{0,1:T(8,128)(2,1)S(1)}, u32[]{:S(2)}, u32[]{:S(2)}) collective-permute-start(bf16[320,128]{0,1:T(8,128)(2,1)S(1)} %pad_maximum_fusion.26), channel_id=1, source_target_pairs={{0,16},{4,20},{8,24},{12,28},{16,0},{20,4},{24,8},{28,12},{1,17},{... | collective-permute-start | bytes 245768 | tf_op jit(solution)/shard_map/ppermute | solution.py:563
  373.0 9.4 %collective-permute-start.20 = (bf16[320,128]{0,1:T(8,128)(2,1)S(1)}, bf16[320,128]{0,1:T(8,128)(2,1)S(1)}, u32[]{:S(2)}, u32[]{:S(2)}) collective-permute-start(bf16[320,128]{0,1:T(8,128)(2,1)S(1)} %pad_maximum_fusion.26), channel_id=1, source_target_pairs={{0,24},{4,28},{8,16},{12,20},{16,8},{20,12},{24,0},{28,4},{1,25},{... | collective-permute-start | bytes 245768 | tf_op jit(solution)/shard_map/ppermute | solution.py:563
  382.6 8.0 %collective-permute-start.23 = (bf16[1280,128]{0,1:T(8,128)(2,1)S(1)}, bf16[1280,128]{0,1:T(8,128)(2,1)S(1)}, u32[]{:S(2)}, u32[]{:S(2)}) collective-permute-start(bf16[1280,128]{0,1:T(8,128)(2,1)S(1)} %concatenate.128), channel_id=1, source_target_pairs={{0,4},{4,0},{8,12},{12,8},{16,20},{20,16},{24,28},{28,24},{1,5},{5... | collective-permute-start | bytes 983048 | tf_op jit(solution)/shard_map/ppermute | solution.py:563
  391.5 7.2 %collective-permute-start.24 = (bf16[1024,128]{0,1:T(8,128)(2,1)}, bf16[1024,128]{0,1:T(8,128)(2,1)}, u32[]{:S(2)}, u32[]{:S(2)}) collective-permute-start(bf16[1024,128]{0,1:T(8,128)(2,1)} %pad_maximum_fusion.18), channel_id=1, source_target_pairs={{0,2},{1,3},{2,0},{3,1},{4,6},{5,7},{6,4},{7,5},{8,10},{9,11},{10,... | collective-permute-start | bytes 786440 | tf_op jit(solution)/shard_map/ppermute | solution.py:563
  399.8 7.2 %collective-permute-start.25 = (bf16[2048,128]{0,1:T(8,128)(2,1)S(1)}, bf16[2048,128]{0,1:T(8,128)(2,1)S(1)}, u32[]{:S(2)}, u32[]{:S(2)}) collective-permute-start(bf16[2048,128]{0,1:T(8,128)(2,1)S(1)} %pad_maximum_fusion.15), channel_id=1, source_target_pairs={{0,1},{1,0},{2,3},{3,2},{4,5},{5,4},{6,7},{7,6},{8,9},{9,8},{10,11... | collective-permute-start | bytes 1572872 | tf_op jit(solution)/shard_map/ppermute | solution.py:563
  (50 other events, 324.3 us)
Sparse Core Ops, SparseCore 0:
  233.3 74.3 all-reduce.5
